TPU v7x, 32 devices: a whole 2x2x4 slice. The times are simulated.
32 devices in a mesh: rep: 2 (over x), shard: 16 (over z, y, core).
Axes of the slice: x: 2, y: 2, z: 4, core: 2. Of those that a mesh axis runs over, the one named last changes fastest.
Arguments:
- tokens: bfloat16 [2, 6144, 1024], P('rep', 'shard'), may hold values from -6 to 6
- cotangent: bfloat16 [2, 6144, 1024], P('rep', 'shard'), may hold values from -6 to 6
- seg_ids: int32 [2, 6144], P('rep'), may hold values from 0 to 7, never falling along the last dimension, each value on 1 to 2000 neighbouring positions
- random_blocks: int32 [2, 16, 96, 3], P('rep', 'shard'), may hold values from 0 to 95
- global_blocks: int32 [2, 2], P('rep'), may hold values from 0 to 95
- ln1_gain: bfloat16 [1024], P('shard'), may hold values from 0.5 to 1.5
- ln1_bias: bfloat16 [1024], P('shard'), may hold values from -1.5 to 1.5
- w_query: bfloat16 [1024, 1024], P('shard'), may hold values from -0.1875 to 0.1875
- b_query: bfloat16 [1024], P('shard'), may hold values from -1.5 to 1.5
- w_key: bfloat16 [1024, 1024], P('shard'), may hold values from -0.1875 to 0.1875
- w_value: bfloat16 [1024, 1024], P('shard'), may hold values from -0.1875 to 0.1875
- b_value: bfloat16 [1024], P('shard'), may hold values from -1.5 to 1.5
- w_out: bfloat16 [1024, 1024], P('shard'), may hold values from -2 to 2
- b_out: bfloat16 [1024], P('shard'), may hold values from -1.5 to 1.5
- ln2_gain: bfloat16 [1024], P('shard'), may hold values from 0.5 to 1.5
- ln2_bias: bfloat16 [1024], P('shard'), may hold values from -1.5 to 1.5
- w_up: bfloat16 [1024, 4096], P('shard'), may hold values from -0.1875 to 0.1875
- b_up: bfloat16 [4096], P('shard'), may hold values from -1.5 to 1.5
- w_down: bfloat16 [4096, 1024], P('shard'), may hold values from -0.125 to 0.125
- b_down: bfloat16 [1024], P('shard'), may hold values from -1.5 to 1.5
Outputs:
- layer_out: bfloat16 [2, 6144, 1024], P('rep', 'shard')
- grad_tokens: bfloat16 [2, 6144, 1024], P('rep', 'shard')
- grad_ln1_gain: float32 [1024], P('shard')
- grad_ln1_bias: float32 [1024], P('shard')
- grad_w_query: float32 [1024, 1024], P('shard')
- grad_b_query: float32 [1024], P('shard')
- grad_w_key: float32 [1024, 1024], P('shard')
- grad_w_value: float32 [1024, 1024], P('shard')
- grad_b_value: float32 [1024], P('shard')
- grad_w_out: float32 [1024, 1024], P('shard')
- grad_b_out: float32 [1024], P('shard')
- grad_ln2_gain: float32 [1024], P('shard')
- grad_ln2_bias: float32 [1024], P('shard')
- grad_w_up: float32 [1024, 4096], P('shard')
- grad_b_up: float32 [4096], P('shard')
- grad_w_down: float32 [4096, 1024], P('shard')
- grad_b_down: float32 [1024], P('shard')
All inputs are finite; a program needn't handle non-finite values.
Results may differ from a plain program's by a relative error of at most 0.019.
Values may be sent and summed in bfloat16 or wider, within the bound.
No kernel may reach another device: no remote copies, remote signals or barrier semaphores. Data moves between devices by JAX's collectives and lax.ppermute only.
A program may use at most 192 MiB of HBM per device.

v0:
```python
import math

import jax
import jax.numpy as jnp
from jax import lax
from jax.sharding import PartitionSpec as P

H = 16
DH = 64
BLK = 64


EPSILON = 1e-05
HIGHEST = lax.Precision.HIGHEST


def layer_norm(values, norm_gain, norm_shift):
    centre = jnp.mean(values, axis=-1, keepdims=True)
    centred = values - centre
    spread = jnp.mean(centred * centred, axis=-1, keepdims=True)
    return centred * lax.rsqrt(spread + EPSILON) * norm_gain + norm_shift


def product(left, right):
    return jnp.dot(left, right, preferred_element_type=jnp.float32)


def product_tn(left, right):
    return lax.dot_general(
        left, right, (((0,), (0,)), ((), ())), preferred_element_type=jnp.float32
    )


def product_nt(left, right):
    return lax.dot_general(
        left, right, (((1,), (1,)), ((), ())), preferred_element_type=jnp.float32
    )


def gelu_tanh(values):
    return jax.nn.gelu(values, approximate=True)


def key_blocks(random_heads, global_ids):
    heads_count, blocks_count = (random_heads.shape[0], random_heads.shape[1])
    position = jnp.arange(blocks_count, dtype=jnp.int32)
    window = jnp.stack([position - 1, position, position + 1], axis=1)
    window = window[None]
    global_all = jnp.broadcast_to(
        global_ids[None, None, :], (heads_count, blocks_count, global_ids.shape[0])
    )
    listed = jnp.concatenate([window, random_heads, global_all], axis=2)
    slot_count = listed.shape[2]
    earlier = jnp.arange(slot_count)[:, None] > jnp.arange(slot_count)[None, :]
    repeated = jnp.any((listed[..., :, None] == listed[..., None, :]) & earlier, axis=-1)
    usable = (listed >= 0) & (listed < blocks_count) & jnp.logical_not(repeated)
    return (jnp.clip(listed, 0, blocks_count - 1), usable)


def pad_blocks(table, axis):
    widths = [(0, 0)] * table.ndim
    widths[axis] = (1, 1)
    return jnp.pad(table, widths)


def window_slots(padded, start, count, axis):
    region = lax.dynamic_slice_in_dim(padded, start, count + 2, axis=axis)
    before = lax.slice_in_dim(region, 0, count, axis=axis)
    centre = lax.slice_in_dim(region, 1, count + 1, axis=axis)
    after = lax.slice_in_dim(region, 2, count + 2, axis=axis)
    return jnp.stack([before, centre, after], axis=axis + 1)


def one_hot_rest(group_chosen, blocks_count, dtype):
    rest = group_chosen[:, :, 3:]
    return (rest[..., None] == jnp.arange(blocks_count, dtype=jnp.int32)).astype(dtype)


def listed_blocks(padded, start, count, hot):
    heads_here, _, block_size, head_size = padded.shape
    blocks_count = padded.shape[1] - 2
    window = window_slots(padded, start, count, 1)
    flat = lax.slice_in_dim(padded, 1, blocks_count + 1, axis=1).reshape(
        heads_here, blocks_count, block_size * head_size
    )
    rest = jnp.einsum("hqkn,hnx->hqkx", hot, flat, preferred_element_type=jnp.float32).astype(
        padded.dtype
    )
    rest = rest.reshape(heads_here, count, hot.shape[2], block_size, head_size)
    return jnp.concatenate([window, rest], axis=2)


def listed_segments(seg_padded, seg_float, start, count, hot_float):
    window = window_slots(seg_padded, start, count, 0)
    window = window[None]
    rest = jnp.einsum("hqkn,nj->hqkj", hot_float, seg_float, precision=HIGHEST)
    return jnp.concatenate([window, rest], axis=2)


def add_listed(padded_grads, start, count, adds, hot_float):
    heads_here, _, block_size, head_size = padded_grads.shape
    blocks_count = padded_grads.shape[1] - 2
    region = lax.dynamic_slice_in_dim(padded_grads, start, count + 2, axis=1)
    delta = jnp.pad(adds[:, :, 0], ((0, 0), (0, 2), (0, 0), (0, 0)))
    delta = delta + jnp.pad(adds[:, :, 1], ((0, 0), (1, 1), (0, 0), (0, 0)))
    delta = delta + jnp.pad(adds[:, :, 2], ((0, 0), (2, 0), (0, 0), (0, 0)))
    padded_grads = lax.dynamic_update_slice_in_dim(padded_grads, region + delta, start, axis=1)
    rest_adds = adds[:, :, 3:].reshape(heads_here, count, adds.shape[2] - 3, block_size * head_size)
    spread = jnp.einsum("hqkn,hqkx->hnx", hot_float, rest_adds, precision=HIGHEST)
    spread = jnp.pad(
        spread.reshape(heads_here, blocks_count, block_size, head_size),
        ((0, 0), (1, 1), (0, 0), (0, 0)),
        constant_values=0.0,
    )
    return padded_grads + spread


def heads_major(table):
    length, heads_here, head_size = table.shape
    return table.reshape(length // BLK, BLK, heads_here, head_size).transpose(2, 0, 1, 3)


def tokens_major(table):
    heads_here, blocks_count, block_size, head_size = table.shape
    return table.transpose(1, 2, 0, 3).reshape(blocks_count * block_size, heads_here, head_size)


def grouped(table, groups_count):
    per_group = table.shape[1] // groups_count
    return jnp.moveaxis(
        table.reshape((table.shape[0], groups_count, per_group) + table.shape[2:]), 1, 0
    )


def ungrouped(table):
    moved = jnp.moveaxis(table, 0, 1)
    return moved.reshape((moved.shape[0], moved.shape[1] * moved.shape[2]) + moved.shape[3:])


def group_scores(query_group, key_group, seg_query, seg_keys, usable):
    factor = 1.0 / math.sqrt(query_group.shape[-1])
    scores = (
        jnp.einsum("hqid,hqkjd->hqikj", query_group, key_group, preferred_element_type=jnp.float32)
        * factor
    )
    allowed = usable[:, :, None, :, None] & (
        seg_query[None, :, :, None, None] == seg_keys[:, :, None, :, :]
    )
    return (scores, allowed)


def log_total(scores, allowed):
    masked = jnp.where(allowed, scores, -1e30)
    highest = jnp.max(masked, axis=(3, 4), keepdims=True)
    total = jnp.sum(jnp.exp(masked - highest), axis=(3, 4), keepdims=True)
    return highest + jnp.log(total)


def chances_from(scores, allowed, log_sum):
    return jnp.where(allowed, jnp.exp(scores - log_sum), 0.0)


def attention_forward(query_table, key_table, value_table, seg_table, chosen, usable):
    blocks_count = chosen.shape[1]
    per_group = math.gcd(blocks_count, 16)
    groups_count = blocks_count // per_group
    key_padded = pad_blocks(key_table, 1)
    value_padded = pad_blocks(value_table, 1)
    seg_float = seg_table.astype(jnp.float32)
    seg_padded = pad_blocks(seg_float, 0)

    def one_group(pieces):
        query_group, group_chosen, group_usable, seg_query, group_index = pieces
        start = group_index * per_group
        hot = one_hot_rest(group_chosen, blocks_count, jnp.bfloat16)
        hot_float = hot.astype(jnp.float32)
        key_group = listed_blocks(key_padded, start, per_group, hot)
        value_group = listed_blocks(value_padded, start, per_group, hot)
        seg_keys = listed_segments(seg_padded, seg_float, start, per_group, hot_float)
        scores, allowed = group_scores(query_group, key_group, seg_query, seg_keys, group_usable)
        log_sum = log_total(scores, allowed)
        chances = chances_from(scores, allowed, log_sum).astype(jnp.bfloat16)
        attended = jnp.einsum(
            "hqikj,hqkjd->hqid", chances, value_group, preferred_element_type=jnp.float32
        )
        return (attended, log_sum)

    seg_groups = seg_float.reshape(groups_count, per_group, seg_table.shape[1])
    group_ids = jnp.arange(groups_count, dtype=jnp.int32)
    attended, log_sum = lax.map(
        one_group,
        (
            grouped(query_table, groups_count),
            grouped(chosen, groups_count),
            grouped(usable, groups_count),
            seg_groups,
            group_ids,
        ),
    )
    return (ungrouped(attended), log_sum)


def attention_backward(
    query_table, key_table, value_table, grad_table, log_sum, seg_table, chosen, usable
):
    blocks_count = chosen.shape[1]
    per_group = math.gcd(blocks_count, 16)
    groups_count = blocks_count // per_group
    factor = 1.0 / math.sqrt(query_table.shape[-1])
    key_padded = pad_blocks(key_table, 1)
    value_padded = pad_blocks(value_table, 1)
    seg_float = seg_table.astype(jnp.float32)
    seg_padded = pad_blocks(seg_float, 0)

    def one_group(carry, pieces):
        key_grads, value_grads = carry
        query_group, grad_group, group_chosen, group_usable, seg_query, group_log, group_index = (
            pieces
        )
        start = group_index * per_group
        hot = one_hot_rest(group_chosen, blocks_count, jnp.bfloat16)
        hot_float = hot.astype(jnp.float32)
        key_group = listed_blocks(key_padded, start, per_group, hot)
        value_group = listed_blocks(value_padded, start, per_group, hot)
        seg_keys = listed_segments(seg_padded, seg_float, start, per_group, hot_float)
        scores, allowed = group_scores(query_group, key_group, seg_query, seg_keys, group_usable)
        chances = chances_from(scores, allowed, group_log)
        value_adds = jnp.einsum(
            "hqikj,hqid->hqkjd",
            chances.astype(jnp.bfloat16),
            grad_group,
            preferred_element_type=jnp.float32,
        )
        grad_chances = jnp.einsum(
            "hqid,hqkjd->hqikj", grad_group, value_group, preferred_element_type=jnp.float32
        )
        inner = jnp.sum(chances * grad_chances, axis=(3, 4), keepdims=True)
        grad_scores = (chances * (grad_chances - inner)).astype(jnp.bfloat16)
        query_grad = (
            jnp.einsum(
                "hqikj,hqkjd->hqid", grad_scores, key_group, preferred_element_type=jnp.float32
            )
            * factor
        )
        key_adds = (
            jnp.einsum(
                "hqikj,hqid->hqkjd", grad_scores, query_group, preferred_element_type=jnp.float32
            )
            * factor
        )
        key_grads = add_listed(key_grads, start, per_group, key_adds, hot_float)
        value_grads = add_listed(value_grads, start, per_group, value_adds, hot_float)
        return ((key_grads, value_grads), query_grad)

    seg_groups = seg_float.reshape(groups_count, per_group, seg_table.shape[1])
    group_ids = jnp.arange(groups_count, dtype=jnp.int32)
    start_grads = jnp.zeros(key_padded.shape, jnp.float32)
    (key_grads, value_grads), query_grads = lax.scan(
        one_group,
        (start_grads, start_grads),
        (
            grouped(query_table, groups_count),
            grouped(grad_table, groups_count),
            grouped(chosen, groups_count),
            grouped(usable, groups_count),
            seg_groups,
            log_sum,
            group_ids,
        ),
    )
    key_grads = key_grads[:, 1 : blocks_count + 1]
    value_grads = value_grads[:, 1 : blocks_count + 1]
    return (ungrouped(query_grads), key_grads, value_grads)


def local(
    tokens,
    cotangent,
    seg_ids,
    random_blocks,
    global_blocks,
    ln1_gain,
    ln1_bias,
    w_query,
    b_query,
    w_key,
    w_value,
    b_value,
    w_out,
    b_out,
    ln2_gain,
    ln2_bias,
    w_up,
    b_up,
    w_down,
    b_down,
):
    token_count = tokens.shape[1]
    width = tokens.shape[2]
    (
        gain_one,
        shift_one,
        weight_query,
        bias_query,
        weight_key,
        weight_value,
        bias_value,
        weight_out,
        bias_out,
    ) = (
        lax.all_gather(ln1_gain, "shard", axis=0, tiled=True),
        lax.all_gather(ln1_bias, "shard", axis=0, tiled=True),
        lax.all_gather(w_query, "shard", axis=0, tiled=True),
        lax.all_gather(b_query, "shard", axis=0, tiled=True),
        lax.all_gather(w_key, "shard", axis=0, tiled=True),
        lax.all_gather(w_value, "shard", axis=0, tiled=True),
        lax.all_gather(b_value, "shard", axis=0, tiled=True),
        lax.all_gather(w_out, "shard", axis=0, tiled=True),
        lax.all_gather(b_out, "shard", axis=0, tiled=True),
    )
    inputs = tokens[0].astype(jnp.float32)
    normed_one, first_pullback = jax.vjp(
        layer_norm, inputs, gain_one.astype(jnp.float32), shift_one.astype(jnp.float32)
    )
    normed_low = normed_one.astype(jnp.bfloat16)
    query = (product(normed_low, weight_query) + bias_query.astype(jnp.float32)).astype(
        jnp.bfloat16
    )
    keys = product(normed_low, weight_key).astype(jnp.bfloat16)
    values = (product(normed_low, weight_value) + bias_value.astype(jnp.float32)).astype(
        jnp.bfloat16
    )
    query_heads, key_heads, value_heads = (
        lax.all_to_all(
            query.reshape(token_count, H, DH), "shard", split_axis=1, concat_axis=0, tiled=True
        ),
        lax.all_to_all(
            keys.reshape(token_count, H, DH), "shard", split_axis=1, concat_axis=0, tiled=True
        ),
        lax.all_to_all(
            values.reshape(token_count, H, DH), "shard", split_axis=1, concat_axis=0, tiled=True
        ),
    )
    query_table = heads_major(query_heads)
    key_table = heads_major(key_heads)
    value_table = heads_major(value_heads)
    chosen, usable = key_blocks(random_blocks[0], global_blocks[0])
    seg_table = seg_ids[0].reshape(-1, BLK)
    attended_table, log_sum = attention_forward(
        query_table, key_table, value_table, seg_table, chosen, usable
    )
    attended_heads = tokens_major(attended_table).astype(jnp.bfloat16)
    attended = lax.all_to_all(
        attended_heads, "shard", split_axis=0, concat_axis=1, tiled=True
    ).reshape(token_count, width)
    middle = inputs + product(attended, weight_out) + bias_out.astype(jnp.float32)
    gain_two, shift_two, weight_up, bias_up, weight_down, bias_down = (
        lax.all_gather(ln2_gain, "shard", axis=0, tiled=True),
        lax.all_gather(ln2_bias, "shard", axis=0, tiled=True),
        lax.all_gather(w_up, "shard", axis=0, tiled=True),
        lax.all_gather(b_up, "shard", axis=0, tiled=True),
        lax.all_gather(w_down, "shard", axis=0, tiled=True),
        lax.all_gather(b_down, "shard", axis=0, tiled=True),
    )
    normed_two, second_pullback = jax.vjp(
        layer_norm, middle, gain_two.astype(jnp.float32), shift_two.astype(jnp.float32)
    )
    normed_two_low = normed_two.astype(jnp.bfloat16)
    hidden_pre = product(normed_two_low, weight_up) + bias_up.astype(jnp.float32)
    hidden_full, gelu_pullback = jax.vjp(gelu_tanh, hidden_pre)
    hidden = hidden_full.astype(jnp.bfloat16)
    result = middle + product(hidden, weight_down) + bias_down.astype(jnp.float32)
    layer_out = result.astype(jnp.bfloat16)[None]
    weight_up, weight_down = (
        lax.all_gather(w_up, "shard", axis=0, tiled=True),
        lax.all_gather(w_down, "shard", axis=0, tiled=True),
    )
    grad_out = cotangent[0]
    grad_down = product_tn(hidden, grad_out)
    grad_down_bias = jnp.sum(grad_out, axis=0, dtype=jnp.float32)
    grad_hidden = product_nt(grad_out, weight_down)
    grad_pre = gelu_pullback(grad_hidden)[0].astype(jnp.bfloat16)
    grad_up = product_tn(normed_two_low, grad_pre)
    grad_up_bias = jnp.sum(grad_pre, axis=0, dtype=jnp.float32)
    grad_normed_two = product_nt(grad_pre, weight_up)
    grad_middle_norm, grad_gain_two, grad_shift_two = second_pullback(grad_normed_two)
    grad_middle = grad_out.astype(jnp.float32) + grad_middle_norm
    grad_gain_two, grad_shift_two, grad_up, grad_up_bias, grad_down, grad_down_bias = (
        lax.psum_scatter(
            grad_gain_two.astype(jnp.bfloat16), "shard", scatter_dimension=0, tiled=True
        ).astype(jnp.float32),
        lax.psum_scatter(
            grad_shift_two.astype(jnp.bfloat16), "shard", scatter_dimension=0, tiled=True
        ).astype(jnp.float32),
        lax.psum_scatter(
            grad_up.astype(jnp.bfloat16), "shard", scatter_dimension=0, tiled=True
        ).astype(jnp.float32),
        lax.psum_scatter(
            grad_up_bias.astype(jnp.bfloat16), "shard", scatter_dimension=0, tiled=True
        ).astype(jnp.float32),
        lax.psum_scatter(
            grad_down.astype(jnp.bfloat16), "shard", scatter_dimension=0, tiled=True
        ).astype(jnp.float32),
        lax.psum_scatter(
            grad_down_bias.astype(jnp.bfloat16), "shard", scatter_dimension=0, tiled=True
        ).astype(jnp.float32),
    )
    weight_query, weight_key, weight_value, weight_out = (
        lax.all_gather(w_query, "shard", axis=0, tiled=True),
        lax.all_gather(w_key, "shard", axis=0, tiled=True),
        lax.all_gather(w_value, "shard", axis=0, tiled=True),
        lax.all_gather(w_out, "shard", axis=0, tiled=True),
    )
    grad_branch = grad_middle.astype(jnp.bfloat16)
    grad_out_weight = product_tn(attended, grad_branch)
    grad_out_bias = jnp.sum(grad_branch, axis=0, dtype=jnp.float32)
    grad_attended = (
        product_nt(grad_branch, weight_out).astype(jnp.bfloat16).reshape(token_count, H, DH)
    )
    grad_heads = lax.all_to_all(grad_attended, "shard", split_axis=1, concat_axis=0, tiled=True)
    query_grads, key_grads, value_grads = attention_backward(
        query_table,
        key_table,
        value_table,
        heads_major(grad_heads),
        log_sum,
        seg_table,
        chosen,
        usable,
    )
    grad_query, grad_keys, grad_values = (
        lax.all_to_all(
            tokens_major(query_grads).astype(jnp.bfloat16),
            "shard",
            split_axis=0,
            concat_axis=1,
            tiled=True,
        ),
        lax.all_to_all(
            tokens_major(key_grads).astype(jnp.bfloat16),
            "shard",
            split_axis=0,
            concat_axis=1,
            tiled=True,
        ),
        lax.all_to_all(
            tokens_major(value_grads).astype(jnp.bfloat16),
            "shard",
            split_axis=0,
            concat_axis=1,
            tiled=True,
        ),
    )
    grad_query = grad_query.reshape(token_count, width)
    grad_keys = grad_keys.reshape(token_count, width)
    grad_values = grad_values.reshape(token_count, width)
    grad_query_weight = product_tn(normed_low, grad_query)
    grad_query_bias = jnp.sum(grad_query, axis=0, dtype=jnp.float32)
    grad_key_weight = product_tn(normed_low, grad_keys)
    grad_value_weight = product_tn(normed_low, grad_values)
    grad_value_bias = jnp.sum(grad_values, axis=0, dtype=jnp.float32)
    grad_normed_one = (
        product_nt(grad_query, weight_query)
        + product_nt(grad_keys, weight_key)
        + product_nt(grad_values, weight_value)
    )
    grad_inputs_norm, grad_gain_one, grad_shift_one = first_pullback(grad_normed_one)
    grad_tokens = (grad_middle + grad_inputs_norm).astype(jnp.bfloat16)[None]
    (
        grad_gain_one,
        grad_shift_one,
        grad_query_weight,
        grad_query_bias,
        grad_key_weight,
        grad_value_weight,
        grad_value_bias,
        grad_out_weight,
        grad_out_bias,
    ) = (
        lax.psum_scatter(
            grad_gain_one.astype(jnp.bfloat16), "shard", scatter_dimension=0, tiled=True
        ).astype(jnp.float32),
        lax.psum_scatter(
            grad_shift_one.astype(jnp.bfloat16), "shard", scatter_dimension=0, tiled=True
        ).astype(jnp.float32),
        lax.psum_scatter(
            grad_query_weight.astype(jnp.bfloat16), "shard", scatter_dimension=0, tiled=True
        ).astype(jnp.float32),
        lax.psum_scatter(
            grad_query_bias.astype(jnp.bfloat16), "shard", scatter_dimension=0, tiled=True
        ).astype(jnp.float32),
        lax.psum_scatter(
            grad_key_weight.astype(jnp.bfloat16), "shard", scatter_dimension=0, tiled=True
        ).astype(jnp.float32),
        lax.psum_scatter(
            grad_value_weight.astype(jnp.bfloat16), "shard", scatter_dimension=0, tiled=True
        ).astype(jnp.float32),
        lax.psum_scatter(
            grad_value_bias.astype(jnp.bfloat16), "shard", scatter_dimension=0, tiled=True
        ).astype(jnp.float32),
        lax.psum_scatter(
            grad_out_weight.astype(jnp.bfloat16), "shard", scatter_dimension=0, tiled=True
        ).astype(jnp.float32),
        lax.psum_scatter(
            grad_out_bias.astype(jnp.bfloat16), "shard", scatter_dimension=0, tiled=True
        ).astype(jnp.float32),
    )
    (
        grad_gain_one,
        grad_shift_one,
        grad_query_weight,
        grad_query_bias,
        grad_key_weight,
        grad_value_weight,
        grad_value_bias,
        grad_out_weight,
        grad_out_bias,
        grad_gain_two,
        grad_shift_two,
        grad_up,
        grad_up_bias,
        grad_down,
        grad_down_bias,
    ) = (
        lax.psum(grad_gain_one.astype(jnp.bfloat16), "rep").astype(jnp.float32),
        lax.psum(grad_shift_one.astype(jnp.bfloat16), "rep").astype(jnp.float32),
        lax.psum(grad_query_weight.astype(jnp.bfloat16), "rep").astype(jnp.float32),
        lax.psum(grad_query_bias.astype(jnp.bfloat16), "rep").astype(jnp.float32),
        lax.psum(grad_key_weight.astype(jnp.bfloat16), "rep").astype(jnp.float32),
        lax.psum(grad_value_weight.astype(jnp.bfloat16), "rep").astype(jnp.float32),
        lax.psum(grad_value_bias.astype(jnp.bfloat16), "rep").astype(jnp.float32),
        lax.psum(grad_out_weight.astype(jnp.bfloat16), "rep").astype(jnp.float32),
        lax.psum(grad_out_bias.astype(jnp.bfloat16), "rep").astype(jnp.float32),
        lax.psum(grad_gain_two.astype(jnp.bfloat16), "rep").astype(jnp.float32),
        lax.psum(grad_shift_two.astype(jnp.bfloat16), "rep").astype(jnp.float32),
        lax.psum(grad_up.astype(jnp.bfloat16), "rep").astype(jnp.float32),
        lax.psum(grad_up_bias.astype(jnp.bfloat16), "rep").astype(jnp.float32),
        lax.psum(grad_down.astype(jnp.bfloat16), "rep").astype(jnp.float32),
        lax.psum(grad_down_bias.astype(jnp.bfloat16), "rep").astype(jnp.float32),
    )
    return (
        layer_out,
        grad_tokens,
        grad_gain_one,
        grad_shift_one,
        grad_query_weight,
        grad_query_bias,
        grad_key_weight,
        grad_value_weight,
        grad_value_bias,
        grad_out_weight,
        grad_out_bias,
        grad_gain_two,
        grad_shift_two,
        grad_up,
        grad_up_bias,
        grad_down,
        grad_down_bias,
    )


def solution(mesh):
    return jax.shard_map(
        local,
        mesh=mesh,
        in_specs=(
            P("rep", "shard", None),
            P("rep", "shard", None),
            P("rep", None),
            P("rep", "shard", None, None),
            P("rep", None),
            P("shard"),
            P("shard"),
            P("shard", None),
            P("shard"),
            P("shard", None),
            P("shard", None),
            P("shard"),
            P("shard", None),
            P("shard"),
            P("shard"),
            P("shard"),
            P("shard", None),
            P("shard"),
            P("shard", None),
            P("shard"),
        ),
        out_specs=(
            P("rep", "shard", None),
            P("rep", "shard", None),
            P("shard"),
            P("shard"),
            P("shard", None),
            P("shard"),
            P("shard", None),
            P("shard", None),
            P("shard"),
            P("shard", None),
            P("shard"),
            P("shard"),
            P("shard"),
            P("shard", None),
            P("shard"),
            P("shard", None),
            P("shard"),
        ),
        check_vma=False,
    )
```

profile of v0, /device:TPU:0, one launch (start us, length us, event | category | flops | bytes accessed | tf_op | source)
XLA Modules:
  0.0 1657.7 jit_solution(4626726606751625593)
XLA Ops:
  18.4 63.3 %all-reduce.29 = (bf16[1024]{0:T(1024)(128)(2,1)S(1)}, bf16[1024]{0:T(1024)(128)(2,1)S(1)}, bf16[1024]{0:T(1024)(128)(2,1)S(1)}, bf16[1024]{0:T(1024)(128)(2,1)S...) all-reduce(bf16[1024]{0:T(1024)(128)(2,1)S(1)} %dynamic-update-slic, ...), channel_id=1, replica_groups=mesh['rep'=2,'shard'=16] {'shard'}, use_global_device_ids=true, to_apply=%add.13 | all-reduce | flops 7168 | bytes 28672
  91.4 8.4 all-gather.8.cloned.1.call-done
  103.6 6.4 all-to-all-done.2
  110.0 6.9 all-to-all-start
  118.0 28.1 %all-gather.10.cloned.1.call-done = bf16[1024,1024]{1,0:T(8,128)(2,1)} async-done(((bf16[64,1024]{1,0:T(8,128)(2,1)}), bf16[1024,1024]{1,0:T(8,128)(2,1)}) %all-gather.10.cloned.1.call-update) | async-done | bytes 2097168 | tf_op jit(solution)/shard_map/all_gather | solution.py:315
  160.0 16.7 %all-to-all-done.1 = bf16[384,16,64]{0,2,1:T(8,128)(2,1)S(1)} async-done(((bf16[384,16,64]{0,2,1:T(8,128)(2,1)}), bf16[384,16,64]{0,2,1:T(8,128)(2,1)S(1)}, u32[]{:S(2)}, u32[]{:S(2)}) %all-to-all-start.1) | async-done | bytes 786464 | tf_op jit(solution)/shard_map/all_to_all | solution.py:337
  182.2 225.9 %while.29 = (s32[]{:T(128)}, bf16[6,1,16,64,64]{4,3,2,1,0:T(8,128)(2,1)}, f32[6,1,16,64,1,1]{3,2,5,4,1,0:T(8,128)}, pred[6,1,16,8]{2,3,1,0:T(8,128)(4,1)}, f32[6...) while((s32[]{:T(128)}, ...), condition=%wide.region_6.7_spmd, body=%wide.region_3.6_spmd.sunk | while | flops 283938304 | bytes 27647812 | solution.py:190
  422.4 29.0 %all-gather = bf16[16,1,256]{2,1,0:T(2,128)(2,1)S(1)} all-gather(bf16[1,1,256]{2,1,0:T(2,128)(2,1)S(1)} %reshape.889), channel_id=1, replica_groups=mesh['rep'=2,'shard'=16] {'shard'}, dimensions={0}, use_global_device_ids=true | all-gather | bytes 8704 | tf_op jit(solution)/shard_map/all_gather | solution.py:361
  457.5 7.0 copy.401
  471.5 10.1 convolution_add_fusion
  481.6 11.6 fusion.131
  513.9 14.7 all-to-all-done.4
  532.6 604.9 %while.30 = (s32[]{:T(128)}, f32[1,98,64,64]{3,2,1,0:T(8,128)}, f32[1,98,64,64]{3,2,1,0:T(8,128)}, bf16[6,1,16,64,64]{4,3,2,1,0:T(8,128)(2,1)}, s32[6]{0:T(128)S...) while((s32[]{:T(128)}, f32[1,98,64,64]{3,2,1,0:T(8,128)}, ...), condition=%wide.region_13.14_spmd.clone, body=%wide.region_11.13_spmd.clone.sunk | while | flops 1243941376 | bytes 124831344 | solution.py:258
  908.7 6.3 fusion.224
  1143.2 25.3 %all_to_all.120 = bf16[16,2,12288]{2,1,0:T(2,128)(2,1)} all-to-all(bf16[16,2,12288]{2,1,0:T(2,128)(2,1)S(1)} %reshape.961), channel_id=1, replica_groups=mesh['rep'=2,'shard'=16] {'shard'}, dimensions={0} | all-to-all | bytes 1572864 | tf_op jit(solution)/shard_map/all_to_all | solution.py:446
  1190.5 26.4 %all_to_all.121 = bf16[16,2,12288]{2,1,0:T(2,128)(2,1)S(1)} all-to-all(bf16[16,2,12288]{2,1,0:T(2,128)(2,1)S(1)} %reshape.959), channel_id=1, replica_groups=mesh['rep'=2,'shard'=16] {'shard'}, dimensions={0} | all-to-all | bytes 1572864 | tf_op jit(solution)/shard_map/all_to_all | solution.py:439
  1238.3 25.7 %all_to_all.122 = bf16[16,2,12288]{2,1,0:T(2,128)(2,1)S(1)} all-to-all(bf16[16,2,12288]{2,1,0:T(2,128)(2,1)S(1)} %reshape.957), channel_id=1, replica_groups=mesh['rep'=2,'shard'=16] {'shard'}, dimensions={0} | all-to-all | bytes 1572864 | tf_op jit(solution)/shard_map/all_to_all | solution.py:432
  1279.2 10.4 convolution_convert_fusion.4
  1291.1 9.0 convolution_convert_fusion.5
  1313.4 60.6 %all-reduce.28 = (bf16[1024]{0:T(1024)(128)(2,1)S(1)}, bf16[1024]{0:T(1024)(128)(2,1)S(1)}, bf16[1024]{0:T(1024)(128)(2,1)S(1)}, bf16[1024]{0:T(1024)(128)(2,1)S...) all-reduce(bf16[1024]{0:T(1024)(128)(2,1)S(1)} %dynamic-update-slic, ...), channel_id=1, replica_groups=mesh['rep'=2,'shard'=16] {'shard'}, use_global_device_ids=true, to_apply=%add.18 | all-reduce | flops 13312 | bytes 53248
  1384.4 95.6 %reduce-scatter.17.cloned.1.call-done = bf16[256,1024]{1,0:T(8,128)(2,1)} async-done(((bf16[4096,1024]{1,0:T(8,128)(2,1)}), bf16[256,1024]{1,0:T(8,128)(2,1)}) %reduce-scatter.17.cloned.1.call-update) | async-done | bytes 524304 | tf_op jit(solution)/shard_map/reduce_scatter | solution.py:401
  1480.0 107.0 %reduce-scatter.15.cloned.1.call-done = bf16[64,4096]{1,0:T(8,128)(2,1)} async-done(((bf16[1024,4096]{1,0:T(8,128)(2,1)}), bf16[64,4096]{1,0:T(8,128)(2,1)}) %reduce-scatter.15.cloned.1.call-update) | async-done | bytes 524304 | tf_op jit(solution)/shard_map/reduce_scatter | solution.py:395
  1590.6 10.6 fusion.106
  1601.1 39.8 %all-reduce.34.cloned.1.call-done = (bf16[64,1024]{1,0:T(8,128)(2,1)}, bf16[64,1024]{1,0:T(8,128)(2,1)}, bf16[64,1024]{1,0:T(8,128)(2,1)}, bf16[64,1024]{1,0:T(8...) async-done(((bf16[64,1024]{1,0:T(8,128)(2,1)}, bf16[64,1024]{1,0:T(8,128)(2,1)}, bf16[64,1024]{1,0:T(8,128)(2,1)}, bf16[64,1024]{1,0:T(8,128)(2,1)}, ...) | async-done | bytes 1572880 | tf_op jit(solution)/shard_map/psum | solution.py:527
  (961 shorter events, 1003.6 us)
Async XLA Ops:
  7.2 75.9 %copy-start.11 = (bf16[1,384,1024]{2,1,0:T(8,128)(2,1)S(1)}, bf16[1,384,1024]{2,1,0:T(8,128)(2,1)}, u32[]{:S(2)}) copy-start(bf16[1,384,1024]{2,1,0:T(8,128)(2,1)} %param.24) | copy-start | bytes 2359300
  7.2 76.8 %all-gather.12.cloned.1.call-start = ((), (), s32[]{:S(2)}) async-start(), calls=%async_computation.16 | async-start | bytes 2228224 | tf_op jit(solution)/shard_map/all_gather | solution.py:316
  7.9 91.9 %all-gather.8.cloned.1.call-start = ((), (), s32[]{:S(2)}) async-start(), calls=%async_computation.14 | async-start | bytes 2228224 | tf_op jit(solution)/shard_map/all_gather | solution.py:313
  8.7 137.4 %all-gather.10.cloned.1.call-start = ((), (), s32[]{:S(2)}) async-start(), calls=%async_computation.15 | async-start | bytes 2228224 | tf_op jit(solution)/shard_map/all_gather | solution.py:315
  9.4 457.5 %all-gather.14.cloned.1.call-start = ((), (), s32[]{:S(2)}) async-start(), calls=%async_computation.17 | async-start | bytes 2228224 | tf_op jit(solution)/shard_map/all_gather | solution.py:318
  10.0 461.5 %all-gather.16.cloned.1.call-start = ((), (), s32[]{:S(2)}) async-start(), calls=%async_computation.18 | async-start | bytes 8912896 | tf_op jit(solution)/shard_map/all_gather | solution.py:360
  81.7 64.4 %copy-start.39 = (f32[1024]{0:T(1024)}, f32[1024]{0:T(1024)S(1)}, u32[]{:S(2)}) copy-start(f32[1024]{0:T(1024)S(1)} %convert_element_type.325) | copy-start | bytes 12292
  81.7 64.4 %copy-start.59 = (f32[1024]{0:T(1024)}, f32[1024]{0:T(1024)S(1)}, u32[]{:S(2)}) copy-start(f32[1024]{0:T(1024)S(1)} %convert_element_type.326) | copy-start | bytes 12292
  87.8 22.3 %all-to-all-start.2 = ((bf16[384,16,64]{0,2,1:T(8,128)(2,1)}), bf16[384,16,64]{0,2,1:T(8,128)(2,1)S(1)}, u32[]{:S(2)}, u32[]{:S(2)}) async-start(bf16[384,16,64]{0,2,1:T(8,128)(2,1)} %bitcast.50), calls=%async_computation.2 | async-start | bytes 1572864 | tf_op jit(solution)/shard_map/all_to_all | solution.py:340
  110.0 39.8 %all-to-all-start = ((bf16[384,16,64]{0,2,1:T(8,128)(2,1)}), bf16[384,16,64]{0,2,1:T(8,128)(2,1)S(1)}, u32[]{:S(2)}, u32[]{:S(2)}) async-start(bf16[384,16,64]{0,2,1:T(8,128)(2,1)} %bitcast.44), calls=%async_computation | async-start | bytes 1572864 | tf_op jit(solution)/shard_map/all_to_all | solution.py:334
  117.0 364.6 %all-gather.18.cloned.1.call-start = ((), (), s32[]{:S(2)}) async-start(), calls=%async_computation.19 | async-start | bytes 8912896 | tf_op jit(solution)/shard_map/all_gather | solution.py:362
  149.9 26.8 %all-to-all-start.1 = ((bf16[384,16,64]{0,2,1:T(8,128)(2,1)}), bf16[384,16,64]{0,2,1:T(8,128)(2,1)S(1)}, u32[]{:S(2)}, u32[]{:S(2)}) async-start(bf16[384,16,64]{0,2,1:T(8,128)(2,1)} %bitcast.47), calls=%async_computation.1 | async-start | bytes 1572864 | tf_op jit(solution)/shard_map/all_to_all | solution.py:337
  416.6 34.9 %all-to-all-start.3 = ((bf16[16,2,12288]{2,1,0:T(2,128)(2,1)}), bf16[16,2,12288]{2,1,0:T(2,128)(2,1)}, u32[]{:S(2)}, u32[]{:S(2)}) async-start(bf16[16,2,12288]{2,1,0:T(2,128)(2,1)} %reshape.955), calls=%async_computation.3 | async-start | bytes 1572864 | tf_op jit(solution)/shard_map/all_to_all | solution.py:353
  422.3 75.2 %copy-start.52 = (f32[1024]{0:T(1024)}, f32[1024]{0:T(1024)S(1)}, u32[]{:S(2)}) copy-start(f32[1024]{0:T(1024)S(1)} %convert_element_type.336) | copy-start | bytes 12292
  505.3 23.3 %all-to-all-start.4 = ((bf16[384,16,64]{0,2,1:T(8,128)(2,1)}), bf16[384,16,64]{0,2,1:T(8,128)(2,1)}, u32[]{:S(2)}, u32[]{:S(2)}) async-start(bf16[384,16,64]{0,2,1:T(8,128)(2,1)} %bitcast.548), calls=%async_computation.4 | async-start | bytes 1572864 | tf_op jit(solution)/shard_map/all_to_all | solution.py:420
  509.9 874.5 %reduce-scatter.13.cloned.1.call-start = ((), (), s32[]{:S(2)}) async-start(), calls=%async_computation.23 | async-start | bytes 2228224 | tf_op jit(solution)/shard_map/reduce_scatter | solution.py:501
  513.9 870.5 %reduce-scatter.11.cloned.1.call-start = ((), (), s32[]{:S(2)}) async-start(), calls=%async_computation.22 | async-start | bytes 2228224 | tf_op jit(solution)/shard_map/reduce_scatter | solution.py:495
  1182.4 202.0 %reduce-scatter.9.cloned.1.call-start = ((), (), s32[]{:S(2)}) async-start(), calls=%async_computation.21 | async-start | bytes 2228224 | tf_op jit(solution)/shard_map/reduce_scatter | solution.py:492
  1231.1 153.4 %reduce-scatter.7.cloned.1.call-start = ((), (), s32[]{:S(2)}) async-start(), calls=%async_computation.20 | async-start | bytes 2228224 | tf_op jit(solution)/shard_map/reduce_scatter | solution.py:486
  1278.1 201.9 %reduce-scatter.17.cloned.1.call-start = ((), (), s32[]{:S(2)}) async-start(), calls=%async_computation.25 | async-start | bytes 8912896 | tf_op jit(solution)/shard_map/reduce_scatter | solution.py:401
  1289.7 297.3 %reduce-scatter.15.cloned.1.call-start = ((), (), s32[]{:S(2)}) async-start(), calls=%async_computation.24 | async-start | bytes 8912896 | tf_op jit(solution)/shard_map/reduce_scatter | solution.py:395
  1300.1 340.9 %all-reduce.34.cloned.1.call-start = ((), (), s32[]{:S(2)}) async-start(), calls=%async_computation.26 | async-start | bytes 3145728 | tf_op jit(solution)/shard_map/psum | solution.py:527
  1311.5 275.6 %copy-start.21 = (bf16[1,384,1024]{2,1,0:T(8,128)(2,1)S(1)}, bf16[1,384,1024]{2,1,0:T(8,128)(2,1)}, u32[]{:S(2)}) copy-start(bf16[1,384,1024]{2,1,0:T(8,128)(2,1)} %param.25) | copy-start | bytes 2359300
  1311.5 275.5 %copy-start.45 = (f32[384]{0:T(512)S(1)}, f32[384]{0:T(512)}, u32[]{:S(2)}) copy-start(f32[384]{0:T(512)} %copy-done.44) | copy-start | bytes 4612
  (165 other events, 716.8 us)
Sparse Core Ops, SparseCore 0:
  10.2 44.2 all-gather.11
  56.6 43.1 all-gather.7
  102.0 44.0 all-gather.9
  148.1 47.2 all-gather.13
  197.4 73.0 all-gather.15
  272.5 72.9 all-gather.17
  514.4 63.1 reduce-scatter.12
  1182.5 62.0 reduce-scatter.10
  1248.3 60.7 reduce-scatter.8
  1312.7 60.8 reduce-scatter.6
  1377.6 102.3 reduce-scatter.16
  1483.9 103.0 reduce-scatter.14
  1589.7 51.2 all-reduce.33
where the time goes:
time: 1670 us; the launch traced here: 1660 us
  local copies, waits for them, and re-layouts  582 us (35%)
  matrix products  347 us (21%)
  waiting for transfers between devices  321 us (19%)
  blocking collectives  235 us (14%)
  other arithmetic  113 us (7%)
  starting transfers between devices  25.3 us (2%)
  loops' own time  17.8 us (1%)
  between operations  17.3 us (1%)
    unnamed x2, blocking collectives  124 us
    slice x48, local copies, waits for them, and re-layouts, listed_blocks(): lax.slice_in_dim(padded, 1, blocks_count + 1, axis=1)  114 us
    reduce_scatter x1, waiting for transfers between devices, local(): lax.psum_scatter(grad_up.astype(jnp.bfloat16), 'shard', scatter_dimension...  107 us
    dot_general x24, local copies, waits for them, and re-layouts, add_listed(): jnp.einsum('hqkn,hqkx->hnx', hot_float, rest_adds, precision=HIGHEST)  96.1 us
    reduce_scatter x1, waiting for transfers between devices, local(): lax.psum_scatter(grad_down.astype(jnp.bfloat16), 'shard', scatter_dimensi...  95.6 us
    another operation x26, local copies, waits for them, and re-layouts  82.5 us
    dot_general x12, matrix products, add_listed(): jnp.einsum('hqkn,hqkx->hnx', hot_float, rest_adds, precision=HIGHEST)  75.2 us
    reshape x24, local copies, waits for them, and re-layouts, listed_blocks(): rest = rest.reshape(heads_here, count, hot.shape[2], block_size, head_size)  74.4 us
  transfers between devices with their start and end apart: 18, of which 8 were waited for; matrix products, arithmetic and copies ran while one was open for 60% of the time, Pallas kernels for 0%

commit v1 on v0

v1 whole, which is shorter than its diff:
```python
import math

import jax
import jax.numpy as jnp
from jax import lax
from jax.experimental import pallas as pl
from jax.experimental.pallas import tpu as pltpu
from jax.sharding import PartitionSpec as P

BLK = 64
DH = 64
SLOTS = 8
EPSILON = 1e-05
FAR = -1e20
BF = jnp.bfloat16
F32 = jnp.float32
VMEM_LIMIT = 56 * 1024 * 1024


def dot_nn(left, right):
    return lax.dot_general(left, right, (((1,), (0,)), ((), ())), preferred_element_type=F32)


def dot_tn(left, right):
    return lax.dot_general(left, right, (((0,), (0,)), ((), ())), preferred_element_type=F32)


def dot_nt(left, right):
    return lax.dot_general(left, right, (((1,), (1,)), ((), ())), preferred_element_type=F32)


def params(*semantics):
    return pltpu.CompilerParams(
        dimension_semantics=semantics if semantics else None, vmem_limit_bytes=VMEM_LIMIT
    )


def lanes_of(shape):
    return lax.broadcasted_iota(jnp.int32, shape, len(shape) - 1)


def normalize(values):
    centre = jnp.mean(values, axis=-1, keepdims=True)
    centred = values - centre
    spread = jnp.mean(centred * centred, axis=-1, keepdims=True)
    scale = lax.rsqrt(spread + EPSILON)
    return centred * scale, scale


def norm_backward(grad, normal, scale, gain):
    scaled = grad * gain
    mean_one = jnp.mean(scaled, axis=-1, keepdims=True)
    mean_two = jnp.mean(scaled * normal, axis=-1, keepdims=True)
    return scale * (scaled - mean_one - normal * mean_two)


def key_blocks(random_heads, global_ids):
    blocks_count = random_heads.shape[0]
    position = jnp.arange(blocks_count, dtype=jnp.int32)
    window = jnp.stack([position - 1, position, position + 1], axis=1)
    global_all = jnp.broadcast_to(global_ids[None, :], (blocks_count, global_ids.shape[0]))
    listed = jnp.concatenate([window, random_heads, global_all], axis=1)
    slot_count = listed.shape[1]
    earlier = jnp.arange(slot_count)[:, None] > jnp.arange(slot_count)[None, :]
    repeated = jnp.any((listed[..., :, None] == listed[..., None, :]) & earlier, axis=-1)
    usable = (listed >= 0) & (listed < blocks_count) & jnp.logical_not(repeated)
    return jnp.where(usable, listed, blocks_count)


def project_kernel(
    tok_ref, w_ref, bias_ref, norm_ref, qext_ref, kext_ref, n_ref, q_ref, k_ref, v_ref
):
    normal, _ = normalize(tok_ref[...].astype(F32))
    normed = (normal * norm_ref[0:1, :] + norm_ref[1:2, :]).astype(BF)
    n_ref[...] = normed
    out = dot_nn(normed, w_ref[...]) + bias_ref[0:1, :]
    out = out.astype(BF).astype(F32)
    both = out[:, :128]
    lane = lanes_of(both.shape)
    q_ref[...] = jnp.where(lane < DH, both * (1.0 / math.sqrt(DH)), qext_ref[...].astype(F32)).astype(BF)
    k_ref[...] = jnp.where(lane < DH, pltpu.roll(both, DH, 1), kext_ref[...].astype(F32)).astype(BF)
    v_ref[...] = out[:, 128:].astype(BF)


def project(tokens, weight, bias, norm_rows, query_extra, key_extra):
    total, width = tokens.shape
    tile = min(512, total)
    row = lambda n: pl.BlockSpec((tile, n), lambda i: (i, 0))
    whole = lambda a: pl.BlockSpec(a.shape, lambda i: (0,) * a.ndim)
    table = jax.ShapeDtypeStruct((total, 128), BF)
    return pl.pallas_call(
        project_kernel,
        grid=(total // tile,),
        in_specs=[row(width), whole(weight), whole(bias), whole(norm_rows), row(128), row(128)],
        out_specs=[row(width), row(128), row(128), row(128)],
        out_shape=[jax.ShapeDtypeStruct((total, width), BF), table, table, table],
        compiler_params=params("arbitrary"),
        name="project",
    )(tokens, weight, bias, norm_rows, query_extra, key_extra)


def load_tables(pairs, sem):
    copies = [
        pltpu.make_async_copy(src, dst, sem.at[i]) for i, (src, dst) in enumerate(pairs)
    ]
    for copy in copies:
        copy.start()
    for copy in copies:
        copy.wait()


def fill_null(k_ref, v_ref, rows):
    lane = lanes_of((BLK, 128))
    k_ref[rows : rows + BLK, :] = jnp.where(
        (lane >= DH) & (lane < DH + 8), FAR, 0.0
    ).astype(BF)
    v_ref[rows : rows + BLK, :] = jnp.zeros((BLK, 128), BF)


def gather_rows(idx_ref, block, ref):
    pieces = []
    for slot in range(SLOTS):
        start = pl.multiple_of(idx_ref[block * SLOTS + slot] * BLK, BLK)
        pieces.append(ref[pl.ds(start, BLK), :])
    return jnp.concatenate(pieces, axis=0)


def softmax_rows(scores):
    top = jnp.max(scores, axis=1, keepdims=True)
    raised = jnp.exp(scores - top)
    return raised * (1.0 / jnp.sum(raised, axis=1, keepdims=True))


def attend_kernel(idx_ref, q_hbm, k_hbm, v_hbm, o_ref, q_ref, k_ref, v_ref, sem):
    rows = q_hbm.shape[0]
    load_tables(
        [
            (q_hbm, q_ref),
            (k_hbm, k_ref.at[pl.ds(0, rows)]),
            (v_hbm, v_ref.at[pl.ds(0, rows)]),
        ],
        sem,
    )
    fill_null(k_ref, v_ref, rows)
    owners, half, _ = o_ref.shape
    per = half // BLK
    lane = lanes_of((BLK, 128))

    def one(block):
        keys = gather_rows(idx_ref, block, k_ref)
        query = q_ref[pl.ds(pl.multiple_of(block * BLK, BLK), BLK), :]
        chances = softmax_rows(dot_nt(query, keys)).astype(BF)
        return dot_nn(chances, gather_rows(idx_ref, block, v_ref))

    def step(owner, carry):
        for part in range(per):
            first = owner * (2 * per) + part
            low, high = one(first), one(first + per)
            o_ref[owner, part * BLK : (part + 1) * BLK, :] = jnp.where(lane < DH, low, high).astype(BF)
        return carry

    lax.fori_loop(0, owners, step, 0)


def attend(idx, query, keys, values, owners):
    rows = query.shape[0]
    anywhere = pl.BlockSpec(memory_space=pl.ANY)
    return pl.pallas_call(
        attend_kernel,
        in_specs=[pl.BlockSpec(memory_space=pltpu.SMEM), anywhere, anywhere, anywhere],
        out_specs=pl.BlockSpec(memory_space=pltpu.VMEM),
        out_shape=jax.ShapeDtypeStruct((owners, rows // owners // 2, 128), BF),
        scratch_shapes=[
            pltpu.VMEM((rows, 128), BF),
            pltpu.VMEM((rows + BLK, 128), BF),
            pltpu.VMEM((rows + BLK, 128), BF),
            pltpu.SemaphoreType.DMA((3,)),
        ],
        compiler_params=params(),
        name="attend",
    )(idx, query, keys, values)


def attend_back_kernel(
    idx_ref, q_hbm, k_hbm, v_hbm, g_hbm, d_ref, q_ref, k_ref, v_ref, g_ref, dk_ref, dv_ref, sem
):
    rows = q_hbm.shape[0]
    load_tables(
        [
            (q_hbm, q_ref),
            (k_hbm, k_ref.at[pl.ds(0, rows)]),
            (v_hbm, v_ref.at[pl.ds(0, rows)]),
            (g_hbm, g_ref),
        ],
        sem,
    )
    fill_null(k_ref, v_ref, rows)
    dk_ref[...] = jnp.zeros_like(dk_ref)
    dv_ref[...] = jnp.zeros_like(dv_ref)
    owners, half, _ = g_ref.shape
    per = half // BLK
    lane = lanes_of((BLK, 128))

    def one(block, grad):
        keys = gather_rows(idx_ref, block, k_ref)
        values = gather_rows(idx_ref, block, v_ref)
        at = pl.ds(pl.multiple_of(block * BLK, BLK), BLK)
        query = q_ref[at, :]
        chances = softmax_rows(dot_nt(query, keys))
        grad_chances = dot_nt(grad, values)
        inner = jnp.sum(chances * grad_chances, axis=1, keepdims=True)
        grad_scores = (chances * (grad_chances - inner)).astype(BF)
        grad_query = dot_nn(grad_scores, keys) * (1.0 / math.sqrt(DH))
        d_ref[at, 0:128] = jnp.where(lane < DH, grad_query, 0.0).astype(BF)
        key_adds = dot_tn(grad_scores, query)
        value_adds = dot_tn(chances.astype(BF), grad)
        for slot in range(SLOTS):
            start = pl.multiple_of(idx_ref[block * SLOTS + slot] * BLK, BLK)
            cut = slice(slot * BLK, (slot + 1) * BLK)
            dk_ref[pl.ds(start, BLK), :] += key_adds[cut]
            dv_ref[pl.ds(start, BLK), :] += value_adds[cut]

    def step(owner, carry):
        for part in range(per):
            first = owner * (2 * per) + part
            grad = g_ref[owner, part * BLK : (part + 1) * BLK, :]
            zero = jnp.zeros_like(grad)
            one(first, jnp.where(lane < DH, grad, zero))
            one(first + per, jnp.where(lane < DH, zero, grad))
        return carry

    lax.fori_loop(0, owners, step, 0)

    chunk = 512

    def finish(i, carry):
        at = pl.ds(pl.multiple_of(i * chunk, chunk), chunk)
        wide = lanes_of((chunk, 128))
        grad_keys = pltpu.roll(dk_ref[at, :], DH, 1)
        grad_query = d_ref[at, 0:128].astype(F32)
        d_ref[at, 0:128] = jnp.where(wide < DH, grad_query, grad_keys).astype(BF)
        grad_values = dv_ref[at, :]
        grad_values = grad_values + pltpu.roll(grad_values, DH, 1)
        d_ref[at, 128:256] = jnp.where(wide < DH, grad_values, 0.0).astype(BF)
        return carry

    lax.fori_loop(0, rows // chunk, finish, 0)


def attend_back(idx, query, keys, values, grads):
    rows = query.shape[0]
    anywhere = pl.BlockSpec(memory_space=pl.ANY)
    return pl.pallas_call(
        attend_back_kernel,
        in_specs=[pl.BlockSpec(memory_space=pltpu.SMEM)] + [anywhere] * 4,
        out_specs=pl.BlockSpec(memory_space=pltpu.VMEM),
        out_shape=jax.ShapeDtypeStruct((rows, 256), BF),
        scratch_shapes=[
            pltpu.VMEM((rows, 128), BF),
            pltpu.VMEM((rows + BLK, 128), BF),
            pltpu.VMEM((rows + BLK, 128), BF),
            pltpu.VMEM(grads.shape, BF),
            pltpu.VMEM((rows + BLK, 128), F32),
            pltpu.VMEM((rows + BLK, 128), F32),
            pltpu.SemaphoreType.DMA((4,)),
        ],
        compiler_params=params(),
        name="attend_back",
    )(idx, query, keys, values, grads)


def middle_kernel(
    att_ref,
    tok_ref,
    cot_ref,
    down_ref,
    up_ref,
    out_w_ref,
    vec_ref,
    lay_ref,
    gm_ref,
    ga_ref,
    gv_ref,
    grads_hbm,
    a_ref,
    mid_ref,
    n2_ref,
    acc_ref,
    gn_ref,
    gd_buf,
    gu_buf,
    sem,
):
    chunk = pl.program_id(0)
    chunks = pl.num_programs(0)
    slot = lax.rem(chunk, 2)
    owners, half, _ = att_ref.shape
    lane = lanes_of((half, 128))
    width = tok_ref.shape[1]
    up_rows = up_ref.shape[1]
    down_block = down_ref.shape[0]
    down_rows = down_ref.shape[1]

    def copies(at, place):
        return (
            pltpu.make_async_copy(
                gd_buf.at[place],
                grads_hbm.at[pl.ds(at * down_block, down_block), pl.ds(0, down_rows)],
                sem.at[0, place],
            ),
            pltpu.make_async_copy(
                gu_buf.at[place],
                grads_hbm.at[:, pl.ds(down_rows + at * up_rows, up_rows)],
                sem.at[1, place],
            ),
        )

    @pl.when(chunk == 0)
    def _():
        for pair in range(owners // 2):
            one = att_ref[2 * pair].astype(F32)
            two = att_ref[2 * pair + 1].astype(F32)
            cut = slice(pair * 128, (pair + 1) * 128)
            a_ref[0:half, cut] = jnp.where(lane < DH, one, pltpu.roll(two, DH, 1)).astype(BF)
            a_ref[half : 2 * half, cut] = jnp.where(lane < DH, pltpu.roll(one, DH, 1), two).astype(BF)
        mid = (
            tok_ref[...].astype(F32)
            + dot_nn(a_ref[...], out_w_ref[...].reshape(width, width))
            + vec_ref[0:1, :]
        )
        mid_ref[...] = mid
        normal, _ = normalize(mid)
        n2_ref[...] = (normal * vec_ref[1:2, :] + vec_ref[2:3, :]).astype(BF)

    @pl.when(chunk >= 2)
    def _():
        for copy in copies(chunk - 2, slot):
            copy.wait()

    w_up = up_ref[...].reshape(width, -1)
    w_down = down_ref[...].reshape(-1, width)
    cot = cot_ref[...]
    n2 = n2_ref[...]
    pre = dot_nn(n2, w_up) + vec_ref[pl.ds(4 + chunk, 1), :]
    root = math.sqrt(2.0 / math.pi)
    square = pre * pre
    bent = jnp.tanh(root * (pre + 0.044715 * (pre * square)))
    hidden = (0.5 * pre * (1.0 + bent)).astype(BF)
    slope = 0.5 * (1.0 + bent) + 0.5 * pre * (1.0 - bent * bent) * (
        root * (1.0 + (3 * 0.044715) * square)
    )
    grad_pre32 = slope * dot_nt(cot, w_down)
    grad_pre = grad_pre32.astype(BF)
    more = dot_nn(hidden, w_down)
    grad_more = dot_nt(grad_pre, w_up)
    first = chunk == 0
    acc_ref[...] = jnp.where(first, more, acc_ref[...] + more)
    gn_ref[...] = jnp.where(first, grad_more, gn_ref[...] + grad_more)
    gv_ref[pl.ds(4 + chunk, 1), :] = jnp.sum(grad_pre.astype(F32), axis=0, keepdims=True)
    gu_buf[slot] = dot_tn(n2, grad_pre).astype(BF).reshape(gu_buf.shape[1:])
    gd_buf[slot] = dot_tn(hidden, cot).astype(BF).reshape(gd_buf.shape[1:])
    for copy in copies(chunk, slot):
        copy.start()

    @pl.when(chunk == chunks - 1)
    def _():
        mid = mid_ref[...]
        lay_ref[...] = (mid + acc_ref[...] + vec_ref[3:4, :]).astype(BF)
        normal, scale = normalize(mid)
        grad = gn_ref[...]
        cot32 = cot.astype(F32)
        grad_mid = cot32 + norm_backward(grad, normal, scale, vec_ref[1:2, :])
        gm_ref[...] = grad_mid
        branch = grad_mid.astype(BF)
        gv_ref[0:1, :] = jnp.sum(branch.astype(F32), axis=0, keepdims=True)
        gv_ref[1:2, :] = jnp.sum(grad * normal, axis=0, keepdims=True)
        gv_ref[2:3, :] = jnp.sum(grad, axis=0, keepdims=True)
        gv_ref[3:4, :] = jnp.sum(cot32, axis=0, keepdims=True)
        grad_att = dot_nt(branch, out_w_ref[...].reshape(width, width))
        for pair in range(owners // 2):
            cut = slice(pair * 128, (pair + 1) * 128)
            top, low = grad_att[0:half, cut], grad_att[half : 2 * half, cut]
            ga_ref[2 * pair] = jnp.where(lane < DH, top, pltpu.roll(low, DH, 1)).astype(BF)
            ga_ref[2 * pair + 1] = jnp.where(lane < DH, pltpu.roll(top, DH, 1), low).astype(BF)
        for copy in copies(chunk - 1, 1 - slot):
            copy.wait()
        gu_buf[1 - slot] = dot_tn(a_ref[...], branch).astype(BF).reshape(gu_buf.shape[1:])
        last = pltpu.make_async_copy(
            gu_buf.at[1 - slot],
            grads_hbm.at[:, pl.ds(down_rows + chunks * up_rows, up_rows)],
            sem.at[1, 1 - slot],
        )
        last.start()
        for copy in copies(chunk, slot):
            copy.wait()
        last.wait()


def middle(attended, tokens, cotangent, weights, vectors):
    owners, per_owner, width = weights.shape
    count = tokens.shape[0]
    up_rows = width // owners
    chunks = (per_owner - up_rows) // (2 * up_rows)
    down_rows = chunks * up_rows
    down_block = owners // chunks
    whole = lambda a: pl.BlockSpec(a.shape, lambda c: (0,) * a.ndim)
    full = lambda s: pl.BlockSpec(s, lambda c: (0,) * len(s))
    first_up = down_rows // up_rows
    return pl.pallas_call(
        middle_kernel,
        grid=(chunks,),
        in_specs=[
            whole(attended),
            whole(tokens),
            whole(cotangent),
            pl.BlockSpec((down_block, down_rows, width), lambda c: (c, 0, 0)),
            pl.BlockSpec((owners, up_rows, width), lambda c: (0, first_up + c, 0)),
            pl.BlockSpec((owners, up_rows, width), lambda c: (0, first_up + chunks, 0)),
            whole(vectors),
        ],
        out_specs=[
            full((count, width)),
            full((count, width)),
            full(attended.shape),
            full((8, width)),
            pl.BlockSpec(memory_space=pl.ANY),
        ],
        out_shape=[
            jax.ShapeDtypeStruct((count, width), BF),
            jax.ShapeDtypeStruct((count, width), F32),
            jax.ShapeDtypeStruct(attended.shape, BF),
            jax.ShapeDtypeStruct((8, width), F32),
            jax.ShapeDtypeStruct(weights.shape, BF),
        ],
        scratch_shapes=[
            pltpu.VMEM((count, width), BF),
            pltpu.VMEM((count, width), F32),
            pltpu.VMEM((count, width), BF),
            pltpu.VMEM((count, width), F32),
            pltpu.VMEM((count, width), F32),
            pltpu.VMEM((2, down_block, down_rows, width), BF),
            pltpu.VMEM((2, owners, up_rows, width), BF),
            pltpu.SemaphoreType.DMA((2, 2)),
        ],
        compiler_params=params("arbitrary"),
        name="middle",
    )(attended, tokens, cotangent, weights, weights, weights, vectors)


def project_back_kernel(n_ref, d_ref, w_ref, part_ref, dw_ref, db_ref):
    grads = d_ref[...]
    part_ref[...] = dot_nt(grads, w_ref[...]).astype(BF)
    more = dot_tn(n_ref[...], grads)
    sums = jnp.broadcast_to(jnp.sum(grads.astype(F32), axis=0, keepdims=True), db_ref.shape)

    @pl.when(pl.program_id(0) == 0)
    def _():
        dw_ref[...] = more
        db_ref[...] = sums

    @pl.when(pl.program_id(0) > 0)
    def _():
        dw_ref[...] += more
        db_ref[...] += sums


def project_back(normed, grads, weight):
    total, width = normed.shape
    tile = min(512, total)
    row = lambda n: pl.BlockSpec((tile, n), lambda i: (i, 0))
    whole = lambda s: pl.BlockSpec(s, lambda i: (0,) * len(s))
    return pl.pallas_call(
        project_back_kernel,
        grid=(total // tile,),
        in_specs=[row(width), row(256), whole(weight.shape)],
        out_specs=[row(width), whole((width, 256)), whole((8, 256))],
        out_shape=[
            jax.ShapeDtypeStruct((total, width), BF),
            jax.ShapeDtypeStruct((width, 256), F32),
            jax.ShapeDtypeStruct((8, 256), F32),
        ],
        compiler_params=params("arbitrary"),
        name="project_back",
    )(normed, grads, weight)


def last_kernel(tok_ref, gn_ref, gm_ref, norm_ref, out_ref):
    normal, scale = normalize(tok_ref[...].astype(F32))
    grad = norm_backward(gn_ref[...].astype(F32), normal, scale, norm_ref[0:1, :])
    out_ref[...] = (gm_ref[...] + grad).astype(BF)


def last(tokens, grad_normed, grad_middle, norm_rows):
    return pl.pallas_call(
        last_kernel,
        out_shape=jax.ShapeDtypeStruct(tokens.shape, BF),
        compiler_params=params(),
        name="last",
    )(tokens, grad_normed, grad_middle, norm_rows)


def exchange(table):
    return lax.all_to_all(table, "shard", split_axis=0, concat_axis=0, tiled=True)


def over_rep(table):
    reps = lax.axis_size("rep")
    if reps == 1:
        return table.astype(F32)
    if reps == 2:
        other = lax.ppermute(table, "rep", [(0, 1), (1, 0)])
        return table.astype(F32) + other.astype(F32)
    return lax.psum(table, "rep").astype(F32)


def local(
    tokens,
    cotangent,
    seg_ids,
    random_blocks,
    global_blocks,
    ln1_gain,
    ln1_bias,
    w_query,
    b_query,
    w_key,
    w_value,
    b_value,
    w_out,
    b_out,
    ln2_gain,
    ln2_bias,
    w_up,
    b_up,
    w_down,
    b_down,
):
    tokens, cotangent, seg_row = tokens[0], cotangent[0], seg_ids[0]
    count, width = tokens.shape
    owners = lax.axis_size("shard")
    own = width // owners
    hidden = w_up.shape[1]
    chunks = hidden // width

    tiles = jnp.concatenate(
        [w.reshape(own, owners, DH) for w in (w_query, w_key, w_value)], axis=2
    ).transpose(1, 0, 2)
    small = jnp.concatenate([b_out, ln2_gain, ln2_bias, b_down, ln1_gain, ln1_bias, b_up])
    small = jnp.pad(small, (0, own * DH - small.shape[0])).reshape(1, own, DH)
    sent = jnp.concatenate([tiles, jnp.broadcast_to(small, (owners, own, DH))], axis=2)
    got = exchange(sent)
    weight = jnp.concatenate([got[:, :, : 3 * DH], got[:, :, 2 * DH : 3 * DH]], axis=2)
    weight = weight.reshape(width, 4 * DH)
    rows = got[:, :, 3 * DH :].reshape(owners, own * DH)[:, : 6 * own + hidden // owners]
    rows = rows.astype(F32)
    fixed = rows[:, : 6 * own].reshape(owners, 6, own).transpose(1, 0, 2).reshape(6, width)
    up_bias = rows[:, 6 * own :].reshape(chunks, width)
    vectors = jnp.concatenate([fixed[:4], up_bias], axis=0)
    norm_rows = jnp.pad(fixed[4:6], ((0, 6), (0, 0)))
    zero = jnp.zeros((DH,), F32)
    bias = jnp.concatenate([b_query.astype(F32), zero, b_value.astype(F32), b_value.astype(F32)])
    bias = jnp.broadcast_to(bias[None], (8, 4 * DH))

    everyone = lax.all_gather(tokens, "shard", axis=0, tiled=True)
    mine = jnp.concatenate(
        [
            w_down,
            w_up.reshape(own, chunks, width).transpose(1, 0, 2).reshape(own * chunks, width),
            w_out,
        ],
        axis=0,
    )
    weights = lax.all_gather(mine, "shard", axis=0)

    lane = jnp.arange(128, dtype=jnp.int32)[None, :] - DH
    seg_column = seg_row[:, None]
    same = lane == seg_column
    query_extra = same.astype(BF)
    key_extra = jnp.where((lane >= 0) & (lane < 8) & ~same, FAR, 0.0).astype(BF)
    idx = key_blocks(random_blocks[0, 0], global_blocks[0]).reshape(-1)

    normed, query, keys, values = project(
        everyone, weight, bias, norm_rows, query_extra, key_extra
    )
    attended = exchange(attend(idx, query, keys, values, owners))
    layer_out, grad_middle, grad_attended, grad_rows, grads = middle(
        attended, tokens, cotangent, weights, vectors
    )
    shares = lax.psum_scatter(
        grads.reshape(-1, width), "shard", scatter_dimension=0, tiled=True
    )
    grad_table = attend_back(idx, query, keys, values, exchange(grad_attended))
    part, grad_weight, grad_bias = project_back(normed, grad_table, weight)
    grad_normed = lax.psum_scatter(part, "shard", scatter_dimension=0, tiled=True)
    grad_tokens = last(tokens, grad_normed, grad_middle, norm_rows)

    used = weight.astype(F32)[:, : 3 * DH]
    sums = grad_bias[0:1, : 3 * DH]
    spread = grad_weight[:, : 3 * DH] - fixed[5][:, None] * sums
    grad_gain = jnp.sum(used * spread, axis=1) / fixed[4]
    grad_shift = jnp.sum(used * sums, axis=1)
    lines = jnp.concatenate([grad_rows[:4], grad_gain[None], grad_shift[None]], axis=0)
    lines = lines.reshape(6, owners, own).transpose(1, 0, 2).reshape(owners, 6 * own)
    lines = jnp.concatenate([lines, grad_rows[4:].reshape(owners, hidden // owners)], axis=1)
    length = lines.shape[1]
    lines = jnp.pad(lines, ((0, 0), (0, own * DH - length))).reshape(owners, own, DH)
    back = jnp.concatenate(
        [grad_weight[:, : 3 * DH].reshape(owners, own, 3 * DH), lines], axis=2
    ).astype(BF)
    back = exchange(back)
    back_sum = jnp.sum(back[:, :, 3 * DH :].astype(F32), axis=0).reshape(own * DH)[:length]
    heads = over_rep(back[:, :, : 3 * DH])
    heads = heads.transpose(1, 2, 0).reshape(own, 3, DH, owners).transpose(1, 0, 3, 2)
    heads = heads.reshape(3, own, width)
    tail = over_rep(
        jnp.concatenate([back_sum, grad_bias[0, :DH], grad_bias[0, 2 * DH : 3 * DH]]).astype(BF)
    )
    piece = lambda i: tail[i * own : (i + 1) * own]
    shares = over_rep(shares)
    down_rows = chunks * own
    grad_down = shares[:down_rows]
    grad_up = shares[down_rows : 2 * down_rows].reshape(chunks, own, width)
    grad_up = grad_up.transpose(1, 0, 2).reshape(own, hidden)
    grad_out = shares[2 * down_rows :]
    return (
        layer_out[None],
        grad_tokens[None],
        piece(4),
        piece(5),
        heads[0],
        tail[length : length + DH],
        heads[1],
        heads[2],
        tail[length + DH :],
        grad_out,
        piece(0),
        piece(1),
        piece(2),
        grad_up,
        tail[6 * own : length],
        grad_down,
        piece(3),
    )


def solution(mesh):
    rows = P("rep", "shard", None)
    one, two = P("shard"), P("shard", None)
    return jax.shard_map(
        local,
        mesh=mesh,
        in_specs=(
            rows, rows, P("rep", None), P("rep", "shard", None, None), P("rep", None),
            one, one, two, one, two, two, one, two, one, one, one, two, one, two, one,
        ),
        out_specs=(
            rows, rows, one, one, two, one, two, two, one, two, one, one, one, two, one, two, one,
        ),
        check_vma=False,
    )
```

time: 1670 us -> 628 us (0.38)
  local copies, waits for them, and re-layouts: 582 us -> 17.8 us
  matrix products: 347 us -> 0 us
  blocking collectives: 235 us -> 28 us
  Pallas kernels: 0 us -> 176 us
  other arithmetic: 113 us -> 15.5 us
  waiting for transfers between devices: 321 us -> 356 us
  loops' own time: 17.8 us -> 0 us
    dot_general x108 -> x0, matrix products: 347 us -> none  [the longest x12 75.2 us: add_listed(): jnp.einsum('hqkn,hqkx->hnx', hot_float, rest_adds, precision=HIGHEST)]
    pallas_call x0 -> x6, Pallas kernels: none -> 176 us  [the longest x1 61.6 us: attend_back(): pl.pallas_call(attend_back_kernel, in_specs=[pl.BlockSpec(memory_space=pl...]
    slice x62 -> x23, local copies, waits for them, and re-layouts: 139 us -> 4.76 us  [the longest x1 1.16 us: local(): grad_down = shares[:down_rows]]
    unnamed x2 -> x0, blocking collectives: 124 us -> none
    another operation x50 -> x0, local copies, waits for them, and re-layouts: 105 us -> none
    dot_general x24 -> x0, local copies, waits for them, and re-layouts: 96.1 us -> none  [add_listed(): jnp.einsum('hqkn,hqkx->hnx', hot_float, rest_adds, precision=HIGHEST)]
    reshape x24 -> x14, local copies, waits for them, and re-layouts: 74.4 us -> 3.61 us  [the longest x1 1.11 us: local(): w_up.reshape(own, chunks, width).transpose(1, 0, 2)]
    all_gather x6 -> x2, waiting for transfers between devices: 36.5 us -> 96.9 us  [the longest x1 78.4 us: local(): everyone = lax.all_gather(tokens, 'shard', axis=0, tiled=True)]
  transfers between devices with their start and end apart: 18 -> 10, of which waited for: 8 -> 8; matrix products, arithmetic and copies ran while one was open for 60% -> 4% of each run, Pallas kernels for 0% -> 22%
where the time goes in v1:
time: 628 us; the launch traced here: 627 us
  waiting for transfers between devices  356 us (57%)
  Pallas kernels  176 us (28%)
  blocking collectives  28 us (4%)
  starting transfers between devices  19.4 us (3%)
  local copies, waits for them, and re-layouts  17.8 us (3%)
  other arithmetic  15.5 us (2%)
  between operations  14.4 us (2%)
    reduce_scatter x1, waiting for transfers between devices, local(): lax.psum_scatter(part, 'shard', scatter_dimension=0, tiled=True)  93 us
    reduce_scatter x1, waiting for transfers between devices, local(): lax.psum_scatter(grads.reshape(-1, width), 'shard', scatter_dimension=0,...  86.8 us
    all_gather x1, waiting for transfers between devices, local(): everyone = lax.all_gather(tokens, 'shard', axis=0, tiled=True)  78.4 us
    pallas_call x1, Pallas kernels, attend_back(): pl.pallas_call(attend_back_kernel, in_specs=[pl.BlockSpec(memory_space=pl...  61.6 us
    all_to_all x3, waiting for transfers between devices, exchange(): lax.all_to_all(table, 'shard', split_axis=0, concat_axis=0, tiled=True)  44.8 us
    pallas_call x1, Pallas kernels, attend(): pl.pallas_call(attend_kernel, in_specs=[pl.BlockSpec(memory_space=pltpu.S...  38.2 us
    pallas_call x1, Pallas kernels, middle(): pl.pallas_call(middle_kernel, grid=(chunks,), in_specs=[whole(attended),...  35.8 us
    ppermute x3, waiting for transfers between devices, over_rep(): other = lax.ppermute(table, 'rep', [(0, 1), (1, 0)])  33.5 us
  transfers between devices with their start and end apart: 10, of which 8 were waited for; matrix products, arithmetic and copies ran while one was open for 4% of the time, Pallas kernels for 22%

profile of v1, /device:TPU:0, one launch (start us, length us, event | category | flops | bytes accessed | tf_op | source)
XLA Modules:
  0.0 626.9 jit_solution(5321734208407071828)
XLA Ops:
  9.1 2.3 pad_maximum_fusion
  13.8 7.4 %all-to-all-start = ((bf16[16,64,256]{2,1,0:T(8,128)(2,1)}), bf16[16,64,256]{2,1,0:T(8,128)(2,1)S(1)}, u32[]{:S(2)}, u32[]{:S(2)}) async-start(bf16[16,64,256]{2,1,0:T(8,128)(2,1)} %pad_maximum_fusion.1), calls=%async_computation | async-start | bytes 1048576 | tf_op jit(solution)/shard_map/all_to_all | solution.py:503
  22.7 3.6 select_convert_fusion.kext_ref
  26.3 3.5 compare_convert_fusion.qext_ref
  29.7 14.4 %all-to-all-done = bf16[16,64,256]{2,1,0:T(8,128)(2,1)S(1)} async-done(((bf16[16,64,256]{2,1,0:T(8,128)(2,1)}), bf16[16,64,256]{2,1,0:T(8,128)(2,1)S(1)}, u32[]{:S(2)}, u32[]{:S(2)}) %all-to-all-start) | async-done | bytes 524320 | tf_op jit(solution)/shard_map/all_to_all | solution.py:503
  46.3 78.4 %all-gather.5.cloned.1.call-done = bf16[1,6144,1024]{2,1,0:T(8,128)(2,1)} async-done(((bf16[1,384,1024]{2,1,0:T(8,128)(2,1)}), bf16[1,6144,1024]{2,1,0:T(8,128)(2,1)}) %all-gather.5.cloned.1.call-update) | async-done | bytes 12582928 | tf_op jit(solution)/shard_map/all_gather | solution.py:564
  125.3 19.0 %project.1 = (bf16[6144,1024]{1,0:T(8,128)(2,1)}, bf16[6144,128]{1,0:T(8,128)(2,1)}, bf16[6144,128]{1,0:T(8,128)(2,1)}, bf16[6144,128]{1,0:T(8,128)(2,1)}) custom-call(bf16[6144,1024]{1,0:T(8,128)(2,1)} %bitcast.53, bf16[1024,256]{1,0:T(8,128)(2,1)} %bitcast.54, f32[8,256]{1,0:T(8,128)} %broadcast_in_dim.52.bias_ref, f32[8,1024]{1,0:T(8,128)} %pad.14.norm_ref, ...), custom_call_target="tpu_custom_call" | custom-call | tf_op jit(solution)/shard_map/project/pallas_call | solution.py:91
  144.3 38.2 %attend.1 = bf16[16,192,128]{2,1,0:T(8,128)(2,1)} custom-call(s32[768]{0:T(1024)} %and_select_fusion.idx_ref, bf16[6144,128]{1,0:T(8,128)(2,1)} %get-tuple-element.29.q_hbm, bf16[6144,128]{1,0:T(8,128)(2,1)} %get-tuple-element.30.k_hbm, bf16[6144,128]{1,0:T(8,128)(2,1)} %get-tuple-element.31.v_hbm), custom_call_target="tpu_custom_call" | custom-call | tf_op jit(solution)/shard_map/attend/pallas_call | solution.py:168
  182.5 3.6 all-to-all-start.1
  187.1 30.5 %all-to-all-done.1.att_ref = bf16[16,192,128]{2,1,0:T(8,128)(2,1)S(1)} async-done(((bf16[16,192,128]{2,1,0:T(8,128)(2,1)}), bf16[16,192,128]{2,1,0:T(8,128)(2,1)S(1)}, u32[]{:S(2)}, u32[]{:S(2)}) %all-to-all-start.1) | async-done | bytes 786464 | tf_op jit(solution)/shard_map/all_to_all | solution.py:503
  217.6 18.5 %all-gather.7.cloned.1.call-done = bf16[9216,1024]{1,0:T(8,128)(2,1)} async-done(((bf16[576,1024]{1,0:T(8,128)(2,1)}), bf16[9216,1024]{1,0:T(8,128)(2,1)}) %all-gather.7.cloned.1.call-update) | async-done | bytes 18874384 | tf_op jit(solution)/shard_map/all_gather | solution.py:573
  236.1 35.8 %middle.1 = (bf16[384,1024]{1,0:T(8,128)(2,1)}, f32[384,1024]{1,0:T(8,128)}, bf16[16,192,128]{2,1,0:T(8,128)(2,1)}, f32[8,1024]{1,0:T(8,128)}, bf16[16,576,1024]{2,1,0:T(8,128)(2,1)}) custom-call(bf16[16,192,128]{2,1,0:T(8,128)(2,1)} %copy-done.1, bf16[384,1024]{1,0:T(8,128)(2,1)} %bitcast.57, bf16[384,1024]{1,0:T(8,128)(2,1)} %bitcast.67, ...), custom_call_target="tpu_custom_call" | custom-call | tf_op jit(solution)/shard_map/middle/pallas_call | solution.py:409
  273.1 28.0 %all_to_all.20.g_hbm = bf16[16,192,128]{2,1,0:T(8,128)(2,1)} all-to-all(bf16[16,192,128]{2,1,0:T(8,128)(2,1)S(1)} %copy-done.4), channel_id=1, replica_groups=mesh['rep'=2,'shard'=16] {'shard'}, dimensions={0} | all-to-all | bytes 1572864 | tf_op jit(solution)/shard_map/all_to_all | solution.py:503
  301.1 61.6 %attend_back.1.d_ref = bf16[6144,256]{1,0:T(8,128)(2,1)} custom-call(s32[768]{0:T(1024)} %and_select_fusion.idx_ref, bf16[6144,128]{1,0:T(8,128)(2,1)} %get-tuple-element.29.q_hbm, bf16[6144,128]{1,0:T(8,128)(2,1)} %get-tuple-element.30.k_hbm, bf16[6144,128]{1,0:T(8,128)(2,1)} %get-tuple-element.31.v_hbm, bf16[16,192,128]{2,1,0:T(8,128)(2,1)} %all_to_all.20.g_hbm), custom_call_target="tpu_custom_call" | custom-call | tf_op jit(solution)/shard_map/attend_back/pallas_call | solution.py:253
  362.7 17.6 %project_back.1 = (bf16[6144,1024]{1,0:T(8,128)(2,1)}, f32[1024,256]{1,0:T(8,128)}, f32[8,256]{1,0:T(8,128)}) custom-call(bf16[6144,1024]{1,0:T(8,128)(2,1)} %get-tuple-element.33.n_ref, bf16[6144,256]{1,0:T(8,128)(2,1)} %attend_back.1.d_ref, bf16[1024,256]{1,0:T(8,128)(2,1)} %bitcast.55), custom_call_target="tpu_custom_call" | custom-call | tf_op jit(solution)/shard_map/project_back/pallas_call | solution.py:472
  383.9 4.5 all-to-all-start.3
  388.4 86.8 %reduce-scatter.5.cloned.1.call-done = bf16[576,1024]{1,0:T(8,128)(2,1)} async-done(((bf16[9216,1024]{1,0:T(8,128)(2,1)}), bf16[576,1024]{1,0:T(8,128)(2,1)}) %reduce-scatter.5.cloned.1.call-update) | async-done | bytes 1179664 | tf_op jit(solution)/shard_map/reduce_scatter | solution.py:589
  475.2 1.5 collective-permute-start.2
  477.6 1.5 collective-permute-start.1
  479.7 24.6 %collective-permute-done = bf16[768]{0:T(1024)(128)(2,1)S(1)} collective-permute-done((bf16[768]{0:T(1024)(128)(2,1)S(1)}, bf16[768]{0:T(1024)(128)(2,1)S(1)}, u32[]{:S(2)}, u32[]{:S(2)}) %collective-permute-start) | collective-permute-done | bytes 1568 | tf_op jit(solution)/shard_map/ppermute | solution.py:511
  505.6 8.9 %collective-permute-done.1 = bf16[16,64,192]{2,1,0:T(8,128)(2,1)} collective-permute-done((bf16[16,64,192]{2,1,0:T(8,128)(2,1)S(1)}, bf16[16,64,192]{2,1,0:T(8,128)(2,1)}, u32[]{:S(2)}, u32[]{:S(2)}) %collective-permute-start.1) | collective-permute-done | bytes 393248 | tf_op jit(solution)/shard_map/ppermute | solution.py:511
  514.4 1.7 copy.128
  520.2 93.0 %reduce-scatter.3.cloned.1.call-done.gn_ref = bf16[384,1024]{1,0:T(8,128)(2,1)} async-done(((bf16[6144,1024]{1,0:T(8,128)(2,1)}), bf16[384,1024]{1,0:T(8,128)(2,1)}) %reduce-scatter.3.cloned.1.call-update) | async-done | bytes 786448 | tf_op jit(solution)/shard_map/reduce_scatter | solution.py:594
  613.1 3.8 last.1
  (144 shorter events, 23.9 us)
Async XLA Ops:
  7.2 117.5 %all-gather.5.cloned.1.call-start = ((), (), s32[]{:S(2)}) async-start(), calls=%async_computation.8 | async-start | bytes 13369344 | tf_op jit(solution)/shard_map/all_gather | solution.py:564
  7.9 3.5 copy-start.5
  7.9 228.2 %all-gather.7.cloned.1.call-start = ((), (), s32[]{:S(2)}) async-start(), calls=%async_computation.9 | async-start | bytes 20054016 | tf_op jit(solution)/shard_map/all_gather | solution.py:573
  9.1 2.6 copy-start.6
  9.1 2.9 copy-start.7
  11.4 1.0 copy-start.16
  12.0 9.3 %copy-start.19 = (bf16[64]{0:T(256)(128)(2,1)S(1)}, bf16[64]{0:T(256)(128)(2,1)}, u32[]{:S(2)}) copy-start(bf16[64]{0:T(256)(128)(2,1)} %param.28) | copy-start | bytes 388
  12.0 9.3 %copy-start.20 = (bf16[64]{0:T(256)(128)(2,1)S(1)}, bf16[64]{0:T(256)(128)(2,1)}, u32[]{:S(2)}) copy-start(bf16[64]{0:T(256)(128)(2,1)} %param.31) | copy-start | bytes 388
  12.0 9.3 %copy-start.11 = (s32[1,1,96,3]{2,1,3,0:T(1,128)S(1)}, s32[1,1,96,3]{2,1,3,0:T(1,128)}, u32[]{:S(2)}) copy-start(s32[1,1,96,3]{2,1,3,0:T(1,128)} %param.23) | copy-start | bytes 3460
  12.2 9.1 %copy-start.21 = (s32[1,2]{1,0:T(1,128)S(1)}, s32[1,2]{1,0:T(1,128)}, u32[]{:S(2)}) copy-start(s32[1,2]{1,0:T(1,128)} %param.24) | copy-start | bytes 28
  12.2 10.5 %copy-start.8 = (s32[1,6144]{1,0:T(1,128)S(1)}, s32[1,6144]{1,0:T(1,128)}, u32[]{:S(2)}) copy-start(s32[1,6144]{1,0:T(1,128)} %param.22) | copy-start | bytes 73732
  13.8 30.3 %all-to-all-start = ((bf16[16,64,256]{2,1,0:T(8,128)(2,1)}), bf16[16,64,256]{2,1,0:T(8,128)(2,1)S(1)}, u32[]{:S(2)}, u32[]{:S(2)}) async-start(bf16[16,64,256]{2,1,0:T(8,128)(2,1)} %pad_maximum_fusion.1), calls=%async_computation | async-start | bytes 1048576 | tf_op jit(solution)/shard_map/all_to_all | solution.py:503
  182.5 35.1 %all-to-all-start.1 = ((bf16[16,192,128]{2,1,0:T(8,128)(2,1)}), bf16[16,192,128]{2,1,0:T(8,128)(2,1)S(1)}, u32[]{:S(2)}, u32[]{:S(2)}) async-start(bf16[16,192,128]{2,1,0:T(8,128)(2,1)} %attend.1), calls=%async_computation.1 | async-start | bytes 1572864 | tf_op jit(solution)/shard_map/all_to_all | solution.py:503
  186.2 289.1 %reduce-scatter.5.cloned.1.call-start = ((), (), s32[]{:S(2)}) async-start(), calls=%async_computation.7 | async-start | bytes 20054016 | tf_op jit(solution)/shard_map/reduce_scatter | solution.py:589
  217.6 18.5 %copy-start.1 = (bf16[16,192,128]{2,1,0:T(8,128)(2,1)}, bf16[16,192,128]{2,1,0:T(8,128)(2,1)S(1)}, u32[]{:S(2)}) copy-start(bf16[16,192,128]{2,1,0:T(8,128)(2,1)S(1)} %all-to-all-done.1.att_ref) | copy-start | bytes 2359300
  272.0 1.1 copy-start.4
  272.0 341.2 %reduce-scatter.3.cloned.1.call-start = ((), (), s32[]{:S(2)}) async-start(), calls=%async_computation.6 | async-start | bytes 13369344 | tf_op jit(solution)/shard_map/reduce_scatter | solution.py:594
  380.3 1.2 copy-start.2
  380.3 1.4 copy-start
  383.9 92.8 %all-to-all-start.3 = ((bf16[16,64,256]{2,1,0:T(8,128)(2,1)}), bf16[16,64,256]{2,1,0:T(8,128)(2,1)S(1)}, u32[]{:S(2)}, u32[]{:S(2)}) async-start(bf16[16,64,256]{2,1,0:T(8,128)(2,1)} %pad_maximum_fusion.3), calls=%async_computation.4 | async-start | bytes 1048576 | tf_op jit(solution)/shard_map/all_to_all | solution.py:503
  475.2 141.7 %collective-permute-start.2 = (bf16[576,1024]{1,0:T(8,128)(2,1)}, bf16[576,1024]{1,0:T(8,128)(2,1)S(1)}, u32[]{:S(2)}, u32[]{:S(2)}) collective-permute-start(bf16[576,1024]{1,0:T(8,128)(2,1)} %reduce-scatter.5.cloned.1.call-done), channel_id=1, source_target_pairs={{0,16},{16,0},{1,17},{17,1},{2,18},{18,2},{3,19},{19,3},{4,20},{20... | collective-permute-start | bytes 3538952 | tf_op jit(solution)/shard_map/ppermute | solution.py:511
  477.0 27.3 %collective-permute-start = (bf16[768]{0:T(1024)(128)(2,1)S(1)}, bf16[768]{0:T(1024)(128)(2,1)S(1)}, u32[]{:S(2)}, u32[]{:S(2)}) collective-permute-start(bf16[768]{0:T(1024)(128)(2,1)S(1)} %pad_maximum_fusion.5), channel_id=1, source_target_pairs={{0,16},{16,0},{1,17},{17,1},{2,18},{18,2},{3,19},{19,3},{4,20},{20... | collective-permute-start | bytes 4616 | tf_op jit(solution)/shard_map/ppermute | solution.py:511
  477.6 36.8 %collective-permute-start.1 = (bf16[16,64,192]{2,1,0:T(8,128)(2,1)S(1)}, bf16[16,64,192]{2,1,0:T(8,128)(2,1)}, u32[]{:S(2)}, u32[]{:S(2)}) collective-permute-start(bf16[16,64,192]{2,1,0:T(8,128)(2,1)S(1)} %bitcast.62), channel_id=1, source_target_pairs={{0,16},{16,0},{1,17},{17,1},{2,18},{18,2},{3,19},{19,3},{4,20},{20... | collective-permute-start | bytes 1179656 | tf_op jit(solution)/shard_map/ppermute | solution.py:511
  519.3 97.7 %copy-start.3 = (bf16[576,1024]{1,0:T(8,128)(2,1)S(1)}, bf16[576,1024]{1,0:T(8,128)(2,1)}, u32[]{:S(2)}) copy-start(bf16[576,1024]{1,0:T(8,128)(2,1)} %reduce-scatter.5.cloned.1.call-done) | copy-start | bytes 3538948
  (8 other events, 7.5 us)
Sparse Core Ops, SparseCore 0:
  10.3 114.3 all-gather.4
  126.3 109.7 all-gather.6
  272.1 203.0 reduce-scatter.4
  479.1 133.9 reduce-scatter.2

commit v2 on v1

v2 whole, which is shorter than its diff:
```python
import functools
import math

import jax
import jax.numpy as jnp
from jax import lax
from jax.experimental import pallas as pl
from jax.experimental.pallas import tpu as pltpu
from jax.sharding import PartitionSpec as P

BLK = 64
DH = 64
SLOTS = 8
EPSILON = 1e-05
FAR = -1e20
BF = jnp.bfloat16
F32 = jnp.float32
VMEM_LIMIT = 56 * 1024 * 1024


def dot_nn(left, right):
    return lax.dot_general(left, right, (((1,), (0,)), ((), ())), preferred_element_type=F32)


def dot_tn(left, right):
    return lax.dot_general(left, right, (((0,), (0,)), ((), ())), preferred_element_type=F32)


def dot_nt(left, right):
    return lax.dot_general(left, right, (((1,), (1,)), ((), ())), preferred_element_type=F32)


def params(*semantics):
    return pltpu.CompilerParams(
        dimension_semantics=semantics if semantics else None, vmem_limit_bytes=VMEM_LIMIT
    )


def lanes_of(shape):
    return lax.broadcasted_iota(jnp.int32, shape, len(shape) - 1)


def normalize(values):
    centre = jnp.mean(values, axis=-1, keepdims=True)
    centred = values - centre
    spread = jnp.mean(centred * centred, axis=-1, keepdims=True)
    scale = lax.rsqrt(spread + EPSILON)
    return centred * scale, scale


def norm_backward(grad, normal, scale, gain):
    scaled = grad * gain
    mean_one = jnp.mean(scaled, axis=-1, keepdims=True)
    mean_two = jnp.mean(scaled * normal, axis=-1, keepdims=True)
    return scale * (scaled - mean_one - normal * mean_two)


def key_blocks(random_heads, global_ids):
    blocks_count = random_heads.shape[0]
    position = jnp.arange(blocks_count, dtype=jnp.int32)
    window = jnp.stack([position - 1, position, position + 1], axis=1)
    global_all = jnp.broadcast_to(global_ids[None, :], (blocks_count, global_ids.shape[0]))
    listed = jnp.concatenate([window, random_heads, global_all], axis=1)
    slot_count = listed.shape[1]
    earlier = jnp.arange(slot_count)[:, None] > jnp.arange(slot_count)[None, :]
    repeated = jnp.any((listed[..., :, None] == listed[..., None, :]) & earlier, axis=-1)
    usable = (listed >= 0) & (listed < blocks_count) & jnp.logical_not(repeated)
    return jnp.where(usable, listed, blocks_count)


def ring_of(mesh):
    chips = [devices[0] for devices in mesh.devices.reshape(-1, mesh.shape["shard"])[0].reshape(-1, 2)]
    count = len(chips)
    at = [getattr(chip, "coords", None) for chip in chips]
    if any(c is None for c in at):
        return tuple(range(count))
    near = lambda i, j: sum(abs(p - q) for p, q in zip(at[i], at[j])) == 1

    def grow(path):
        if len(path) == count:
            return path if near(path[-1], path[0]) else None
        for chip in range(count):
            if chip not in path and near(path[-1], chip):
                found = grow(path + [chip])
                if found:
                    return found
        return None

    return tuple(grow([0]) or range(count))


class Ring:
    def __init__(self, order):
        self.order = order
        self.count = len(order)
        self.far = self.count // 2
        self.stages = [[(0, 0), (0, 1)]]
        for k in range(1, self.far):
            self.stages.append([(k, 0), (self.count - k, 0), (k, 1), (self.count - k, 1)])
        self.stages.append([(self.far, 0), (self.far, 1)])
        self.pieces = [piece for stage in self.stages for piece in stage]

    def hop(self, table, by):
        pairs = [
            (2 * self.order[i] + core, 2 * self.order[(i + by) % self.count] + core)
            for i in range(self.count)
            for core in range(2)
        ]
        return lax.ppermute(table, "shard", pairs)

    def swap(self, table):
        return lax.ppermute(table, "shard", [(s, s ^ 1) for s in range(2 * self.count)])

    def sources(self):
        me = lax.axis_index("shard")
        order = jnp.array(self.order, jnp.int32)
        chip, core = me // 2, me % 2
        place = jnp.sum(jnp.where(order == chip, jnp.arange(self.count, dtype=jnp.int32), 0))
        ahead = jnp.array([k for k, _ in self.pieces], jnp.int32)
        other = jnp.array([e for _, e in self.pieces], jnp.int32)
        wanted = (place + ahead) % self.count
        found = jnp.sum(
            jnp.where(wanted[:, None] == jnp.arange(self.count, dtype=jnp.int32)[None], order[None], 0), axis=1
        )
        return 2 * found + jnp.bitwise_xor(core, other)

    def gather(self, table, use, ready):
        tie = lax.optimization_barrier
        half = table.shape[0] // 2
        used = []
        behind = ahead = table
        stages = [[table, self.swap(table)]]
        for k in range(1, self.far + 1):
            if k < self.far:
                ahead, behind = tie((self.hop(ahead, -1), self.hop(behind, 1)))
            else:
                ahead, behind = tie((self.hop(ahead[:half], -1), self.hop(behind[half:], 1)))
            if k == 2:
                ahead, behind, ready = tie((ahead, behind, ready))
            if k >= 2:
                used = used + [use(k - 2, stages[k - 2], ready)]
                ahead, behind, used = tie((ahead, behind, used))
            if k < self.far:
                stages.append([ahead, behind, self.swap(ahead), self.swap(behind)])
        both = jnp.concatenate([ahead, behind], axis=0)
        stages.append([both, self.swap(both)])
        return used + [use(i, stages[i], ready) for i in range(len(used), len(stages))], ahead

    def scatter_order(self):
        n, far = self.count, self.far
        return [far] + [k for near in range(far - 1, 0, -1) for k in (near, n - near)] + [0]

    def scatter_sum(self, own, other, release, finish):
        low = lambda t: t.astype(BF)
        n, far = self.count, self.far
        swapped = {k: self.swap(other[k]) for k in self.scatter_order()}
        own = {k: own[k].astype(F32) + swapped[k].astype(F32) for k in own}
        half = own[far].shape[0] // 2
        start = release(low(own[far]))
        up, down = self.hop(start[:half], 1), self.hop(start[half:], -1)
        blank = jnp.zeros(up.shape, F32)
        up = jnp.concatenate([up.astype(F32), blank], axis=0)
        down = jnp.concatenate([blank, down.astype(F32)], axis=0)
        for k in range(far - 1, 0, -1):
            up, down = low(own[k] + up), low(own[n - k] + down)
            if k == 1:
                up = finish(up)
            up, down = lax.optimization_barrier((up, down))
            up, down = self.hop(up, 1).astype(F32), self.hop(down, -1).astype(F32)
        return own[0] + up + down


def project_kernel(count, *refs):
    tokens, (seg_ref, w_ref, bias_ref, norm_ref), outs = refs[:count], refs[count : count + 4], refs[count + 4 :]
    n_ref, q_ref, k_ref, v_ref = outs
    for i, tok_ref in enumerate(tokens):
        length = tok_ref.shape[0]
        cut = slice(i * length, (i + 1) * length)
        normal, _ = normalize(tok_ref[...].astype(F32))
        normed = (normal * norm_ref[0:1, :] + norm_ref[1:2, :]).astype(BF)
        n_ref[cut] = normed
        out = dot_nn(normed, w_ref[...]) + bias_ref[0:1, :]
        out = out.astype(BF).astype(F32)
        both = out[:, :128]
        lane = lanes_of(both.shape)
        seg = jnp.broadcast_to(seg_ref[i : i + 1, :].astype(F32), (128, length)).T
        same = seg == (lane - DH).astype(F32)
        key_extra = jnp.where((lane < DH + 8) & ~same, FAR, 0.0)
        query = jnp.where(lane < DH, both * (1.0 / math.sqrt(DH)), jnp.where(same, 1.0, 0.0))
        q_ref[cut] = query.astype(BF)
        k_ref[cut] = jnp.where(lane < DH, pltpu.roll(both, DH, 1), key_extra).astype(BF)
        v_ref[cut] = out[:, 128:].astype(BF)


def project(pieces, segs, weight, bias, norm_rows):
    length, width = pieces[0].shape
    total = length * len(pieces)
    table = jax.ShapeDtypeStruct((total, 128), BF)
    return pl.pallas_call(
        functools.partial(project_kernel, len(pieces)),
        out_shape=[jax.ShapeDtypeStruct((total, width), BF), table, table, table],
        compiler_params=params(),
        name="project",
    )(*pieces, segs, weight, bias, norm_rows)


def load_tables(pairs, sem):
    copies = []
    for sources, dst in pairs:
        start = 0
        for src in sources:
            count = src.shape[0]
            place = sem.at[len(copies)]
            copies.append(pltpu.make_async_copy(src, dst.at[pl.ds(start, count)], place))
            start += count
    for copy in copies:
        copy.start()
    for copy in copies:
        copy.wait()


def fill_null(k_ref, v_ref, rows):
    lane = lanes_of((BLK, 128))
    k_ref[rows : rows + BLK, :] = jnp.where(
        (lane >= DH) & (lane < DH + 8), FAR, 0.0
    ).astype(BF)
    v_ref[rows : rows + BLK, :] = jnp.zeros((BLK, 128), BF)


def starts_of(idx_ref, place_ref, block):
    return [
        pl.multiple_of(place_ref[idx_ref[block * SLOTS + slot]] * BLK, BLK) for slot in range(SLOTS)
    ]


def gather_rows(starts, ref):
    return jnp.concatenate([ref[pl.ds(start, BLK), :] for start in starts], axis=0)


def softmax_rows(scores):
    top = jnp.max(scores, axis=1, keepdims=True)
    raised = jnp.exp(scores - top)
    return raised * (1.0 / jnp.sum(raised, axis=1, keepdims=True))


def attend_kernel(parts, idx_ref, src_ref, place_ref, *refs):
    tables, (o_ref, q_ref, k_ref, v_ref, sem) = refs[: 3 * parts], refs[3 * parts :]
    rows = q_ref.shape[0]
    load_tables(
        [(tables[i * parts : (i + 1) * parts], dst) for i, dst in enumerate((q_ref, k_ref, v_ref))],
        sem,
    )
    fill_null(k_ref, v_ref, rows)
    owners, half, _ = o_ref.shape
    per = half // BLK
    lane = lanes_of((BLK, 128))

    def one(piece, owner, part):
        starts = starts_of(idx_ref, place_ref, owner * (2 * per) + part)
        keys = gather_rows(starts, k_ref)
        query = q_ref[pl.ds(pl.multiple_of((piece * (2 * per) + part) * BLK, BLK), BLK), :]
        chances = softmax_rows(dot_nt(query, keys)).astype(BF)
        return dot_nn(chances, gather_rows(starts, v_ref))

    def step(piece, carry):
        owner = src_ref[piece]
        for part in range(per):
            low, high = one(piece, owner, part), one(piece, owner, part + per)
            o_ref[owner, part * BLK : (part + 1) * BLK, :] = jnp.where(lane < DH, low, high).astype(BF)
        return carry

    lax.fori_loop(0, owners, step, 0)


def attend(scalars, tables, owners):
    parts = len(tables[0])
    rows = sum(t.shape[0] for t in tables[0])
    anywhere = pl.BlockSpec(memory_space=pl.ANY)
    flat = [t for table in tables for t in table]
    return pl.pallas_call(
        functools.partial(attend_kernel, parts),
        in_specs=[pl.BlockSpec(memory_space=pltpu.SMEM)] * 3 + [anywhere] * len(flat),
        out_specs=pl.BlockSpec(memory_space=pltpu.VMEM),
        out_shape=jax.ShapeDtypeStruct((owners, rows // owners // 2, 128), BF),
        scratch_shapes=[
            pltpu.VMEM((rows, 128), BF),
            pltpu.VMEM((rows + BLK, 128), BF),
            pltpu.VMEM((rows + BLK, 128), BF),
            pltpu.SemaphoreType.DMA((len(flat),)),
        ],
        compiler_params=params(),
        name="attend",
    )(*scalars, *flat)


def attend_back_kernel(parts, idx_ref, src_ref, place_ref, *refs):
    tables, (d_ref, q_ref, k_ref, v_ref, g_ref, dk_ref, dv_ref, sem) = (
        refs[: 3 * parts + 1],
        refs[3 * parts + 1 :],
    )
    rows = q_ref.shape[0]
    load_tables(
        [(tables[i * parts : (i + 1) * parts], dst) for i, dst in enumerate((q_ref, k_ref, v_ref))]
        + [(tables[3 * parts :], g_ref)],
        sem,
    )
    fill_null(k_ref, v_ref, rows)
    dk_ref[...] = jnp.zeros_like(dk_ref)
    dv_ref[...] = jnp.zeros_like(dv_ref)
    owners, half, _ = g_ref.shape
    per = half // BLK
    lane = lanes_of((BLK, 128))

    def one(piece, owner, part, grad):
        starts = starts_of(idx_ref, place_ref, owner * (2 * per) + part)
        keys = gather_rows(starts, k_ref)
        values = gather_rows(starts, v_ref)
        at = pl.ds(pl.multiple_of((piece * (2 * per) + part) * BLK, BLK), BLK)
        query = q_ref[at, :]
        chances = softmax_rows(dot_nt(query, keys))
        grad_chances = dot_nt(grad, values)
        inner = jnp.sum(chances * grad_chances, axis=1, keepdims=True)
        grad_scores = (chances * (grad_chances - inner)).astype(BF)
        grad_query = dot_nn(grad_scores, keys) * (1.0 / math.sqrt(DH))
        d_ref[at, 0:128] = jnp.where(lane < DH, grad_query, 0.0).astype(BF)
        key_adds = dot_tn(grad_scores, query)
        value_adds = dot_tn(chances.astype(BF), grad)
        for slot, start in enumerate(starts):
            cut = slice(slot * BLK, (slot + 1) * BLK)
            dk_ref[pl.ds(start, BLK), :] += key_adds[cut]
            dv_ref[pl.ds(start, BLK), :] += value_adds[cut]

    def step(piece, carry):
        owner = src_ref[piece]
        for part in range(per):
            grad = g_ref[owner, part * BLK : (part + 1) * BLK, :]
            zero = jnp.zeros_like(grad)
            one(piece, owner, part, jnp.where(lane < DH, grad, zero))
            one(piece, owner, part + per, jnp.where(lane < DH, zero, grad))
        return carry

    lax.fori_loop(0, owners, step, 0)

    chunk = 512

    def finish(i, carry):
        at = pl.ds(pl.multiple_of(i * chunk, chunk), chunk)
        wide = lanes_of((chunk, 128))
        grad_keys = pltpu.roll(dk_ref[at, :], DH, 1)
        grad_query = d_ref[at, 0:128].astype(F32)
        d_ref[at, 0:128] = jnp.where(wide < DH, grad_query, grad_keys).astype(BF)
        grad_values = dv_ref[at, :]
        grad_values = grad_values + pltpu.roll(grad_values, DH, 1)
        d_ref[at, 128:256] = jnp.where(wide < DH, grad_values, 0.0).astype(BF)
        return carry

    lax.fori_loop(0, rows // chunk, finish, 0)


def attend_back(scalars, tables, grads):
    parts = len(tables[0])
    rows = sum(t.shape[0] for t in tables[0])
    anywhere = pl.BlockSpec(memory_space=pl.ANY)
    flat = [t for table in tables for t in table] + [grads]
    return pl.pallas_call(
        functools.partial(attend_back_kernel, parts),
        in_specs=[pl.BlockSpec(memory_space=pltpu.SMEM)] * 3 + [anywhere] * len(flat),
        out_specs=pl.BlockSpec(memory_space=pltpu.VMEM),
        out_shape=jax.ShapeDtypeStruct((rows, 256), BF),
        scratch_shapes=[
            pltpu.VMEM((rows, 128), BF),
            pltpu.VMEM((rows + BLK, 128), BF),
            pltpu.VMEM((rows + BLK, 128), BF),
            pltpu.VMEM(grads.shape, BF),
            pltpu.VMEM((rows + BLK, 128), F32),
            pltpu.VMEM((rows + BLK, 128), F32),
            pltpu.SemaphoreType.DMA((len(flat),)),
        ],
        compiler_params=params(),
        name="attend_back",
    )(*scalars, *flat)


def pack_heads(table_ref, flat):
    half = flat.shape[0] // 2
    lane = lanes_of((half, 128))
    for pair in range(table_ref.shape[0] // 2):
        cut = slice(pair * 128, (pair + 1) * 128)
        top, low = flat[:half, cut], flat[half:, cut]
        table_ref[2 * pair] = jnp.where(lane < DH, top, pltpu.roll(low, DH, 1)).astype(BF)
        table_ref[2 * pair + 1] = jnp.where(lane < DH, pltpu.roll(top, DH, 1), low).astype(BF)


def unpack_heads(flat_ref, table_ref):
    owners, half, _ = table_ref.shape
    lane = lanes_of((half, 128))
    for pair in range(owners // 2):
        one = table_ref[2 * pair].astype(F32)
        two = table_ref[2 * pair + 1].astype(F32)
        cut = slice(pair * 128, (pair + 1) * 128)
        flat_ref[0:half, cut] = jnp.where(lane < DH, one, pltpu.roll(two, DH, 1)).astype(BF)
        flat_ref[half : 2 * half, cut] = jnp.where(lane < DH, pltpu.roll(one, DH, 1), two).astype(BF)


def out_kernel(att_ref, tok_ref, w_ref, vec_ref, a_ref, mid_ref, n2_ref):
    width = tok_ref.shape[1]
    unpack_heads(a_ref, att_ref)
    mid = (
        tok_ref[...].astype(F32)
        + dot_nn(a_ref[...], w_ref[...].reshape(width, width))
        + vec_ref[0:1, :]
    )
    mid_ref[...] = mid
    normal, _ = normalize(mid)
    n2_ref[...] = (normal * vec_ref[1:2, :] + vec_ref[2:3, :]).astype(BF)


def whole(shape):
    return pl.BlockSpec(shape, lambda c: (0,) * len(shape))


def out_rows(weights):
    owners, rows, width = weights.shape
    own = width // owners
    return pl.BlockSpec((owners, own, width), lambda c: (0, rows // own - 1, 0))


def project_out(attended, tokens, weights, vectors):
    shape = tokens.shape
    return pl.pallas_call(
        out_kernel,
        grid=(1,),
        in_specs=[whole(attended.shape), whole(shape), out_rows(weights), whole(vectors.shape)],
        out_specs=[whole(shape)] * 3,
        out_shape=[
            jax.ShapeDtypeStruct(shape, BF),
            jax.ShapeDtypeStruct(shape, F32),
            jax.ShapeDtypeStruct(shape, BF),
        ],
        compiler_params=params("arbitrary"),
        name="project_out",
    )(attended, tokens, weights, vectors)


def feed_kernel(n2_ref, cot_ref, down_ref, up_ref, vec_ref, out_ref, gn_ref, hid_ref, pre_ref, gb_ref, acc_ref, acc_gn):
    chunk = pl.program_id(0)
    width = n2_ref.shape[1]
    w_up = up_ref[...].reshape(width, -1)
    w_down = down_ref[...].reshape(-1, width)
    pre = dot_nn(n2_ref[...], w_up) + vec_ref[pl.ds(4 + chunk, 1), :]
    root = math.sqrt(2.0 / math.pi)
    square = pre * pre
    bent = jnp.tanh(root * (pre + 0.044715 * (pre * square)))
    hidden = (0.5 * pre * (1.0 + bent)).astype(BF)
    slope = 0.5 * (1.0 + bent) + 0.5 * pre * (1.0 - bent * bent) * (
        root * (1.0 + (3 * 0.044715) * square)
    )
    grad_pre = (slope * dot_nt(cot_ref[...], w_down)).astype(BF)
    hid_ref[...] = hidden
    pre_ref[...] = grad_pre
    gb_ref[pl.ds(chunk, 1), :] = jnp.sum(grad_pre.astype(F32), axis=0, keepdims=True)
    more = dot_nn(hidden, w_down)
    grad_more = dot_nt(grad_pre, w_up)

    @pl.when(chunk == 0)
    def _():
        acc_ref[...] = more
        acc_gn[...] = grad_more

    @pl.when(chunk > 0)
    def _():
        out_ref[...] = (acc_ref[...] + more).astype(out_ref.dtype)
        gn_ref[...] = (acc_gn[...] + grad_more).astype(gn_ref.dtype)


def layout_of(weights):
    owners, rows, width = weights.shape
    own = width // owners
    units = (rows - own) // 2
    chunks = units // own
    return owners, own, width, units, chunks


def feed(normed, cotangent, weights, vectors, kind):
    owners, own, width, units, chunks = layout_of(weights)
    assert chunks == 2
    count = normed.shape[0]
    first_up = units // own
    column = pl.BlockSpec((count, width), lambda c: (0, c))
    wide = jax.ShapeDtypeStruct((count, chunks * width), BF)
    return pl.pallas_call(
        feed_kernel,
        grid=(chunks,),
        in_specs=[
            whole(normed.shape),
            whole(cotangent.shape),
            pl.BlockSpec((owners // chunks, units, width), lambda c: (c, 0, 0)),
            pl.BlockSpec((owners, own, width), lambda c: (0, first_up + c, 0)),
            whole(vectors.shape),
        ],
        out_specs=[whole((count, width))] * 2 + [column, column, whole((8, width))],
        out_shape=[
            jax.ShapeDtypeStruct((count, width), kind),
            jax.ShapeDtypeStruct((count, width), kind),
            wide,
            wide,
            jax.ShapeDtypeStruct((8, width), F32),
        ],
        scratch_shapes=[pltpu.VMEM((count, width), F32), pltpu.VMEM((count, width), F32)],
        compiler_params=params("arbitrary"),
        name="feed",
    )(normed, cotangent, weights, weights, vectors)


def feed_grads_kernel(na_ref, nb_ref, ca_ref, cb_ref, ha_ref, hb_ref, pa_ref, pb_ref, grads_hbm, gd_buf, gu_buf, sem):
    chunk = pl.program_id(0)
    down_block, down_rows = gd_buf.shape[1:3]
    up_rows = gu_buf.shape[2]
    down = dot_tn(ha_ref[...], ca_ref[...]) + dot_tn(hb_ref[...], cb_ref[...])
    gd_buf[chunk] = down.astype(BF).reshape(gd_buf.shape[1:])
    copy_down = lambda c: pltpu.make_async_copy(
        gd_buf.at[c],
        grads_hbm.at[pl.ds(c * down_block, down_block), pl.ds(0, down_rows)],
        sem.at[0, c],
    )
    copy_up = lambda c: pltpu.make_async_copy(
        gu_buf.at[c],
        grads_hbm.at[:, pl.ds(down_rows + c * up_rows, up_rows)],
        sem.at[1, c],
    )
    copy_down(chunk).start()
    up = dot_tn(na_ref[...], pa_ref[...]) + dot_tn(nb_ref[...], pb_ref[...])
    gu_buf[chunk] = up.astype(BF).reshape(gu_buf.shape[1:])
    copy_up(chunk).start()

    @pl.when(chunk == 1)
    def _():
        for c in range(2):
            copy_down(c).wait()
            copy_up(c).wait()


def feed_grads(own_part, other_part, weights):
    owners, own, width, units, chunks = layout_of(weights)
    count = own_part[0].shape[0]
    column = pl.BlockSpec((count, width), lambda c: (0, c))
    inputs = [t for both in zip(own_part, other_part) for t in both]
    return pl.pallas_call(
        feed_grads_kernel,
        grid=(chunks,),
        in_specs=[whole((count, width))] * 4 + [column] * 4,
        out_specs=pl.BlockSpec(memory_space=pl.ANY),
        out_shape=jax.ShapeDtypeStruct(weights.shape, BF),
        scratch_shapes=[
            pltpu.VMEM((chunks, owners // chunks, units, width), BF),
            pltpu.VMEM((chunks, owners, own, width), BF),
            pltpu.SemaphoreType.DMA((2, chunks)),
        ],
        compiler_params=params("arbitrary"),
        name="feed_grads",
    )(*inputs)


def out_back_kernel(
    mid_ref, gn_ref, other_ref, cot_ref, a_ref, w_ref, vec_ref, _, gm_ref, ga_ref, gv_ref, grads_hbm, buf, sem
):
    width = mid_ref.shape[1]
    rows = grads_hbm.shape[1]
    normal, scale = normalize(mid_ref[...])
    grad = gn_ref[...] + other_ref[...].astype(F32)
    cot = cot_ref[...].astype(F32)
    grad_mid = cot + norm_backward(grad, normal, scale, vec_ref[1:2, :])
    gm_ref[...] = grad_mid
    branch = grad_mid.astype(BF)
    pack_heads(ga_ref, dot_nt(branch, w_ref[...].reshape(width, width)))
    buf[...] = dot_tn(a_ref[...], branch).astype(BF).reshape(buf.shape)
    copy = pltpu.make_async_copy(buf, grads_hbm.at[:, pl.ds(rows - buf.shape[1], buf.shape[1])], sem)
    copy.start()
    gv_ref[...] = jnp.zeros_like(gv_ref)
    gv_ref[0:1, :] = jnp.sum(branch.astype(F32), axis=0, keepdims=True)
    gv_ref[1:2, :] = jnp.sum(grad * normal, axis=0, keepdims=True)
    gv_ref[2:3, :] = jnp.sum(grad, axis=0, keepdims=True)
    gv_ref[3:4, :] = jnp.sum(cot, axis=0, keepdims=True)
    copy.wait()


def project_out_back(mid, grad, other, cotangent, flat, weights, vectors, grads):
    owners, own, width, units, chunks = layout_of(weights)
    shape = mid.shape
    packed = (owners, shape[0] // 2, 128)
    anywhere = pl.BlockSpec(memory_space=pl.ANY)
    return pl.pallas_call(
        out_back_kernel,
        grid=(1,),
        in_specs=[whole(shape)] * 5 + [out_rows(weights), whole(vectors.shape), anywhere],
        out_specs=[whole(shape), whole(packed), whole((8, width)), anywhere],
        out_shape=[
            jax.ShapeDtypeStruct(shape, F32),
            jax.ShapeDtypeStruct(packed, BF),
            jax.ShapeDtypeStruct((8, width), F32),
            jax.ShapeDtypeStruct(grads.shape, BF),
        ],
        scratch_shapes=[pltpu.VMEM((owners, own, width), BF), pltpu.SemaphoreType.DMA],
        input_output_aliases={7: 3},
        compiler_params=params("arbitrary"),
        name="project_out_back",
    )(mid, grad, other, cotangent, flat, weights, vectors, grads)


def shares_kernel(starts, d_ref, w_ref, *outs):
    weight = w_ref[...]
    for start, out_ref in zip(starts, outs):
        out_ref[...] = dot_nt(d_ref[start : start + out_ref.shape[0], :], weight).astype(BF)


def head_shares(grad_table, weight, starts, count):
    width = weight.shape[0]
    return pl.pallas_call(
        functools.partial(shares_kernel, starts),
        out_shape=[jax.ShapeDtypeStruct((count, width), BF)] * len(starts),
        compiler_params=params(),
        name="head_shares",
    )(grad_table, weight)


def last_kernel(tok_ref, gn_ref, gm_ref, norm_ref, out_ref):
    normal, scale = normalize(tok_ref[...].astype(F32))
    grad = norm_backward(gn_ref[...], normal, scale, norm_ref[0:1, :])
    out_ref[...] = (gm_ref[...] + grad).astype(BF)


def last(tokens, grad_normed, grad_middle, norm_rows):
    return pl.pallas_call(
        last_kernel,
        out_shape=jax.ShapeDtypeStruct(tokens.shape, BF),
        compiler_params=params(),
        name="last",
    )(tokens, grad_normed, grad_middle, norm_rows)


def exchange(table):
    return lax.all_to_all(table, "shard", split_axis=0, concat_axis=0, tiled=True)


def trade(table):
    reps = lax.axis_size("rep")
    return lax.ppermute(table, "rep", [(r, r ^ 1) for r in range(reps)])


def over_alike(table):
    reps = lax.axis_size("rep")
    if reps == 2:
        return table
    groups = [list(range(first, reps, 2)) for first in range(2)]
    return lax.psum(table, "rep", axis_index_groups=groups)


def local(
    ring,
    tokens,
    cotangent,
    seg_ids,
    random_blocks,
    global_blocks,
    ln1_gain,
    ln1_bias,
    w_query,
    b_query,
    w_key,
    w_value,
    b_value,
    w_out,
    b_out,
    ln2_gain,
    ln2_bias,
    w_up,
    b_up,
    w_down,
    b_down,
):
    tokens, cotangent, seg_row = tokens[0], cotangent[0], seg_ids[0]
    count, width = tokens.shape
    owners = lax.axis_size("shard")
    own = width // owners
    hidden = w_up.shape[1]
    units = hidden // owners // 2
    half = lax.axis_index("rep") % 2

    tiles = jnp.concatenate(
        [w.reshape(own, owners, DH) for w in (w_query, w_key, w_value)], axis=2
    ).transpose(1, 0, 2)
    small = jnp.concatenate([b_out, ln2_gain, ln2_bias, b_down, ln1_gain, ln1_bias, b_up])
    small = jnp.pad(small, (0, own * DH - small.shape[0])).reshape(1, own, DH)
    sent = jnp.concatenate([tiles, jnp.broadcast_to(small, (owners, own, DH))], axis=2)
    got = exchange(sent)
    weight = jnp.concatenate([got[:, :, : 3 * DH], got[:, :, 2 * DH : 3 * DH]], axis=2)
    weight = weight.reshape(width, 4 * DH)
    rows = got[:, :, 3 * DH :].reshape(owners, own * DH)[:, : 6 * own + hidden // owners]
    rows = rows.astype(F32)
    fixed = rows[:, : 6 * own].reshape(owners, 6, own).transpose(1, 0, 2).reshape(6, width)
    up_bias = lax.dynamic_slice_in_dim(rows[:, 6 * own :], half * units, units, axis=1)
    vectors = jnp.concatenate([fixed[:4], up_bias.reshape(2, width), jnp.zeros((2, width), F32)], axis=0)
    norm_rows = jnp.pad(fixed[4:6], ((0, 6), (0, 0)))
    zero = jnp.zeros((DH,), F32)
    bias = jnp.concatenate([b_query.astype(F32), zero, b_value.astype(F32), b_value.astype(F32)])
    bias = jnp.broadcast_to(bias[None], (8, 4 * DH))

    up_half = lax.dynamic_index_in_dim(w_up.reshape(own, owners, 2, units), half, 2, keepdims=False)
    mine = jnp.concatenate(
        [
            lax.dynamic_slice_in_dim(w_down, half * units, units, axis=0),
            up_half.reshape(own, 2, width).transpose(1, 0, 2).reshape(2 * own, width),
            w_out,
        ],
        axis=0,
    )
    other_cotangent = trade(cotangent)

    per = count // BLK
    sources = ring.sources()
    idx = key_blocks(random_blocks[0, 0], global_blocks[0])
    position = jnp.arange(owners, dtype=jnp.int32)
    piece_of = jnp.sum(jnp.where(sources[None] == position[:, None], position[None], 0), axis=1)
    place = piece_of[:, None] * per + jnp.arange(per, dtype=jnp.int32)[None]
    place = jnp.concatenate([place.reshape(-1), jnp.full((1,), owners * per, jnp.int32)])
    scalars = (idx.reshape(-1), sources, place)
    segs = seg_row.reshape(owners, count)[sources]

    def use(stage, pieces, ready):
        first = sum(len(earlier) for earlier in ring.stages[:stage])
        segs_here = jnp.pad(segs[first : first + len(pieces)], ((0, 8 - len(pieces)), (0, 0)))
        return project(pieces, segs_here, *ready)

    projected, late = ring.gather(tokens, use, (weight, bias, norm_rows))
    mine, _ = lax.optimization_barrier((mine, late))
    weights = lax.all_gather(mine, "shard", axis=0)
    projected, other_cotangent = lax.optimization_barrier((projected, other_cotangent))
    tables = [[stage[i] for stage in projected] for i in (1, 2, 3)]
    attended = exchange(attend(scalars, tables, owners))
    flat, mid, normed_two = project_out(attended, tokens, weights, vectors)
    other_normed = trade(normed_two)
    more, grad_two, hid, grad_pre, bias_one = feed(normed_two, cotangent, weights, vectors, F32)
    other_normed, grad_two = lax.optimization_barrier((other_normed, grad_two))
    other_more, other_grad, other_hid, other_pre, bias_two = feed(
        other_normed, other_cotangent, weights, vectors, BF
    )
    other_grad = trade(other_grad)
    other_more = trade(other_more)
    grads = feed_grads(
        (normed_two, cotangent, hid, grad_pre),
        (other_normed, other_cotangent, other_hid, other_pre),
        weights,
    )
    grad_middle, grad_attended, grad_rows, grads = project_out_back(
        mid, grad_two, other_grad, cotangent, flat, weights, vectors, grads
    )
    layer_out = (mid + more + other_more.astype(F32) + fixed[3][None]).astype(BF)
    shares = lax.psum_scatter(
        grads.reshape(-1, width), "shard", scatter_dimension=0, tiled=True
    )
    grad_table = attend_back(scalars, tables, exchange(grad_attended))
    at = {piece: i * count for i, piece in enumerate(ring.pieces)}
    order = ring.scatter_order()
    other_shares = head_shares(grad_table, weight, [at[k, 1] for k in order], count)
    table_later, _ = lax.optimization_barrier((grad_table, other_shares))
    own_shares = head_shares(table_later, weight, [at[k, 0] for k in order], count)
    results = []

    def release(first):
        first, table = lax.optimization_barrier((first, grad_table))
        results.append(weight_grads(table))
        return first

    def weight_grads(table):
        grad_weight, done = 0.0, 0
        for stage in projected:
            normed = stage[0]
            grad_weight = grad_weight + dot_tn(normed, table[done : done + normed.shape[0]])
            done += normed.shape[0]
        return finish_weights(grad_weight, jnp.sum(table.astype(F32), axis=0, keepdims=True))

    def finish(rows):
        tied = lax.optimization_barrier((rows, results[0]))
        results[0] = tied[1]
        return tied[0]

    def finish_weights(grad_weight, grad_bias):
        used = weight.astype(F32)[:, : 3 * DH]
        sums = grad_bias[0:1, : 3 * DH]
        spread = grad_weight[:, : 3 * DH] - fixed[5][:, None] * sums
        grad_gain = jnp.sum(used * spread, axis=1) / fixed[4]
        grad_shift = jnp.sum(used * sums, axis=1)
        lines = jnp.concatenate([grad_rows[:4], grad_gain[None], grad_shift[None]], axis=0)
        lines = lines.reshape(6, owners, own).transpose(1, 0, 2).reshape(owners, 6 * own)
        up_lines = (bias_one[:2] + bias_two[:2]).reshape(owners, units)
        lines = jnp.concatenate([lines, up_lines], axis=1)
        length = lines.shape[1]
        lines = jnp.pad(lines, ((0, 0), (0, own * DH - length))).reshape(owners, own, DH)
        back = jnp.concatenate(
            [grad_weight[:, : 3 * DH].reshape(owners, own, 3 * DH), lines], axis=2
        ).astype(BF)
        back = exchange(back)
        back_sum = jnp.sum(back[:, :, 3 * DH :].astype(F32), axis=0).reshape(own * DH)[:length]
        heads = over_alike(back[:, :, : 3 * DH])
        heads = heads.astype(F32) + trade(heads).astype(F32)
        heads = heads.transpose(1, 2, 0).reshape(own, 3, DH, owners).transpose(1, 0, 3, 2)
        heads = heads.reshape(3, own, width)
        tail = jnp.concatenate([back_sum, grad_bias[0, :DH], grad_bias[0, 2 * DH : 3 * DH]])
        tail = over_alike(tail.astype(BF))
        tail_other = trade(tail).astype(F32)
        tail = tail.astype(F32)
        total = tail + tail_other
        piece = lambda i: total[i * own : (i + 1) * own]

        def in_order(here, there, axis):
            both = [jnp.where(half == 0, here, there), jnp.where(half == 0, there, here)]
            return jnp.stack(both, axis=axis)

        grad_up_bias = in_order(tail[6 * own : length], tail_other[6 * own : length], 0).reshape(-1)
        ours = over_alike(shares)
        theirs = trade(ours)
        ours, theirs = ours.astype(F32), theirs.astype(F32)
        grad_down = in_order(ours[:units], theirs[:units], 0).reshape(2 * units, width)
        up_of = lambda t: t[units : 2 * units].reshape(2, own, width).transpose(1, 0, 2).reshape(
            own, owners, units
        )
        grad_up = in_order(up_of(ours), up_of(theirs), 2).reshape(own, hidden)
        grad_out = ours[2 * units :] + theirs[2 * units :]
        return (
            piece(4),
            piece(5),
            heads[0],
            total[length : length + DH],
            heads[1],
            heads[2],
            total[length + DH :],
            grad_out,
            piece(0),
            piece(1),
            piece(2),
            grad_up,
            grad_up_bias,
            grad_down,
            piece(3),
        )

    grad_normed = ring.scatter_sum(
        dict(zip(order, own_shares)), dict(zip(order, other_shares)), release, finish
    )
    grad_tokens = last(tokens, grad_normed, grad_middle, norm_rows)
    return (layer_out[None], grad_tokens[None], *results[0])


def solution(mesh):
    rows = P("rep", "shard", None)
    one, two = P("shard"), P("shard", None)
    return jax.shard_map(
        functools.partial(local, Ring(ring_of(mesh))),
        mesh=mesh,
        in_specs=(
            rows, rows, P("rep", None), P("rep", "shard", None, None), P("rep", None),
            one, one, two, one, two, two, one, two, one, one, one, two, one, two, one,
        ),
        out_specs=(
            rows, rows, one, one, two, one, two, two, one, two, one, one, one, two, one, two, one,
        ),
        check_vma=False,
    )
```

time: 628 us -> 520 us (0.83); the launches traced: 627 us -> 512 us
  waiting for transfers between devices: 356 us -> 133 us
  starting transfers between devices: 19.4 us -> 52.2 us
  other arithmetic: 15.5 us -> 43.4 us
  local copies, waits for them, and re-layouts: 17.8 us -> 44.5 us
  Pallas kernels: 176 us -> 196 us
    reduce_scatter x1 -> x0, waiting for transfers between devices: 93 us -> none  [local(): lax.psum_scatter(part, 'shard', scatter_dimension=0, tiled=True)]
    reduce_scatter x1, waiting for transfers between devices: 86.8 us -> 0.02 us  [local(): lax.psum_scatter(grads.reshape(-1, width), 'shard', scatter_dimension=0,...]
    all_gather x1 -> x0, waiting for transfers between devices: 78.4 us -> none  [local(): everyone = lax.all_gather(tokens, 'shard', axis=0, tiled=True)]
    ppermute x3 -> x39, waiting for transfers between devices: 33.5 us -> 85.2 us  [the longest x16 73.2 us: hop(): return lax.ppermute(table, 'shard', pairs)]
    ppermute x3 -> x39, starting transfers between devices: 3.5 us -> 37 us  [the longest x16 23.1 us: hop(): return lax.ppermute(table, 'shard', pairs)]
    pallas_call x5 -> x14, Pallas kernels: 172 us -> 191 us  [the longest x1 61.4 us: attend_back(): pl.pallas_call(functools.partial(attend_back_kernel, parts), in_specs=[pl...]
    convert_element_type x2 -> x11, other arithmetic: 7.05 us -> 17.2 us  [the longest x7 15.7 us: scatter_sum(): low = lambda t: t.astype(BF)]
    unnamed x46 -> x92, local copies, waits for them, and re-layouts: 2.81 us -> 12.1 us
  transfers between devices with their start and end apart: 10 -> 44, of which waited for: 8 -> 19; matrix products, arithmetic and copies ran while one was open for 4% -> 15% of each run, Pallas kernels for 22% -> 32%
where the time goes in v2:
time: 520 us; the launch traced here: 512 us
  Pallas kernels  196 us (38%)
  waiting for transfers between devices  133 us (26%)
  starting transfers between devices  52.2 us (10%)
  local copies, waits for them, and re-layouts  44.5 us (9%)
  other arithmetic  43.4 us (8%)
  blocking collectives  23.8 us (5%)
  between operations  15.4 us (3%)
    ppermute x16, waiting for transfers between devices, hop(): return lax.ppermute(table, 'shard', pairs)  73.2 us
    pallas_call x1, Pallas kernels, attend_back(): pl.pallas_call(functools.partial(attend_back_kernel, parts), in_specs=[pl...  61.4 us
    pallas_call x1, Pallas kernels, attend(): pl.pallas_call(functools.partial(attend_kernel, parts), in_specs=[pl.Bloc...  38.4 us
    all_to_all x3, waiting for transfers between devices, exchange(): lax.all_to_all(table, 'shard', split_axis=0, concat_axis=0, tiled=True)  37.4 us
    pallas_call x5, Pallas kernels, project(): pl.pallas_call(functools.partial(project_kernel, len(pieces)), out_shape=...  28.5 us
    pallas_call x2, Pallas kernels, feed(): pl.pallas_call(feed_kernel, grid=(chunks,), in_specs=[whole(normed.shape)...  25.3 us
    all_to_all x1, blocking collectives, exchange(): lax.all_to_all(table, 'shard', split_axis=0, concat_axis=0, tiled=True)  23.8 us
    ppermute x16, starting transfers between devices, hop(): return lax.ppermute(table, 'shard', pairs)  23.1 us
  transfers between devices with their start and end apart: 44, of which 19 were waited for; matrix products, arithmetic and copies ran while one was open for 15% of the time, Pallas kernels for 32%

profile of v2, /device:TPU:0, one launch (start us, length us, event | category | flops | bytes accessed | tf_op | source)
XLA Modules:
  0.0 512.3 jit_solution(8056282263748850097)
XLA Ops:
  10.5 4.7 concatenate.67
  19.3 6.3 %all-to-all-start = ((bf16[16,64,256]{2,1,0:T(8,128)(2,1)}), bf16[16,64,256]{2,1,0:T(8,128)(2,1)S(1)}, u32[]{:S(2)}, u32[]{:S(2)}) async-start(bf16[16,64,256]{2,1,0:T(8,128)(2,1)} %pad_maximum_fusion.3), calls=%async_computation | async-start | bytes 1048576 | tf_op jit(solution)/shard_map/all_to_all | solution.py:642
  34.5 7.9 %all-to-all-done = bf16[16,64,256]{2,1,0:T(8,128)(2,1)S(1)} async-done(((bf16[16,64,256]{2,1,0:T(8,128)(2,1)}), bf16[16,64,256]{2,1,0:T(8,128)(2,1)S(1)}, u32[]{:S(2)}, u32[]{:S(2)}) %all-to-all-start) | async-done | bytes 524320 | tf_op jit(solution)/shard_map/all_to_all | solution.py:642
  44.7 8.8 %collective-permute-done.2.refs_0_ = bf16[384,1024]{1,0:T(8,128)(2,1)} collective-permute-done((bf16[384,1024]{1,0:T(8,128)(2,1)}, bf16[384,1024]{1,0:T(8,128)(2,1)}, u32[]{:S(2)}, u32[]{:S(2)}) %collective-permute-start.2) | collective-permute-done | bytes 786464 | tf_op jit(solution)/shard_map/ppermute | solution.py:109
  65.4 6.6 %project.6 = (bf16[1536,1024]{1,0:T(8,128)(2,1)}, bf16[1536,128]{1,0:T(8,128)(2,1)}, bf16[1536,128]{1,0:T(8,128)(2,1)}, bf16[1536,128]{1,0:T(8,128)(2,1)}) custom-call(bf16[384,1024]{1,0:T(8,128)(2,1)} %collective-permute-done.refs_0_, bf16[384,1024]{1,0:T(8,128)(2,1)} %copy-done.18, bf16[384,1024]{1,0:T(8,128)(2,1)} %collective-permute-done.7.refs_2_, ...), custom_call_target="tpu_custom_call" | custom-call | tf_op jit(solution)/shard_map/project/pallas_call | solution.py:199
  72.0 9.4 %collective-permute-done.5.refs_0_ = bf16[384,1024]{1,0:T(8,128)(2,1)} collective-permute-done((bf16[384,1024]{1,0:T(8,128)(2,1)}, bf16[384,1024]{1,0:T(8,128)(2,1)}, u32[]{:S(2)}, u32[]{:S(2)}) %collective-permute-start.5) | collective-permute-done | bytes 786464 | tf_op jit(solution)/shard_map/ppermute | solution.py:109
  93.8 6.6 %project.7 = (bf16[1536,1024]{1,0:T(8,128)(2,1)}, bf16[1536,128]{1,0:T(8,128)(2,1)}, bf16[1536,128]{1,0:T(8,128)(2,1)}, bf16[1536,128]{1,0:T(8,128)(2,1)}) custom-call(bf16[384,1024]{1,0:T(8,128)(2,1)} %collective-permute-done.2.refs_0_, bf16[384,1024]{1,0:T(8,128)(2,1)} %collective-permute-done.3.refs_1_, bf16[384,1024]{1,0:T(8,128)(2,1)} %copy-done.21, ...), custom_call_target="tpu_custom_call" | custom-call | tf_op jit(solution)/shard_map/project/pallas_call | solution.py:199
  107.2 7.0 %project.8 = (bf16[1536,1024]{1,0:T(8,128)(2,1)}, bf16[1536,128]{1,0:T(8,128)(2,1)}, bf16[1536,128]{1,0:T(8,128)(2,1)}, bf16[1536,128]{1,0:T(8,128)(2,1)}) custom-call(bf16[384,1024]{1,0:T(8,128)(2,1)} %collective-permute-done.5.refs_0_, bf16[384,1024]{1,0:T(8,128)(2,1)} %collective-permute-done.6.refs_1_, ...), custom_call_target="tpu_custom_call" | custom-call | tf_op jit(solution)/shard_map/project/pallas_call | solution.py:199
  118.3 38.4 %attend.1 = bf16[16,192,128]{2,1,0:T(8,128)(2,1)} custom-call(s32[768]{0:T(1024)} %and_select_fusion.idx_ref, s32[16]{0:T(128)} %copy-done.30, s32[97]{0:T(128)} %pad_add_fusion.place_ref, bf16[768,128]{1,0:T(8,128)(2,1)} %get-tuple-element.225.refs_0_, bf16[1536,128]{1,0:T(8,128)(2,1)} %get-tuple-element.226.refs_1_, ...), custom_call_target="tpu_custom_call" | custom-call | tf_op jit(solution)/shard_map/attend/pallas_call | solution.py:280
  156.8 4.6 all-to-all-start.1
  162.8 29.5 %all-to-all-done.1.att_ref = bf16[16,192,128]{2,1,0:T(8,128)(2,1)S(1)} async-done(((bf16[16,192,128]{2,1,0:T(8,128)(2,1)}), bf16[16,192,128]{2,1,0:T(8,128)(2,1)S(1)}, u32[]{:S(2)}, u32[]{:S(2)}) %all-to-all-start.1) | async-done | bytes 786464 | tf_op jit(solution)/shard_map/all_to_all | solution.py:642
  192.3 10.5 %all-gather.3.cloned.1.call-done = bf16[5120,1024]{1,0:T(8,128)(2,1)} async-done(((bf16[320,1024]{1,0:T(8,128)(2,1)}), bf16[5120,1024]{1,0:T(8,128)(2,1)}) %all-gather.3.cloned.1.call-update) | async-done | bytes 10485776 | tf_op jit(solution)/shard_map/all_gather | solution.py:736
  208.8 12.9 %feed.2 = (f32[384,1024]{1,0:T(8,128)}, f32[384,1024]{1,0:T(8,128)}, bf16[384,2048]{1,0:T(8,128)(2,1)}, bf16[384,2048]{1,0:T(8,128)(2,1)}, f32[8,1024]{1,0:T(8,128)}) custom-call(bf16[384,1024]{1,0:T(8,128)(2,1)} %get-tuple-element.242.n2_ref.na_ref, bf16[384,1024]{1,0:T(8,128)(2,1)} %bitcast.77, bf16[16,320,1024]{2,1,0:T(8,128)(2,1)} %bitcast.63, ...), custom_call_target="tpu_custom_call" | custom-call | tf_op jit(solution)/shard_map/feed/pallas_call | solution.py:491
  221.7 5.5 %collective-permute-done.17.n2_ref.nb_ref = bf16[384,1024]{1,0:T(8,128)(2,1)S(1)} collective-permute-done((bf16[384,1024]{1,0:T(8,128)(2,1)}, bf16[384,1024]{1,0:T(8,128)(2,1)S(1)}, u32[]{:S(2)}, u32[]{:S(2)}) %collective-permute-start.17) | collective-permute-done | bytes 786464 | tf_op jit(solution)/shard_map/ppermute | solution.py:647
  228.1 12.4 %feed.3 = (bf16[384,1024]{1,0:T(8,128)(2,1)}, bf16[384,1024]{1,0:T(8,128)(2,1)}, bf16[384,2048]{1,0:T(8,128)(2,1)}, bf16[384,2048]{1,0:T(8,128)(2,1)}, f32[8,1024]{1,0:T(8,128)}) custom-call(bf16[384,1024]{1,0:T(8,128)(2,1)} %copy-done.8, bf16[384,1024]{1,0:T(8,128)(2,1)} %copy-done.7, bf16[16,320,1024]{2,1,0:T(8,128)(2,1)} %bitcast.65, ...), custom_call_target="tpu_custom_call" | custom-call | tf_op jit(solution)/shard_map/feed/pallas_call | solution.py:491
  242.0 13.7 %feed_grads.1._ = bf16[16,320,1024]{2,1,0:T(8,128)(2,1)} custom-call(bf16[384,1024]{1,0:T(8,128)(2,1)} %get-tuple-element.242.n2_ref.na_ref, bf16[384,1024]{1,0:T(8,128)(2,1)} %copy-done.8, bf16[384,1024]{1,0:T(8,128)(2,1)} %bitcast.78, bf16[384,1024]{1,0:T(8,128)(2,1)} %copy-done.7, bf16[384,2048]{1,0:T(8,128)(2,1)} %get-tuple-element.251.ha_ref, ...), custom_call_target="tpu_custom_call" | custom-call | tf_op jit(solution)/shard_map/feed_grads/pallas_call | solution.py:548
  260.5 9.3 %project_out_back.1 = (f32[384,1024]{1,0:T(8,128)}, bf16[16,192,128]{2,1,0:T(8,128)(2,1)}, f32[8,1024]{1,0:T(8,128)}, bf16[16,320,1024]{2,1,0:T(8,128)(2,1)}) custom-call(f32[384,1024]{1,0:T(8,128)} %get-tuple-element.241.mid_ref, f32[384,1024]{1,0:T(8,128)} %get-tuple-element.248.gn_ref, ...), custom_call_target="tpu_custom_call", output_to_operand_aliasing={{3}: (7, {})} | custom-call | tf_op jit(solution)/shard_map/project_out_back/pallas_call | solution.py:592
  270.9 23.8 %all_to_all.20.refs_15_ = bf16[16,192,128]{2,1,0:T(8,128)(2,1)} all-to-all(bf16[16,192,128]{2,1,0:T(8,128)(2,1)S(1)} %copy-done.15), channel_id=1, replica_groups=mesh['rep'=2,'shard'=16] {'shard'}, dimensions={0} | all-to-all | bytes 1572864 | tf_op jit(solution)/shard_map/all_to_all | solution.py:642
  294.7 61.4 %attend_back.1.d_ref = bf16[6144,256]{1,0:T(8,128)(2,1)} custom-call(s32[768]{0:T(1024)} %and_select_fusion.idx_ref, s32[16]{0:T(128)} %copy-done.30, s32[97]{0:T(128)} %pad_add_fusion.place_ref, bf16[768,128]{1,0:T(8,128)(2,1)} %get-tuple-element.225.refs_0_, bf16[1536,128]{1,0:T(8,128)(2,1)} %get-tuple-element.226.refs_1_, ...), custom_call_target="tpu_custom_call" | custom-call | tf_op jit(solution)/shard_map/attend_back/pallas_call | solution.py:365
  356.1 5.2 %head_shares.2 = (bf16[384,1024]{1,0:T(8,128)(2,1)}, bf16[384,1024]{1,0:T(8,128)(2,1)}, bf16[384,1024]{1,0:T(8,128)(2,1)}, bf16[384,1024]{1,0:T(8,128)(2,1)}, bf...) custom-call(bf16[6144,256]{1,0:T(8,128)(2,1)} %attend_back.1.d_ref, ...), custom_call_target="tpu_custom_call" | custom-call | tf_op jit(solution)/shard_map/head_shares/pallas_call | solution.py:618
  364.5 5.2 %head_shares.3 = (bf16[384,1024]{1,0:T(8,128)(2,1)}, bf16[384,1024]{1,0:T(8,128)(2,1)}, bf16[384,1024]{1,0:T(8,128)(2,1)}, bf16[384,1024]{1,0:T(8,128)(2,1)}, bf...) custom-call(bf16[6144,256]{1,0:T(8,128)(2,1)} %attend_back.1.d_ref, ...), custom_call_target="tpu_custom_call" | custom-call | tf_op jit(solution)/shard_map/head_shares/pallas_call | solution.py:618
  390.1 15.5 %collective-permute-done.27 = bf16[192,1024]{1,0:T(8,128)(2,1)S(1)} collective-permute-done((bf16[192,1024]{1,0:T(8,128)(2,1)S(1)}, bf16[192,1024]{1,0:T(8,128)(2,1)S(1)}, u32[]{:S(2)}, u32[]{:S(2)}) %collective-permute-start.27) | collective-permute-done | bytes 393248 | tf_op jit(solution)/shard_map/ppermute | solution.py:109
  418.2 13.0 %collective-permute-done.28 = bf16[384,1024]{1,0:T(8,128)(2,1)} collective-permute-done((bf16[384,1024]{1,0:T(8,128)(2,1)}, bf16[384,1024]{1,0:T(8,128)(2,1)}, u32[]{:S(2)}, u32[]{:S(2)}) %collective-permute-start.28) | collective-permute-done | bytes 786464 | tf_op jit(solution)/shard_map/ppermute | solution.py:109
  482.5 14.0 %collective-permute-done.37 = bf16[384,1024]{1,0:T(8,128)(2,1)S(1)} collective-permute-done((bf16[384,1024]{1,0:T(8,128)(2,1)}, bf16[384,1024]{1,0:T(8,128)(2,1)S(1)}, u32[]{:S(2)}, u32[]{:S(2)}) %collective-permute-start.37) | collective-permute-done | bytes 786464 | tf_op jit(solution)/shard_map/ppermute | solution.py:109
  (316 shorter events, 164.7 us)
Async XLA Ops:
  7.2 47.5 %collective-permute-start.4 = (bf16[384,1024]{1,0:T(8,128)(2,1)}, bf16[384,1024]{1,0:T(8,128)(2,1)S(1)}, u32[]{:S(2)}, u32[]{:S(2)}) collective-permute-start(bf16[384,1024]{1,0:T(8,128)(2,1)} %bitcast.81), channel_id=1, source_target_pairs={{0,1},{1,0},{2,3},{3,2},{4,5},{5,4},{6,7},{7,6},{8,9},{9,8},{10,11... | collective-permute-start | bytes 2359304 | tf_op jit(solution)/shard_map/ppermute | solution.py:112
  7.8 21.4 %collective-permute-start.1 = (bf16[384,1024]{1,0:T(8,128)(2,1)}, bf16[384,1024]{1,0:T(8,128)(2,1)S(1)}, u32[]{:S(2)}, u32[]{:S(2)}) collective-permute-start(bf16[384,1024]{1,0:T(8,128)(2,1)} %bitcast.82), channel_id=1, source_target_pairs={{0,2},{1,3},{2,6},{3,7},{6,10},{7,11},{10,14},{11,15},{14,12},{15,... | collective-permute-start | bytes 2359304 | tf_op jit(solution)/shard_map/ppermute | solution.py:109
  10.3 21.0 %collective-permute-start = (bf16[384,1024]{1,0:T(8,128)(2,1)}, bf16[384,1024]{1,0:T(8,128)(2,1)}, u32[]{:S(2)}, u32[]{:S(2)}) collective-permute-start(bf16[384,1024]{1,0:T(8,128)(2,1)} %bitcast.83), channel_id=1, source_target_pairs={{0,4},{1,5},{2,0},{3,1},{6,2},{7,3},{10,6},{11,7},{14,10},{15,11},... | collective-permute-start | bytes 2359304 | tf_op jit(solution)/shard_map/ppermute | solution.py:109
  19.3 23.1 %all-to-all-start = ((bf16[16,64,256]{2,1,0:T(8,128)(2,1)}), bf16[16,64,256]{2,1,0:T(8,128)(2,1)S(1)}, u32[]{:S(2)}, u32[]{:S(2)}) async-start(bf16[16,64,256]{2,1,0:T(8,128)(2,1)} %pad_maximum_fusion.3), calls=%async_computation | async-start | bytes 1048576 | tf_op jit(solution)/shard_map/all_to_all | solution.py:642
  25.7 177.0 %all-gather.3.cloned.1.call-start = ((), (), s32[]{:S(2)}) async-start(), calls=%async_computation.6 | async-start | bytes 11141120 | tf_op jit(solution)/shard_map/all_gather | solution.py:736
  31.3 22.1 %collective-permute-start.2 = (bf16[384,1024]{1,0:T(8,128)(2,1)}, bf16[384,1024]{1,0:T(8,128)(2,1)}, u32[]{:S(2)}, u32[]{:S(2)}) collective-permute-start(bf16[384,1024]{1,0:T(8,128)(2,1)} %collective-permute-done.refs_0_), channel_id=1, source_target_pairs={{0,4},{1,5},{2,0},{3,1},{6,2},{7,3},{10,6},{11,7},{14,10},{15,11},... | collective-permute-start | bytes 2359304 | tf_op jit(solution)/shard_map/ppermute | solution.py:109
  31.3 22.8 %collective-permute-start.3 = (bf16[384,1024]{1,0:T(8,128)(2,1)S(1)}, bf16[384,1024]{1,0:T(8,128)(2,1)}, u32[]{:S(2)}, u32[]{:S(2)}) collective-permute-start(bf16[384,1024]{1,0:T(8,128)(2,1)S(1)} %collective-permute-done.1.refs_1_), channel_id=1, source_target_pairs={{0,2},{1,3},{2,6},{3,7},{6,10},{7,11},{10,14},{11,15},{14,12},{15,... | collective-permute-start | bytes 2359304 | tf_op jit(solution)/shard_map/ppermute | solution.py:109
  34.0 30.3 %collective-permute-start.7 = (bf16[384,1024]{1,0:T(8,128)(2,1)}, bf16[384,1024]{1,0:T(8,128)(2,1)}, u32[]{:S(2)}, u32[]{:S(2)}) collective-permute-start(bf16[384,1024]{1,0:T(8,128)(2,1)} %collective-permute-done.refs_0_), channel_id=1, source_target_pairs={{0,1},{1,0},{2,3},{3,2},{4,5},{5,4},{6,7},{7,6},{8,9},{9,8},{10,11... | collective-permute-start | bytes 2359304 | tf_op jit(solution)/shard_map/ppermute | solution.py:112
  34.0 31.4 %collective-permute-start.8 = (bf16[384,1024]{1,0:T(8,128)(2,1)S(1)}, bf16[384,1024]{1,0:T(8,128)(2,1)}, u32[]{:S(2)}, u32[]{:S(2)}) collective-permute-start(bf16[384,1024]{1,0:T(8,128)(2,1)S(1)} %collective-permute-done.1.refs_1_), channel_id=1, source_target_pairs={{0,1},{1,0},{2,3},{3,2},{4,5},{5,4},{6,7},{7,6},{8,9},{9,8},{10,11... | collective-permute-start | bytes 2359304 | tf_op jit(solution)/shard_map/ppermute | solution.py:112
  59.7 21.7 %collective-permute-start.5 = (bf16[384,1024]{1,0:T(8,128)(2,1)}, bf16[384,1024]{1,0:T(8,128)(2,1)}, u32[]{:S(2)}, u32[]{:S(2)}) collective-permute-start(bf16[384,1024]{1,0:T(8,128)(2,1)} %collective-permute-done.2.refs_0_), channel_id=1, source_target_pairs={{0,4},{1,5},{2,0},{3,1},{6,2},{7,3},{10,6},{11,7},{14,10},{15,11},... | collective-permute-start | bytes 2359304 | tf_op jit(solution)/shard_map/ppermute | solution.py:109
  64.3 28.6 %collective-permute-start.11 = (bf16[384,1024]{1,0:T(8,128)(2,1)}, bf16[384,1024]{1,0:T(8,128)(2,1)S(1)}, u32[]{:S(2)}, u32[]{:S(2)}) collective-permute-start(bf16[384,1024]{1,0:T(8,128)(2,1)} %collective-permute-done.2.refs_0_), channel_id=1, source_target_pairs={{0,1},{1,0},{2,3},{3,2},{4,5},{5,4},{6,7},{7,6},{8,9},{9,8},{10,11... | collective-permute-start | bytes 2359304 | tf_op jit(solution)/shard_map/ppermute | solution.py:112
  64.3 28.6 %collective-permute-start.12 = (bf16[384,1024]{1,0:T(8,128)(2,1)}, bf16[384,1024]{1,0:T(8,128)(2,1)}, u32[]{:S(2)}, u32[]{:S(2)}) collective-permute-start(bf16[384,1024]{1,0:T(8,128)(2,1)} %collective-permute-done.3.refs_1_), channel_id=1, source_target_pairs={{0,1},{1,0},{2,3},{3,2},{4,5},{5,4},{6,7},{7,6},{8,9},{9,8},{10,11... | collective-permute-start | bytes 2359304 | tf_op jit(solution)/shard_map/ppermute | solution.py:112
  156.8 35.5 %all-to-all-start.1 = ((bf16[16,192,128]{2,1,0:T(8,128)(2,1)}), bf16[16,192,128]{2,1,0:T(8,128)(2,1)S(1)}, u32[]{:S(2)}, u32[]{:S(2)}) async-start(bf16[16,192,128]{2,1,0:T(8,128)(2,1)} %attend.1), calls=%async_computation.1 | async-start | bytes 1572864 | tf_op jit(solution)/shard_map/all_to_all | solution.py:642
  161.4 285.4 %reduce-scatter.2.cloned.1.call-start = ((), (), s32[]{:S(2)}) async-start(), calls=%async_computation.5 | async-start | bytes 11141120 | tf_op jit(solution)/shard_map/reduce_scatter | solution.py:758
  363.9 44.1 %collective-permute-start.23 = (bf16[384,1024]{1,0:T(8,128)(2,1)}, bf16[384,1024]{1,0:T(8,128)(2,1)S(1)}, u32[]{:S(2)}, u32[]{:S(2)}) collective-permute-start(bf16[384,1024]{1,0:T(8,128)(2,1)} %get-tuple-element.257), channel_id=1, source_target_pairs={{0,1},{1,0},{2,3},{3,2},{4,5},{5,4},{6,7},{7,6},{8,9},{9,8},{10,11... | collective-permute-start | bytes 2359304 | tf_op jit(solution)/shard_map/ppermute | solution.py:112
  364.0 26.2 %collective-permute-start.26 = (bf16[384,1024]{1,0:T(8,128)(2,1)}, bf16[384,1024]{1,0:T(8,128)(2,1)}, u32[]{:S(2)}, u32[]{:S(2)}) collective-permute-start(bf16[384,1024]{1,0:T(8,128)(2,1)} %get-tuple-element.258), channel_id=1, source_target_pairs={{0,1},{1,0},{2,3},{3,2},{4,5},{5,4},{6,7},{7,6},{8,9},{9,8},{10,11... | collective-permute-start | bytes 2359304 | tf_op jit(solution)/shard_map/ppermute | solution.py:112
  384.0 28.7 %all-to-all-start.3 = ((bf16[16,64,256]{2,1,0:T(8,128)(2,1)}), bf16[16,64,256]{2,1,0:T(8,128)(2,1)S(1)}, u32[]{:S(2)}, u32[]{:S(2)}) async-start(bf16[16,64,256]{2,1,0:T(8,128)(2,1)} %pad_maximum_fusion.5), calls=%async_computation.3 | async-start | bytes 1048576 | tf_op jit(solution)/shard_map/all_to_all | solution.py:642
  389.7 28.5 %collective-permute-start.22 = (bf16[384,1024]{1,0:T(8,128)(2,1)}, bf16[384,1024]{1,0:T(8,128)(2,1)}, u32[]{:S(2)}, u32[]{:S(2)}) collective-permute-start(bf16[384,1024]{1,0:T(8,128)(2,1)} %get-tuple-element.259), channel_id=1, source_target_pairs={{0,1},{1,0},{2,3},{3,2},{4,5},{5,4},{6,7},{7,6},{8,9},{9,8},{10,11... | collective-permute-start | bytes 2359304 | tf_op jit(solution)/shard_map/ppermute | solution.py:112
  409.2 22.0 %collective-permute-start.28 = (bf16[384,1024]{1,0:T(8,128)(2,1)}, bf16[384,1024]{1,0:T(8,128)(2,1)}, u32[]{:S(2)}, u32[]{:S(2)}) collective-permute-start(bf16[384,1024]{1,0:T(8,128)(2,1)} %add_convert_fusion.5), channel_id=1, source_target_pairs={{0,2},{1,3},{2,6},{3,7},{6,10},{7,11},{10,14},{11,15},{14,12},{15,... | collective-permute-start | bytes 2359304 | tf_op jit(solution)/shard_map/ppermute | solution.py:109
  414.5 39.5 %collective-permute-start.21 = (bf16[384,1024]{1,0:T(8,128)(2,1)}, bf16[384,1024]{1,0:T(8,128)(2,1)}, u32[]{:S(2)}, u32[]{:S(2)}) collective-permute-start(bf16[384,1024]{1,0:T(8,128)(2,1)} %get-tuple-element.261), channel_id=1, source_target_pairs={{0,1},{1,0},{2,3},{3,2},{4,5},{5,4},{6,7},{7,6},{8,9},{9,8},{10,11... | collective-permute-start | bytes 2359304 | tf_op jit(solution)/shard_map/ppermute | solution.py:112
  416.6 21.2 %collective-permute-start.30 = (bf16[384,1024]{1,0:T(8,128)(2,1)S(1)}, bf16[384,1024]{1,0:T(8,128)(2,1)S(1)}, u32[]{:S(2)}, u32[]{:S(2)}) collective-permute-start(bf16[384,1024]{1,0:T(8,128)(2,1)S(1)} %copy-done.24), channel_id=1, source_target_pairs={{0,4},{1,5},{2,0},{3,1},{6,2},{7,3},{10,6},{11,7},{14,10},{15,11},... | collective-permute-start | bytes 2359304 | tf_op jit(solution)/shard_map/ppermute | solution.py:109
  418.2 43.1 %collective-permute-start.35 = (bf16[384,1024]{1,0:T(8,128)(2,1)}, bf16[384,1024]{1,0:T(8,128)(2,1)}, u32[]{:S(2)}, u32[]{:S(2)}) collective-permute-start(bf16[384,1024]{1,0:T(8,128)(2,1)} %get-tuple-element.262), channel_id=1, source_target_pairs={{0,1},{1,0},{2,3},{3,2},{4,5},{5,4},{6,7},{7,6},{8,9},{9,8},{10,11... | collective-permute-start | bytes 2359304 | tf_op jit(solution)/shard_map/ppermute | solution.py:112
  454.1 25.5 %collective-permute-start.18 = (bf16[384,1024]{1,0:T(8,128)(2,1)}, bf16[384,1024]{1,0:T(8,128)(2,1)}, u32[]{:S(2)}, u32[]{:S(2)}) collective-permute-start(bf16[384,1024]{1,0:T(8,128)(2,1)} %get-tuple-element.247), channel_id=1, source_target_pairs={{0,16},{16,0},{1,17},{17,1},{2,18},{18,2},{3,19},{19,3},{4,20},{20... | collective-permute-start | bytes 2359304 | tf_op jit(solution)/shard_map/ppermute | solution.py:647
  458.6 24.0 %collective-permute-start.20 = (bf16[384,1024]{1,0:T(8,128)(2,1)}, bf16[384,1024]{1,0:T(8,128)(2,1)}, u32[]{:S(2)}, u32[]{:S(2)}) collective-permute-start(bf16[384,1024]{1,0:T(8,128)(2,1)} %get-tuple-element.263), channel_id=1, source_target_pairs={{0,1},{1,0},{2,3},{3,2},{4,5},{5,4},{6,7},{7,6},{8,9},{9,8},{10,11... | collective-permute-start | bytes 2359304 | tf_op jit(solution)/shard_map/ppermute | solution.py:112
  (64 other events, 814.4 us)
Sparse Core Ops, SparseCore 0:
  100.6 102.0 all-gather.2
  269.9 118.6 reduce-scatter.1

commit v3 on v2

--- a/solution.py
+++ b/solution.py
@@ -172,33 +172,55 @@
 
 def project_kernel(count, *refs):
     tokens, (seg_ref, w_ref, bias_ref, norm_ref), outs = refs[:count], refs[count : count + 4], refs[count + 4 :]
-    n_ref, q_ref, k_ref, v_ref = outs
+    n_ref, k_ref, kv_ref, q_ref, kt_ref, vt_ref = outs
     for i, tok_ref in enumerate(tokens):
         length = tok_ref.shape[0]
+        tiles = length // 128
         cut = slice(i * length, (i + 1) * length)
         normal, _ = normalize(tok_ref[...].astype(F32))
         normed = (normal * norm_ref[0:1, :] + norm_ref[1:2, :]).astype(BF)
         n_ref[cut] = normed
         out = dot_nn(normed, w_ref[...]) + bias_ref[0:1, :]
         out = out.astype(BF).astype(F32)
-        both = out[:, :128]
-        lane = lanes_of(both.shape)
-        seg = jnp.broadcast_to(seg_ref[i : i + 1, :].astype(F32), (128, length)).T
-        same = seg == (lane - DH).astype(F32)
-        key_extra = jnp.where((lane < DH + 8) & ~same, FAR, 0.0)
-        query = jnp.where(lane < DH, both * (1.0 / math.sqrt(DH)), jnp.where(same, 1.0, 0.0))
-        q_ref[cut] = query.astype(BF)
-        k_ref[cut] = jnp.where(lane < DH, pltpu.roll(both, DH, 1), key_extra).astype(BF)
-        v_ref[cut] = out[:, 128:].astype(BF)
+        pair = out[:, :128]
+        lane = lanes_of(pair.shape)
+        seg = seg_ref[i : i + 1, :].astype(F32)
+        apart = jnp.broadcast_to(seg, (128, length)).T != (lane - DH).astype(F32)
+        extra = jnp.where((lane < DH + 8) & apart, FAR, 0.0)
+        kv_ref[cut] = pair.astype(BF)
+        k_ref[cut] = jnp.where(lane < DH, pair, extra).astype(BF)
+        flat = pair.T
+        query = out[:, 128:].T * (1.0 / math.sqrt(DH))
+        for tile in range(tiles):
+            across = slice(tile * 128, (tile + 1) * 128)
+            row = lax.broadcasted_iota(jnp.int32, (128, 128), 0)
+            same = jnp.broadcast_to(seg[:, across], (128, 128)) == (row - DH).astype(F32)
+            hot = jnp.where((row < DH + 8) & same, 1.0, 0.0)
+            q_ref[i * tiles + tile] = jnp.where(row < DH, query[:, across], hot).astype(BF)
+            both = flat[:, across]
+            turned = pltpu.roll(both, DH, 1)
+            left = lanes_of(both.shape) < DH
+            for block, twice in enumerate((jnp.where(left, both, turned), jnp.where(left, turned, both))):
+                at = (i * tiles + tile) * 2 + block
+                kt_ref[at] = twice[:DH].astype(BF)
+                vt_ref[at] = twice[DH:].astype(BF)
 
 
 def project(pieces, segs, weight, bias, norm_rows):
     length, width = pieces[0].shape
     total = length * len(pieces)
     table = jax.ShapeDtypeStruct((total, 128), BF)
+    turned = jax.ShapeDtypeStruct((total // BLK, DH, 128), BF)
     return pl.pallas_call(
         functools.partial(project_kernel, len(pieces)),
-        out_shape=[jax.ShapeDtypeStruct((total, width), BF), table, table, table],
+        out_shape=[
+            jax.ShapeDtypeStruct((total, width), BF),
+            table,
+            table,
+            jax.ShapeDtypeStruct((total // 128, 128, 128), BF),
+            turned,
+            turned,
+        ],
         compiler_params=params(),
         name="project",
     )(*pieces, segs, weight, bias, norm_rows)
@@ -219,54 +241,60 @@
         copy.wait()
 
 
-def fill_null(k_ref, v_ref, rows):
+def null_keys():
     lane = lanes_of((BLK, 128))
-    k_ref[rows : rows + BLK, :] = jnp.where(
-        (lane >= DH) & (lane < DH + 8), FAR, 0.0
-    ).astype(BF)
-    v_ref[rows : rows + BLK, :] = jnp.zeros((BLK, 128), BF)
-
-
-def starts_of(idx_ref, place_ref, block):
-    return [
-        pl.multiple_of(place_ref[idx_ref[block * SLOTS + slot]] * BLK, BLK) for slot in range(SLOTS)
-    ]
-
-
-def gather_rows(starts, ref):
-    return jnp.concatenate([ref[pl.ds(start, BLK), :] for start in starts], axis=0)
-
-
-def softmax_rows(scores):
-    top = jnp.max(scores, axis=1, keepdims=True)
-    raised = jnp.exp(scores - top)
-    return raised * (1.0 / jnp.sum(raised, axis=1, keepdims=True))
+    return jnp.where((lane >= DH) & (lane < DH + 8), FAR, 0.0).astype(BF)
+
+
+def blocks_of(idx_ref, place_ref, block):
+    return [place_ref[idx_ref[block * SLOTS + slot]] for slot in range(SLOTS)]
+
+
+def rows_of(blocks, ref):
+    return jnp.concatenate([ref[pl.ds(pl.multiple_of(b * BLK, BLK), BLK), :] for b in blocks], axis=0)
+
+
+def turned_of(blocks, ref):
+    left = lanes_of((DH, 128)) < DH
+    pairs = [jnp.where(left, ref[one], ref[two]) for one, two in zip(blocks[::2], blocks[1::2])]
+    return jnp.concatenate(pairs, axis=1)
+
+
+def halves(table):
+    left = lanes_of(table.shape) < DH
+    zero = jnp.zeros_like(table)
+    return jnp.where(left, table, zero), jnp.where(left, zero, table)
+
+
+def chances_of(low, high, query, k_ref):
+    keys = jnp.concatenate([rows_of(low, k_ref), rows_of(high, k_ref)], axis=1)
+    scores = dot_nn(keys, jnp.concatenate(halves(query), axis=0))
+    raised = jnp.exp(scores - jnp.max(scores, axis=0, keepdims=True))
+    return raised * (1.0 / jnp.sum(raised, axis=0, keepdims=True))
 
 
 def attend_kernel(parts, idx_ref, src_ref, place_ref, *refs):
-    tables, (o_ref, q_ref, k_ref, v_ref, sem) = refs[: 3 * parts], refs[3 * parts :]
-    rows = q_ref.shape[0]
+    tables, (o_ref, k_ref, q_ref, vt_ref, sem) = refs[: 3 * parts], refs[3 * parts :]
     load_tables(
-        [(tables[i * parts : (i + 1) * parts], dst) for i, dst in enumerate((q_ref, k_ref, v_ref))],
+        [(tables[i * parts : (i + 1) * parts], dst) for i, dst in enumerate((k_ref, q_ref, vt_ref))],
         sem,
     )
-    fill_null(k_ref, v_ref, rows)
-    owners, half, _ = o_ref.shape
-    per = half // BLK
-    lane = lanes_of((BLK, 128))
-
-    def one(piece, owner, part):
-        starts = starts_of(idx_ref, place_ref, owner * (2 * per) + part)
-        keys = gather_rows(starts, k_ref)
-        query = q_ref[pl.ds(pl.multiple_of((piece * (2 * per) + part) * BLK, BLK), BLK), :]
-        chances = softmax_rows(dot_nt(query, keys)).astype(BF)
-        return dot_nn(chances, gather_rows(starts, v_ref))
+    rows = k_ref.shape[0] - BLK
+    k_ref[rows:] = null_keys()
+    vt_ref[rows // BLK] = jnp.zeros((DH, 128), BF)
+    owners, _, count = o_ref.shape
+    tiles = count // 128
+    left = lanes_of((DH, 128)) < DH
 
     def step(piece, carry):
         owner = src_ref[piece]
-        for part in range(per):
-            low, high = one(piece, owner, part), one(piece, owner, part + per)
-            o_ref[owner, part * BLK : (part + 1) * BLK, :] = jnp.where(lane < DH, low, high).astype(BF)
+        for tile in range(tiles):
+            block = (owner * tiles + tile) * 2
+            low, high = blocks_of(idx_ref, place_ref, block), blocks_of(idx_ref, place_ref, block + 1)
+            chances = chances_of(low, high, q_ref[piece * tiles + tile], k_ref).astype(BF)
+            values = jnp.concatenate([turned_of(low, vt_ref), turned_of(high, vt_ref)], axis=0)
+            out = dot_nn(values, chances)
+            o_ref[owner, :, tile * 128 : (tile + 1) * 128] = jnp.where(left, out[:DH], out[DH:]).astype(BF)
         return carry
 
     lax.fori_loop(0, owners, step, 0)
@@ -281,11 +309,11 @@
         functools.partial(attend_kernel, parts),
         in_specs=[pl.BlockSpec(memory_space=pltpu.SMEM)] * 3 + [anywhere] * len(flat),
         out_specs=pl.BlockSpec(memory_space=pltpu.VMEM),
-        out_shape=jax.ShapeDtypeStruct((owners, rows // owners // 2, 128), BF),
+        out_shape=jax.ShapeDtypeStruct((owners, DH, rows // owners), BF),
         scratch_shapes=[
-            pltpu.VMEM((rows, 128), BF),
             pltpu.VMEM((rows + BLK, 128), BF),
-            pltpu.VMEM((rows + BLK, 128), BF),
+            pltpu.VMEM((rows // 128, 128, 128), BF),
+            pltpu.VMEM((rows // BLK + 1, DH, 128), BF),
             pltpu.SemaphoreType.DMA((len(flat),)),
         ],
         compiler_params=params(),
@@ -294,67 +322,72 @@
 
 
 def attend_back_kernel(parts, idx_ref, src_ref, place_ref, *refs):
-    tables, (d_ref, q_ref, k_ref, v_ref, g_ref, dk_ref, dv_ref, sem) = (
-        refs[: 3 * parts + 1],
-        refs[3 * parts + 1 :],
-    )
-    rows = q_ref.shape[0]
+    tables, (d_ref, k_ref, kv_ref, q_ref, kt_ref, g_ref, acc_ref, dq_ref, sem) = (
+        refs[: 4 * parts + 1],
+        refs[4 * parts + 1 :],
+    )
     load_tables(
-        [(tables[i * parts : (i + 1) * parts], dst) for i, dst in enumerate((q_ref, k_ref, v_ref))]
-        + [(tables[3 * parts :], g_ref)],
+        [
+            (tables[i * parts : (i + 1) * parts], dst)
+            for i, dst in enumerate((k_ref, kv_ref, q_ref, kt_ref))
+        ]
+        + [(tables[4 * parts :], g_ref)],
         sem,
     )
-    fill_null(k_ref, v_ref, rows)
-    dk_ref[...] = jnp.zeros_like(dk_ref)
-    dv_ref[...] = jnp.zeros_like(dv_ref)
-    owners, half, _ = g_ref.shape
-    per = half // BLK
-    lane = lanes_of((BLK, 128))
-
-    def one(piece, owner, part, grad):
-        starts = starts_of(idx_ref, place_ref, owner * (2 * per) + part)
-        keys = gather_rows(starts, k_ref)
-        values = gather_rows(starts, v_ref)
-        at = pl.ds(pl.multiple_of((piece * (2 * per) + part) * BLK, BLK), BLK)
-        query = q_ref[at, :]
-        chances = softmax_rows(dot_nt(query, keys))
-        grad_chances = dot_nt(grad, values)
-        inner = jnp.sum(chances * grad_chances, axis=1, keepdims=True)
-        grad_scores = (chances * (grad_chances - inner)).astype(BF)
-        grad_query = dot_nn(grad_scores, keys) * (1.0 / math.sqrt(DH))
-        d_ref[at, 0:128] = jnp.where(lane < DH, grad_query, 0.0).astype(BF)
-        key_adds = dot_tn(grad_scores, query)
-        value_adds = dot_tn(chances.astype(BF), grad)
-        for slot, start in enumerate(starts):
-            cut = slice(slot * BLK, (slot + 1) * BLK)
-            dk_ref[pl.ds(start, BLK), :] += key_adds[cut]
-            dv_ref[pl.ds(start, BLK), :] += value_adds[cut]
+    rows = k_ref.shape[0] - BLK
+    k_ref[rows:] = null_keys()
+    kv_ref[rows:] = jnp.zeros((BLK, 128), BF)
+    kt_ref[rows // BLK] = jnp.zeros((DH, 128), BF)
+    acc_ref[...] = jnp.zeros_like(acc_ref)
+    owners, _, count = g_ref.shape
+    tiles = count // 128
+    left = lanes_of((DH, 128)) < DH
+    zero = jnp.zeros((DH, 128), BF)
 
     def step(piece, carry):
         owner = src_ref[piece]
-        for part in range(per):
-            grad = g_ref[owner, part * BLK : (part + 1) * BLK, :]
-            zero = jnp.zeros_like(grad)
-            one(piece, owner, part, jnp.where(lane < DH, grad, zero))
-            one(piece, owner, part + per, jnp.where(lane < DH, zero, grad))
+        for tile in range(tiles):
+            block = (owner * tiles + tile) * 2
+            low, high = blocks_of(idx_ref, place_ref, block), blocks_of(idx_ref, place_ref, block + 1)
+            query = q_ref[piece * tiles + tile]
+            chances = chances_of(low, high, query, k_ref)
+            grad_low, grad_high = halves(g_ref[owner, :, tile * 128 : (tile + 1) * 128])
+            values = jnp.concatenate([rows_of(low, kv_ref), rows_of(high, kv_ref)], axis=1)
+            grad_chances = dot_nn(values, jnp.concatenate([zero, grad_low, zero, grad_high], axis=0))
+            inner = jnp.sum(chances * grad_chances, axis=0, keepdims=True)
+            grad_scores = (chances * (grad_chances - inner)).astype(BF)
+            query_low, query_high = halves(query[:DH])
+            right = jnp.concatenate(
+                [
+                    jnp.concatenate([query_low, zero], axis=1),
+                    jnp.concatenate([zero, grad_low], axis=1),
+                    jnp.concatenate([query_high, zero], axis=1),
+                    jnp.concatenate([zero, grad_high], axis=1),
+                ],
+                axis=0,
+            )
+            adds = dot_nt(jnp.concatenate([grad_scores, chances.astype(BF)], axis=1), right)
+            keys = jnp.concatenate([turned_of(low, kt_ref), turned_of(high, kt_ref)], axis=0)
+            grad_query = dot_nn(keys, grad_scores)
+            dq_ref[piece * tiles + tile] = jnp.where(left, grad_query[:DH], grad_query[DH:]) * (
+                1.0 / math.sqrt(DH)
+            )
+            for side, blocks in enumerate((low, high)):
+                for slot, b in enumerate(blocks):
+                    at = pl.ds(pl.multiple_of(b * BLK, BLK), BLK)
+                    acc_ref[at, :] += adds[slot * BLK : (slot + 1) * BLK, side * 128 : (side + 1) * 128]
         return carry
 
     lax.fori_loop(0, owners, step, 0)
 
-    chunk = 512
-
     def finish(i, carry):
-        at = pl.ds(pl.multiple_of(i * chunk, chunk), chunk)
-        wide = lanes_of((chunk, 128))
-        grad_keys = pltpu.roll(dk_ref[at, :], DH, 1)
-        grad_query = d_ref[at, 0:128].astype(F32)
-        d_ref[at, 0:128] = jnp.where(wide < DH, grad_query, grad_keys).astype(BF)
-        grad_values = dv_ref[at, :]
-        grad_values = grad_values + pltpu.roll(grad_values, DH, 1)
-        d_ref[at, 128:256] = jnp.where(wide < DH, grad_values, 0.0).astype(BF)
+        at = pl.ds(pl.multiple_of(i * 128, 128), 128)
+        d_ref[at, 0:128] = acc_ref[at, :].astype(BF)
+        tile = jnp.concatenate([dq_ref[i], jnp.zeros((DH, 128), F32)], axis=0)
+        d_ref[at, 128:256] = tile.T.astype(BF)
         return carry
 
-    lax.fori_loop(0, rows // chunk, finish, 0)
+    lax.fori_loop(0, rows // 128, finish, 0, unroll=4)
 
 
 def attend_back(scalars, tables, grads):
@@ -368,12 +401,13 @@
         out_specs=pl.BlockSpec(memory_space=pltpu.VMEM),
         out_shape=jax.ShapeDtypeStruct((rows, 256), BF),
         scratch_shapes=[
-            pltpu.VMEM((rows, 128), BF),
             pltpu.VMEM((rows + BLK, 128), BF),
             pltpu.VMEM((rows + BLK, 128), BF),
+            pltpu.VMEM((rows // 128, 128, 128), BF),
+            pltpu.VMEM((rows // BLK + 1, DH, 128), BF),
             pltpu.VMEM(grads.shape, BF),
             pltpu.VMEM((rows + BLK, 128), F32),
-            pltpu.VMEM((rows + BLK, 128), F32),
+            pltpu.VMEM((rows // 128, DH, 128), F32),
             pltpu.SemaphoreType.DMA((len(flat),)),
         ],
         compiler_params=params(),
@@ -381,33 +415,11 @@
     )(*scalars, *flat)
 
 
-def pack_heads(table_ref, flat):
-    half = flat.shape[0] // 2
-    lane = lanes_of((half, 128))
-    for pair in range(table_ref.shape[0] // 2):
-        cut = slice(pair * 128, (pair + 1) * 128)
-        top, low = flat[:half, cut], flat[half:, cut]
-        table_ref[2 * pair] = jnp.where(lane < DH, top, pltpu.roll(low, DH, 1)).astype(BF)
-        table_ref[2 * pair + 1] = jnp.where(lane < DH, pltpu.roll(top, DH, 1), low).astype(BF)
-
-
-def unpack_heads(flat_ref, table_ref):
-    owners, half, _ = table_ref.shape
-    lane = lanes_of((half, 128))
-    for pair in range(owners // 2):
-        one = table_ref[2 * pair].astype(F32)
-        two = table_ref[2 * pair + 1].astype(F32)
-        cut = slice(pair * 128, (pair + 1) * 128)
-        flat_ref[0:half, cut] = jnp.where(lane < DH, one, pltpu.roll(two, DH, 1)).astype(BF)
-        flat_ref[half : 2 * half, cut] = jnp.where(lane < DH, pltpu.roll(one, DH, 1), two).astype(BF)
-
-
-def out_kernel(att_ref, tok_ref, w_ref, vec_ref, a_ref, mid_ref, n2_ref):
+def out_kernel(att_ref, tok_ref, w_ref, vec_ref, mid_ref, n2_ref):
     width = tok_ref.shape[1]
-    unpack_heads(a_ref, att_ref)
     mid = (
         tok_ref[...].astype(F32)
-        + dot_nn(a_ref[...], w_ref[...].reshape(width, width))
+        + dot_tn(att_ref[...].reshape(width, -1), w_ref[...].reshape(width, width))
         + vec_ref[0:1, :]
     )
     mid_ref[...] = mid
@@ -431,12 +443,8 @@
         out_kernel,
         grid=(1,),
         in_specs=[whole(attended.shape), whole(shape), out_rows(weights), whole(vectors.shape)],
-        out_specs=[whole(shape)] * 3,
-        out_shape=[
-            jax.ShapeDtypeStruct(shape, BF),
-            jax.ShapeDtypeStruct(shape, F32),
-            jax.ShapeDtypeStruct(shape, BF),
-        ],
+        out_specs=[whole(shape)] * 2,
+        out_shape=[jax.ShapeDtypeStruct(shape, F32), jax.ShapeDtypeStruct(shape, BF)],
         compiler_params=params("arbitrary"),
         name="project_out",
     )(attended, tokens, weights, vectors)
@@ -562,7 +570,7 @@
 
 
 def out_back_kernel(
-    mid_ref, gn_ref, other_ref, cot_ref, a_ref, w_ref, vec_ref, _, gm_ref, ga_ref, gv_ref, grads_hbm, buf, sem
+    mid_ref, gn_ref, other_ref, cot_ref, att_ref, w_ref, vec_ref, _, gm_ref, ga_ref, gv_ref, grads_hbm, buf, sem
 ):
     width = mid_ref.shape[1]
     rows = grads_hbm.shape[1]
@@ -572,8 +580,8 @@
     grad_mid = cot + norm_backward(grad, normal, scale, vec_ref[1:2, :])
     gm_ref[...] = grad_mid
     branch = grad_mid.astype(BF)
-    pack_heads(ga_ref, dot_nt(branch, w_ref[...].reshape(width, width)))
-    buf[...] = dot_tn(a_ref[...], branch).astype(BF).reshape(buf.shape)
+    ga_ref[...] = dot_nt(w_ref[...].reshape(width, width), branch).astype(BF).reshape(ga_ref.shape)
+    buf[...] = dot_nn(att_ref[...].reshape(width, -1), branch).astype(BF).reshape(buf.shape)
     copy = pltpu.make_async_copy(buf, grads_hbm.at[:, pl.ds(rows - buf.shape[1], buf.shape[1])], sem)
     copy.start()
     gv_ref[...] = jnp.zeros_like(gv_ref)
@@ -584,15 +592,15 @@
     copy.wait()
 
 
-def project_out_back(mid, grad, other, cotangent, flat, weights, vectors, grads):
+def project_out_back(mid, grad, other, cotangent, attended, weights, vectors, grads):
     owners, own, width, units, chunks = layout_of(weights)
     shape = mid.shape
-    packed = (owners, shape[0] // 2, 128)
+    packed = attended.shape
     anywhere = pl.BlockSpec(memory_space=pl.ANY)
     return pl.pallas_call(
         out_back_kernel,
         grid=(1,),
-        in_specs=[whole(shape)] * 5 + [out_rows(weights), whole(vectors.shape), anywhere],
+        in_specs=[whole(shape)] * 4 + [whole(packed), out_rows(weights), whole(vectors.shape), anywhere],
         out_specs=[whole(shape), whole(packed), whole((8, width)), anywhere],
         out_shape=[
             jax.ShapeDtypeStruct(shape, F32),
@@ -604,7 +612,7 @@
         input_output_aliases={7: 3},
         compiler_params=params("arbitrary"),
         name="project_out_back",
-    )(mid, grad, other, cotangent, flat, weights, vectors, grads)
+    )(mid, grad, other, cotangent, attended, weights, vectors, grads)
 
 
 def shares_kernel(starts, d_ref, w_ref, *outs):
@@ -687,14 +695,13 @@
     half = lax.axis_index("rep") % 2
 
     tiles = jnp.concatenate(
-        [w.reshape(own, owners, DH) for w in (w_query, w_key, w_value)], axis=2
+        [w.reshape(own, owners, DH) for w in (w_key, w_value, w_query)], axis=2
     ).transpose(1, 0, 2)
     small = jnp.concatenate([b_out, ln2_gain, ln2_bias, b_down, ln1_gain, ln1_bias, b_up])
     small = jnp.pad(small, (0, own * DH - small.shape[0])).reshape(1, own, DH)
     sent = jnp.concatenate([tiles, jnp.broadcast_to(small, (owners, own, DH))], axis=2)
     got = exchange(sent)
-    weight = jnp.concatenate([got[:, :, : 3 * DH], got[:, :, 2 * DH : 3 * DH]], axis=2)
-    weight = weight.reshape(width, 4 * DH)
+    weight = jnp.pad(got[:, :, : 3 * DH], ((0, 0), (0, 0), (0, DH))).reshape(width, 4 * DH)
     rows = got[:, :, 3 * DH :].reshape(owners, own * DH)[:, : 6 * own + hidden // owners]
     rows = rows.astype(F32)
     fixed = rows[:, : 6 * own].reshape(owners, 6, own).transpose(1, 0, 2).reshape(6, width)
@@ -702,7 +709,7 @@
     vectors = jnp.concatenate([fixed[:4], up_bias.reshape(2, width), jnp.zeros((2, width), F32)], axis=0)
     norm_rows = jnp.pad(fixed[4:6], ((0, 6), (0, 0)))
     zero = jnp.zeros((DH,), F32)
-    bias = jnp.concatenate([b_query.astype(F32), zero, b_value.astype(F32), b_value.astype(F32)])
+    bias = jnp.concatenate([zero, b_value.astype(F32), b_query.astype(F32), zero])
     bias = jnp.broadcast_to(bias[None], (8, 4 * DH))
 
     up_half = lax.dynamic_index_in_dim(w_up.reshape(own, owners, 2, units), half, 2, keepdims=False)
@@ -735,9 +742,9 @@
     mine, _ = lax.optimization_barrier((mine, late))
     weights = lax.all_gather(mine, "shard", axis=0)
     projected, other_cotangent = lax.optimization_barrier((projected, other_cotangent))
-    tables = [[stage[i] for stage in projected] for i in (1, 2, 3)]
-    attended = exchange(attend(scalars, tables, owners))
-    flat, mid, normed_two = project_out(attended, tokens, weights, vectors)
+    table = lambda *which: [[stage[i] for stage in projected] for i in which]
+    attended = exchange(attend(scalars, table(1, 3, 5), owners))
+    mid, normed_two = project_out(attended, tokens, weights, vectors)
     other_normed = trade(normed_two)
     more, grad_two, hid, grad_pre, bias_one = feed(normed_two, cotangent, weights, vectors, F32)
     other_normed, grad_two = lax.optimization_barrier((other_normed, grad_two))
@@ -752,13 +759,13 @@
         weights,
     )
     grad_middle, grad_attended, grad_rows, grads = project_out_back(
-        mid, grad_two, other_grad, cotangent, flat, weights, vectors, grads
+        mid, grad_two, other_grad, cotangent, attended, weights, vectors, grads
     )
     layer_out = (mid + more + other_more.astype(F32) + fixed[3][None]).astype(BF)
     shares = lax.psum_scatter(
         grads.reshape(-1, width), "shard", scatter_dimension=0, tiled=True
     )
-    grad_table = attend_back(scalars, tables, exchange(grad_attended))
+    grad_table = attend_back(scalars, table(1, 2, 3, 4), exchange(grad_attended))
     at = {piece: i * count for i, piece in enumerate(ring.pieces)}
     order = ring.scatter_order()
     other_shares = head_shares(grad_table, weight, [at[k, 1] for k in order], count)
@@ -805,7 +812,7 @@
         heads = heads.astype(F32) + trade(heads).astype(F32)
         heads = heads.transpose(1, 2, 0).reshape(own, 3, DH, owners).transpose(1, 0, 3, 2)
         heads = heads.reshape(3, own, width)
-        tail = jnp.concatenate([back_sum, grad_bias[0, :DH], grad_bias[0, 2 * DH : 3 * DH]])
+        tail = jnp.concatenate([back_sum, grad_bias[0, 2 * DH : 3 * DH], grad_bias[0, DH : 2 * DH]])
         tail = over_alike(tail.astype(BF))
         tail_other = trade(tail).astype(F32)
         tail = tail.astype(F32)
@@ -829,10 +836,10 @@
         return (
             piece(4),
             piece(5),
+            heads[2],
+            total[length : length + DH],
             heads[0],
-            total[length : length + DH],
             heads[1],
-            heads[2],
             total[length + DH :],
             grad_out,
             piece(0),

time: 520 us -> 517 us (level)
  Pallas kernels: 196 us -> 157 us
  waiting for transfers between devices: 133 us -> 169 us
    pallas_call x1, Pallas kernels: 61.4 us -> 36.3 us  [attend_back(): pl.pallas_call(functools.partial(attend_back_kernel, parts), in_specs=[pl...]
    ppermute x16, waiting for transfers between devices: 73.2 us -> 91.8 us  [hop(): return lax.ppermute(table, 'shard', pairs)]
    pallas_call x1, Pallas kernels: 38.4 us -> 22.9 us  [attend(): pl.pallas_call(functools.partial(attend_kernel, parts), in_specs=[pl.Bloc...]
    all_gather x1, waiting for transfers between devices: 10.5 us -> 24.6 us  [local(): weights = lax.all_gather(mine, 'shard', axis=0)]
    unnamed x92 -> x94, local copies, waits for them, and re-layouts: 12.1 us -> 12.1 us
  transfers between devices with their start and end apart: 44 -> 44, of which waited for: 19 -> 20; matrix products, arithmetic and copies ran while one was open for 15% -> 16% of each run, Pallas kernels for 32% -> 25%
where the time goes in v3:
time: 517 us; the launch traced here: 509 us
  waiting for transfers between devices  169 us (33%)
  Pallas kernels  157 us (30%)
  starting transfers between devices  51.8 us (10%)
  local copies, waits for them, and re-layouts  44.5 us (9%)
  other arithmetic  43.2 us (8%)
  blocking collectives  23.8 us (5%)
  between operations  15.4 us (3%)
    ppermute x16, waiting for transfers between devices, hop(): return lax.ppermute(table, 'shard', pairs)  91.8 us
    all_to_all x3, waiting for transfers between devices, exchange(): lax.all_to_all(table, 'shard', split_axis=0, concat_axis=0, tiled=True)  38.4 us
    pallas_call x1, Pallas kernels, attend_back(): pl.pallas_call(functools.partial(attend_back_kernel, parts), in_specs=[pl...  36.3 us
    pallas_call x5, Pallas kernels, project(): pl.pallas_call(functools.partial(project_kernel, len(pieces)), out_shape=...  30.2 us
    pallas_call x2, Pallas kernels, feed(): pl.pallas_call(feed_kernel, grid=(chunks,), in_specs=[whole(normed.shape)...  25.3 us
    all_gather x1, waiting for transfers between devices, local(): weights = lax.all_gather(mine, 'shard', axis=0)  24.6 us
    all_to_all x1, blocking collectives, exchange(): lax.all_to_all(table, 'shard', split_axis=0, concat_axis=0, tiled=True)  23.8 us
    ppermute x16, starting transfers between devices, hop(): return lax.ppermute(table, 'shard', pairs)  23.3 us
  transfers between devices with their start and end apart: 44, of which 20 were waited for; matrix products, arithmetic and copies ran while one was open for 16% of the time, Pallas kernels for 25%

profile of v3, /device:TPU:0, one launch (start us, length us, event | category | flops | bytes accessed | tf_op | source)
XLA Modules:
  0.0 508.7 jit_solution(15803731963848200854)
XLA Ops:
  10.5 4.7 concatenate.64
  19.4 6.5 %all-to-all-start = ((bf16[16,64,256]{2,1,0:T(8,128)(2,1)}), bf16[16,64,256]{2,1,0:T(8,128)(2,1)S(1)}, u32[]{:S(2)}, u32[]{:S(2)}) async-start(bf16[16,64,256]{2,1,0:T(8,128)(2,1)} %pad_maximum_fusion.3), calls=%async_computation | async-start | bytes 1048576 | tf_op jit(solution)/shard_map/all_to_all | solution.py:650
  34.6 7.8 %all-to-all-done = bf16[16,64,256]{2,1,0:T(8,128)(2,1)S(1)} async-done(((bf16[16,64,256]{2,1,0:T(8,128)(2,1)}), bf16[16,64,256]{2,1,0:T(8,128)(2,1)S(1)}, u32[]{:S(2)}, u32[]{:S(2)}) %all-to-all-start) | async-done | bytes 524320 | tf_op jit(solution)/shard_map/all_to_all | solution.py:650
  44.5 8.9 %collective-permute-done.2.refs_0_ = bf16[384,1024]{1,0:T(8,128)(2,1)} collective-permute-done((bf16[384,1024]{1,0:T(8,128)(2,1)}, bf16[384,1024]{1,0:T(8,128)(2,1)}, u32[]{:S(2)}, u32[]{:S(2)}) %collective-permute-start.2) | collective-permute-done | bytes 786464 | tf_op jit(solution)/shard_map/ppermute | solution.py:109
  65.6 7.1 %project.6 = (bf16[1536,1024]{1,0:T(8,128)(2,1)}, bf16[1536,128]{1,0:T(8,128)(2,1)}, bf16[1536,128]{1,0:T(8,128)(2,1)}, bf16[12,128,128]{2,1,0:T(8,128)(2,1)}, b...) custom-call(bf16[384,1024]{1,0:T(8,128)(2,1)} %collective-permute-done.refs_0_, bf16[384,1024]{1,0:T(8,128)(2,1)} %copy-done.18, ...), custom_call_target="tpu_custom_call" | custom-call | tf_op jit(solution)/shard_map/project/pallas_call | solution.py:214
  72.7 8.7 %collective-permute-done.5.refs_0_ = bf16[384,1024]{1,0:T(8,128)(2,1)} collective-permute-done((bf16[384,1024]{1,0:T(8,128)(2,1)}, bf16[384,1024]{1,0:T(8,128)(2,1)}, u32[]{:S(2)}, u32[]{:S(2)}) %collective-permute-start.5) | collective-permute-done | bytes 786464 | tf_op jit(solution)/shard_map/ppermute | solution.py:109
  93.9 7.1 %project.7 = (bf16[1536,1024]{1,0:T(8,128)(2,1)}, bf16[1536,128]{1,0:T(8,128)(2,1)}, bf16[1536,128]{1,0:T(8,128)(2,1)}, bf16[12,128,128]{2,1,0:T(8,128)(2,1)}, b...) custom-call(bf16[384,1024]{1,0:T(8,128)(2,1)} %collective-permute-done.2.refs_0_, ...), custom_call_target="tpu_custom_call" | custom-call | tf_op jit(solution)/shard_map/project/pallas_call | solution.py:214
  107.7 7.4 %project.8 = (bf16[1536,1024]{1,0:T(8,128)(2,1)}, bf16[1536,128]{1,0:T(8,128)(2,1)}, bf16[1536,128]{1,0:T(8,128)(2,1)}, bf16[12,128,128]{2,1,0:T(8,128)(2,1)}, b...) custom-call(bf16[384,1024]{1,0:T(8,128)(2,1)} %collective-permute-done.5.refs_0_, ...), custom_call_target="tpu_custom_call" | custom-call | tf_op jit(solution)/shard_map/project/pallas_call | solution.py:214
  119.4 22.9 %attend.1 = bf16[16,64,384]{2,1,0:T(8,128)(2,1)} custom-call(s32[768]{0:T(1024)} %and_select_fusion.idx_ref, s32[16]{0:T(128)} %copy-done.30, s32[97]{0:T(128)} %pad_add_fusion.place_ref, bf16[768,128]{1,0:T(8,128)(2,1)} %get-tuple-element.278.refs_0_, bf16[1536,128]{1,0:T(8,128)(2,1)} %get-tuple-element.279.refs_1_, ...), custom_call_target="tpu_custom_call" | custom-call | tf_op jit(solution)/shard_map/attend/pallas_call | solution.py:308
  142.3 4.8 all-to-all-start.1
  148.1 30.5 %all-to-all-done.1.att_ref = bf16[16,64,384]{2,1,0:T(8,128)(2,1)S(1)} async-done(((bf16[16,64,384]{2,1,0:T(8,128)(2,1)}), bf16[16,64,384]{2,1,0:T(8,128)(2,1)S(1)}, u32[]{:S(2)}, u32[]{:S(2)}) %all-to-all-start.1) | async-done | bytes 786464 | tf_op jit(solution)/shard_map/all_to_all | solution.py:650
  178.6 24.6 %all-gather.3.cloned.1.call-done = bf16[5120,1024]{1,0:T(8,128)(2,1)} async-done(((bf16[320,1024]{1,0:T(8,128)(2,1)}), bf16[5120,1024]{1,0:T(8,128)(2,1)}) %all-gather.3.cloned.1.call-update) | async-done | bytes 10485776 | tf_op jit(solution)/shard_map/all_gather | solution.py:743
  209.1 12.9 %feed.2 = (f32[384,1024]{1,0:T(8,128)}, f32[384,1024]{1,0:T(8,128)}, bf16[384,2048]{1,0:T(8,128)(2,1)}, bf16[384,2048]{1,0:T(8,128)(2,1)}, f32[8,1024]{1,0:T(8,128)}) custom-call(bf16[384,1024]{1,0:T(8,128)(2,1)} %get-tuple-element.295.n2_ref.na_ref, bf16[384,1024]{1,0:T(8,128)(2,1)} %bitcast.76, bf16[16,320,1024]{2,1,0:T(8,128)(2,1)} %bitcast.62, ...), custom_call_target="tpu_custom_call" | custom-call | tf_op jit(solution)/shard_map/feed/pallas_call | solution.py:499
  222.0 5.6 %collective-permute-done.17.n2_ref.nb_ref = bf16[384,1024]{1,0:T(8,128)(2,1)S(1)} collective-permute-done((bf16[384,1024]{1,0:T(8,128)(2,1)}, bf16[384,1024]{1,0:T(8,128)(2,1)S(1)}, u32[]{:S(2)}, u32[]{:S(2)}) %collective-permute-start.17) | collective-permute-done | bytes 786464 | tf_op jit(solution)/shard_map/ppermute | solution.py:655
  228.5 12.4 %feed.3 = (bf16[384,1024]{1,0:T(8,128)(2,1)}, bf16[384,1024]{1,0:T(8,128)(2,1)}, bf16[384,2048]{1,0:T(8,128)(2,1)}, bf16[384,2048]{1,0:T(8,128)(2,1)}, f32[8,1024]{1,0:T(8,128)}) custom-call(bf16[384,1024]{1,0:T(8,128)(2,1)} %copy-done.9, bf16[384,1024]{1,0:T(8,128)(2,1)} %copy-done.8, bf16[16,320,1024]{2,1,0:T(8,128)(2,1)} %bitcast.64, ...), custom_call_target="tpu_custom_call" | custom-call | tf_op jit(solution)/shard_map/feed/pallas_call | solution.py:499
  242.3 13.7 %feed_grads.1._ = bf16[16,320,1024]{2,1,0:T(8,128)(2,1)} custom-call(bf16[384,1024]{1,0:T(8,128)(2,1)} %get-tuple-element.295.n2_ref.na_ref, bf16[384,1024]{1,0:T(8,128)(2,1)} %copy-done.9, bf16[384,1024]{1,0:T(8,128)(2,1)} %bitcast.77, bf16[384,1024]{1,0:T(8,128)(2,1)} %copy-done.8, bf16[384,2048]{1,0:T(8,128)(2,1)} %get-tuple-element.313.ha_ref, ...), custom_call_target="tpu_custom_call" | custom-call | tf_op jit(solution)/shard_map/feed_grads/pallas_call | solution.py:556
  260.8 9.5 %project_out_back.1 = (f32[384,1024]{1,0:T(8,128)}, bf16[16,64,384]{2,1,0:T(8,128)(2,1)}, f32[8,1024]{1,0:T(8,128)}, bf16[16,320,1024]{2,1,0:T(8,128)(2,1)}) custom-call(f32[384,1024]{1,0:T(8,128)} %get-tuple-element.294.mid_ref, f32[384,1024]{1,0:T(8,128)} %get-tuple-element.311.gn_ref, ...), custom_call_target="tpu_custom_call", output_to_operand_aliasing={{3}: (7, {})} | custom-call | tf_op jit(solution)/shard_map/project_out_back/pallas_call | solution.py:600
  271.5 23.8 %all_to_all.20.refs_20_ = bf16[16,64,384]{2,1,0:T(8,128)(2,1)} all-to-all(bf16[16,64,384]{2,1,0:T(8,128)(2,1)S(1)} %copy-done.15), channel_id=1, replica_groups=mesh['rep'=2,'shard'=16] {'shard'}, dimensions={0} | all-to-all | bytes 1572864 | tf_op jit(solution)/shard_map/all_to_all | solution.py:650
  295.2 36.3 %attend_back.1.d_ref = bf16[6144,256]{1,0:T(8,128)(2,1)} custom-call(s32[768]{0:T(1024)} %and_select_fusion.idx_ref, s32[16]{0:T(128)} %copy-done.30, s32[97]{0:T(128)} %pad_add_fusion.place_ref, bf16[768,128]{1,0:T(8,128)(2,1)} %get-tuple-element.278.refs_0_, bf16[1536,128]{1,0:T(8,128)(2,1)} %get-tuple-element.279.refs_1_, ...), custom_call_target="tpu_custom_call" | custom-call | tf_op jit(solution)/shard_map/attend_back/pallas_call | solution.py:398
  331.6 5.2 %head_shares.2 = (bf16[384,1024]{1,0:T(8,128)(2,1)}, bf16[384,1024]{1,0:T(8,128)(2,1)}, bf16[384,1024]{1,0:T(8,128)(2,1)}, bf16[384,1024]{1,0:T(8,128)(2,1)}, bf...) custom-call(bf16[6144,256]{1,0:T(8,128)(2,1)} %attend_back.1.d_ref, ...), custom_call_target="tpu_custom_call" | custom-call | tf_op jit(solution)/shard_map/head_shares/pallas_call | solution.py:626
  340.0 5.2 %head_shares.3 = (bf16[384,1024]{1,0:T(8,128)(2,1)}, bf16[384,1024]{1,0:T(8,128)(2,1)}, bf16[384,1024]{1,0:T(8,128)(2,1)}, bf16[384,1024]{1,0:T(8,128)(2,1)}, bf...) custom-call(bf16[6144,256]{1,0:T(8,128)(2,1)} %attend_back.1.d_ref, ...), custom_call_target="tpu_custom_call" | custom-call | tf_op jit(solution)/shard_map/head_shares/pallas_call | solution.py:626
  365.7 32.2 %collective-permute-done.27 = bf16[192,1024]{1,0:T(8,128)(2,1)S(1)} collective-permute-done((bf16[192,1024]{1,0:T(8,128)(2,1)S(1)}, bf16[192,1024]{1,0:T(8,128)(2,1)S(1)}, u32[]{:S(2)}, u32[]{:S(2)}) %collective-permute-start.27) | collective-permute-done | bytes 393248 | tf_op jit(solution)/shard_map/ppermute | solution.py:109
  414.7 13.4 %collective-permute-done.28 = bf16[384,1024]{1,0:T(8,128)(2,1)} collective-permute-done((bf16[384,1024]{1,0:T(8,128)(2,1)}, bf16[384,1024]{1,0:T(8,128)(2,1)}, u32[]{:S(2)}, u32[]{:S(2)}) %collective-permute-start.28) | collective-permute-done | bytes 786464 | tf_op jit(solution)/shard_map/ppermute | solution.py:109
  479.8 13.1 %collective-permute-done.37 = bf16[384,1024]{1,0:T(8,128)(2,1)S(1)} collective-permute-done((bf16[384,1024]{1,0:T(8,128)(2,1)}, bf16[384,1024]{1,0:T(8,128)(2,1)S(1)}, u32[]{:S(2)}, u32[]{:S(2)}) %collective-permute-start.37) | collective-permute-done | bytes 786464 | tf_op jit(solution)/shard_map/ppermute | solution.py:109
  (318 shorter events, 168.9 us)
Async XLA Ops:
  7.2 47.7 %collective-permute-start.4 = (bf16[384,1024]{1,0:T(8,128)(2,1)}, bf16[384,1024]{1,0:T(8,128)(2,1)S(1)}, u32[]{:S(2)}, u32[]{:S(2)}) collective-permute-start(bf16[384,1024]{1,0:T(8,128)(2,1)} %bitcast.80), channel_id=1, source_target_pairs={{0,1},{1,0},{2,3},{3,2},{4,5},{5,4},{6,7},{7,6},{8,9},{9,8},{10,11... | collective-permute-start | bytes 2359304 | tf_op jit(solution)/shard_map/ppermute | solution.py:112
  7.8 21.4 %collective-permute-start.1 = (bf16[384,1024]{1,0:T(8,128)(2,1)}, bf16[384,1024]{1,0:T(8,128)(2,1)S(1)}, u32[]{:S(2)}, u32[]{:S(2)}) collective-permute-start(bf16[384,1024]{1,0:T(8,128)(2,1)} %bitcast.81), channel_id=1, source_target_pairs={{0,2},{1,3},{2,6},{3,7},{6,10},{7,11},{10,14},{11,15},{14,12},{15,... | collective-permute-start | bytes 2359304 | tf_op jit(solution)/shard_map/ppermute | solution.py:109
  19.4 23.1 %all-to-all-start = ((bf16[16,64,256]{2,1,0:T(8,128)(2,1)}), bf16[16,64,256]{2,1,0:T(8,128)(2,1)S(1)}, u32[]{:S(2)}, u32[]{:S(2)}) async-start(bf16[16,64,256]{2,1,0:T(8,128)(2,1)} %pad_maximum_fusion.3), calls=%async_computation | async-start | bytes 1048576 | tf_op jit(solution)/shard_map/all_to_all | solution.py:650
  25.8 177.4 %all-gather.3.cloned.1.call-start = ((), (), s32[]{:S(2)}) async-start(), calls=%async_computation.6 | async-start | bytes 11141120 | tf_op jit(solution)/shard_map/all_gather | solution.py:743
  31.3 22.1 %collective-permute-start.2 = (bf16[384,1024]{1,0:T(8,128)(2,1)}, bf16[384,1024]{1,0:T(8,128)(2,1)}, u32[]{:S(2)}, u32[]{:S(2)}) collective-permute-start(bf16[384,1024]{1,0:T(8,128)(2,1)} %collective-permute-done.refs_0_), channel_id=1, source_target_pairs={{0,4},{1,5},{2,0},{3,1},{6,2},{7,3},{10,6},{11,7},{14,10},{15,11},... | collective-permute-start | bytes 2359304 | tf_op jit(solution)/shard_map/ppermute | solution.py:109
  31.3 23.0 %collective-permute-start.3 = (bf16[384,1024]{1,0:T(8,128)(2,1)S(1)}, bf16[384,1024]{1,0:T(8,128)(2,1)}, u32[]{:S(2)}, u32[]{:S(2)}) collective-permute-start(bf16[384,1024]{1,0:T(8,128)(2,1)S(1)} %collective-permute-done.1.refs_1_), channel_id=1, source_target_pairs={{0,2},{1,3},{2,6},{3,7},{6,10},{7,11},{10,14},{11,15},{14,12},{15,... | collective-permute-start | bytes 2359304 | tf_op jit(solution)/shard_map/ppermute | solution.py:109
  34.1 30.4 %collective-permute-start.7 = (bf16[384,1024]{1,0:T(8,128)(2,1)}, bf16[384,1024]{1,0:T(8,128)(2,1)}, u32[]{:S(2)}, u32[]{:S(2)}) collective-permute-start(bf16[384,1024]{1,0:T(8,128)(2,1)} %collective-permute-done.refs_0_), channel_id=1, source_target_pairs={{0,1},{1,0},{2,3},{3,2},{4,5},{5,4},{6,7},{7,6},{8,9},{9,8},{10,11... | collective-permute-start | bytes 2359304 | tf_op jit(solution)/shard_map/ppermute | solution.py:112
  34.1 31.5 %collective-permute-start.8 = (bf16[384,1024]{1,0:T(8,128)(2,1)S(1)}, bf16[384,1024]{1,0:T(8,128)(2,1)}, u32[]{:S(2)}, u32[]{:S(2)}) collective-permute-start(bf16[384,1024]{1,0:T(8,128)(2,1)S(1)} %collective-permute-done.1.refs_1_), channel_id=1, source_target_pairs={{0,1},{1,0},{2,3},{3,2},{4,5},{5,4},{6,7},{7,6},{8,9},{9,8},{10,11... | collective-permute-start | bytes 2359304 | tf_op jit(solution)/shard_map/ppermute | solution.py:112
  60.0 21.4 %collective-permute-start.5 = (bf16[384,1024]{1,0:T(8,128)(2,1)}, bf16[384,1024]{1,0:T(8,128)(2,1)}, u32[]{:S(2)}, u32[]{:S(2)}) collective-permute-start(bf16[384,1024]{1,0:T(8,128)(2,1)} %collective-permute-done.2.refs_0_), channel_id=1, source_target_pairs={{0,4},{1,5},{2,0},{3,1},{6,2},{7,3},{10,6},{11,7},{14,10},{15,11},... | collective-permute-start | bytes 2359304 | tf_op jit(solution)/shard_map/ppermute | solution.py:109
  64.5 28.5 %collective-permute-start.11 = (bf16[384,1024]{1,0:T(8,128)(2,1)}, bf16[384,1024]{1,0:T(8,128)(2,1)S(1)}, u32[]{:S(2)}, u32[]{:S(2)}) collective-permute-start(bf16[384,1024]{1,0:T(8,128)(2,1)} %collective-permute-done.2.refs_0_), channel_id=1, source_target_pairs={{0,1},{1,0},{2,3},{3,2},{4,5},{5,4},{6,7},{7,6},{8,9},{9,8},{10,11... | collective-permute-start | bytes 2359304 | tf_op jit(solution)/shard_map/ppermute | solution.py:112
  64.5 28.5 %collective-permute-start.12 = (bf16[384,1024]{1,0:T(8,128)(2,1)}, bf16[384,1024]{1,0:T(8,128)(2,1)}, u32[]{:S(2)}, u32[]{:S(2)}) collective-permute-start(bf16[384,1024]{1,0:T(8,128)(2,1)} %collective-permute-done.3.refs_1_), channel_id=1, source_target_pairs={{0,1},{1,0},{2,3},{3,2},{4,5},{5,4},{6,7},{7,6},{8,9},{9,8},{10,11... | collective-permute-start | bytes 2359304 | tf_op jit(solution)/shard_map/ppermute | solution.py:112
  142.3 36.3 %all-to-all-start.1 = ((bf16[16,64,384]{2,1,0:T(8,128)(2,1)}), bf16[16,64,384]{2,1,0:T(8,128)(2,1)S(1)}, u32[]{:S(2)}, u32[]{:S(2)}) async-start(bf16[16,64,384]{2,1,0:T(8,128)(2,1)} %attend.1), calls=%async_computation.1 | async-start | bytes 1572864 | tf_op jit(solution)/shard_map/all_to_all | solution.py:650
  147.1 297.0 %reduce-scatter.2.cloned.1.call-start = ((), (), s32[]{:S(2)}) async-start(), calls=%async_computation.5 | async-start | bytes 11141120 | tf_op jit(solution)/shard_map/reduce_scatter | solution.py:765
  339.4 60.8 %collective-permute-start.23 = (bf16[384,1024]{1,0:T(8,128)(2,1)}, bf16[384,1024]{1,0:T(8,128)(2,1)S(1)}, u32[]{:S(2)}, u32[]{:S(2)}) collective-permute-start(bf16[384,1024]{1,0:T(8,128)(2,1)} %get-tuple-element.319), channel_id=1, source_target_pairs={{0,1},{1,0},{2,3},{3,2},{4,5},{5,4},{6,7},{7,6},{8,9},{9,8},{10,11... | collective-permute-start | bytes 2359304 | tf_op jit(solution)/shard_map/ppermute | solution.py:112
  339.5 26.2 %collective-permute-start.26 = (bf16[384,1024]{1,0:T(8,128)(2,1)}, bf16[384,1024]{1,0:T(8,128)(2,1)}, u32[]{:S(2)}, u32[]{:S(2)}) collective-permute-start(bf16[384,1024]{1,0:T(8,128)(2,1)} %get-tuple-element.320), channel_id=1, source_target_pairs={{0,1},{1,0},{2,3},{3,2},{4,5},{5,4},{6,7},{7,6},{8,9},{9,8},{10,11... | collective-permute-start | bytes 2359304 | tf_op jit(solution)/shard_map/ppermute | solution.py:112
  359.5 49.8 %all-to-all-start.3 = ((bf16[16,64,256]{2,1,0:T(8,128)(2,1)}), bf16[16,64,256]{2,1,0:T(8,128)(2,1)S(1)}, u32[]{:S(2)}, u32[]{:S(2)}) async-start(bf16[16,64,256]{2,1,0:T(8,128)(2,1)} %pad_maximum_fusion.4), calls=%async_computation.3 | async-start | bytes 1048576 | tf_op jit(solution)/shard_map/all_to_all | solution.py:650
  363.3 34.6 %collective-permute-start.27 = (bf16[192,1024]{1,0:T(8,128)(2,1)S(1)}, bf16[192,1024]{1,0:T(8,128)(2,1)S(1)}, u32[]{:S(2)}, u32[]{:S(2)}) collective-permute-start(bf16[192,1024]{1,0:T(8,128)(2,1)S(1)} %get-tuple-element.384), channel_id=1, source_target_pairs={{0,4},{1,5},{2,0},{3,1},{6,2},{7,3},{10,6},{11,7},{14,10},{15,11},... | collective-permute-start | bytes 1179656 | tf_op jit(solution)/shard_map/ppermute | solution.py:109
  365.2 49.5 %collective-permute-start.22 = (bf16[384,1024]{1,0:T(8,128)(2,1)}, bf16[384,1024]{1,0:T(8,128)(2,1)}, u32[]{:S(2)}, u32[]{:S(2)}) collective-permute-start(bf16[384,1024]{1,0:T(8,128)(2,1)} %get-tuple-element.321), channel_id=1, source_target_pairs={{0,1},{1,0},{2,3},{3,2},{4,5},{5,4},{6,7},{7,6},{8,9},{9,8},{10,11... | collective-permute-start | bytes 2359304 | tf_op jit(solution)/shard_map/ppermute | solution.py:112
  365.2 39.0 %collective-permute-start.25 = (bf16[192,1024]{1,0:T(8,128)(2,1)S(1)}, bf16[192,1024]{1,0:T(8,128)(2,1)S(1)}, u32[]{:S(2)}, u32[]{:S(2)}) collective-permute-start(bf16[192,1024]{1,0:T(8,128)(2,1)S(1)} %get-tuple-element.385), channel_id=1, source_target_pairs={{0,2},{1,3},{2,6},{3,7},{6,10},{7,11},{10,14},{11,15},{14,12},{15,... | collective-permute-start | bytes 1179656 | tf_op jit(solution)/shard_map/ppermute | solution.py:109
  405.4 22.7 %collective-permute-start.28 = (bf16[384,1024]{1,0:T(8,128)(2,1)}, bf16[384,1024]{1,0:T(8,128)(2,1)}, u32[]{:S(2)}, u32[]{:S(2)}) collective-permute-start(bf16[384,1024]{1,0:T(8,128)(2,1)} %add_convert_fusion.5), channel_id=1, source_target_pairs={{0,2},{1,3},{2,6},{3,7},{6,10},{7,11},{10,14},{11,15},{14,12},{15,... | collective-permute-start | bytes 2359304 | tf_op jit(solution)/shard_map/ppermute | solution.py:109
  411.1 40.2 %collective-permute-start.21 = (bf16[384,1024]{1,0:T(8,128)(2,1)}, bf16[384,1024]{1,0:T(8,128)(2,1)}, u32[]{:S(2)}, u32[]{:S(2)}) collective-permute-start(bf16[384,1024]{1,0:T(8,128)(2,1)} %get-tuple-element.323), channel_id=1, source_target_pairs={{0,1},{1,0},{2,3},{3,2},{4,5},{5,4},{6,7},{7,6},{8,9},{9,8},{10,11... | collective-permute-start | bytes 2359304 | tf_op jit(solution)/shard_map/ppermute | solution.py:112
  414.7 43.1 %collective-permute-start.35 = (bf16[384,1024]{1,0:T(8,128)(2,1)}, bf16[384,1024]{1,0:T(8,128)(2,1)}, u32[]{:S(2)}, u32[]{:S(2)}) collective-permute-start(bf16[384,1024]{1,0:T(8,128)(2,1)} %get-tuple-element.324), channel_id=1, source_target_pairs={{0,1},{1,0},{2,3},{3,2},{4,5},{5,4},{6,7},{7,6},{8,9},{9,8},{10,11... | collective-permute-start | bytes 2359304 | tf_op jit(solution)/shard_map/ppermute | solution.py:112
  451.2 25.6 %collective-permute-start.18 = (bf16[384,1024]{1,0:T(8,128)(2,1)}, bf16[384,1024]{1,0:T(8,128)(2,1)}, u32[]{:S(2)}, u32[]{:S(2)}) collective-permute-start(bf16[384,1024]{1,0:T(8,128)(2,1)} %get-tuple-element.300), channel_id=1, source_target_pairs={{0,16},{16,0},{1,17},{17,1},{2,18},{18,2},{3,19},{19,3},{4,20},{20... | collective-permute-start | bytes 2359304 | tf_op jit(solution)/shard_map/ppermute | solution.py:655
  455.0 24.8 %collective-permute-start.20 = (bf16[384,1024]{1,0:T(8,128)(2,1)}, bf16[384,1024]{1,0:T(8,128)(2,1)}, u32[]{:S(2)}, u32[]{:S(2)}) collective-permute-start(bf16[384,1024]{1,0:T(8,128)(2,1)} %get-tuple-element.325), channel_id=1, source_target_pairs={{0,1},{1,0},{2,3},{3,2},{4,5},{5,4},{6,7},{7,6},{8,9},{9,8},{10,11... | collective-permute-start | bytes 2359304 | tf_op jit(solution)/shard_map/ppermute | solution.py:112
  (65 other events, 883.7 us)
Sparse Core Ops, SparseCore 0:
  101.1 102.0 all-gather.2
  270.5 134.5 reduce-scatter.1

commit v4 on v3

--- a/solution.py
+++ b/solution.py
@@ -13,6 +13,7 @@
 SLOTS = 8
 EPSILON = 1e-05
 FAR = -1e20
+GATE = 4
 BF = jnp.bfloat16
 F32 = jnp.float32
 VMEM_LIMIT = 56 * 1024 * 1024
@@ -124,7 +125,7 @@
         )
         return 2 * found + jnp.bitwise_xor(core, other)
 
-    def gather(self, table, use, ready):
+    def gather(self, table, use, ready, gate, step):
         tie = lax.optimization_barrier
         half = table.shape[0] // 2
         used = []
@@ -140,34 +141,51 @@
             if k >= 2:
                 used = used + [use(k - 2, stages[k - 2], ready)]
                 ahead, behind, used = tie((ahead, behind, used))
+            if k == step:
+                ahead = gate(ahead)
             if k < self.far:
                 stages.append([ahead, behind, self.swap(ahead), self.swap(behind)])
         both = jnp.concatenate([ahead, behind], axis=0)
         stages.append([both, self.swap(both)])
-        return used + [use(i, stages[i], ready) for i in range(len(used), len(stages))], ahead
+        return used + [use(i, stages[i], ready) for i in range(len(used), len(stages))]
 
     def scatter_order(self):
         n, far = self.count, self.far
         return [far] + [k for near in range(far - 1, 0, -1) for k in (near, n - near)] + [0]
 
     def scatter_sum(self, own, other, release, finish):
-        low = lambda t: t.astype(BF)
         n, far = self.count, self.far
         swapped = {k: self.swap(other[k]) for k in self.scatter_order()}
-        own = {k: own[k].astype(F32) + swapped[k].astype(F32) for k in own}
-        half = own[far].shape[0] // 2
-        start = release(low(own[far]))
-        up, down = self.hop(start[:half], 1), self.hop(start[half:], -1)
-        blank = jnp.zeros(up.shape, F32)
-        up = jnp.concatenate([up.astype(F32), blank], axis=0)
-        down = jnp.concatenate([blank, down.astype(F32)], axis=0)
+        first = (own[far].astype(F32) + swapped[far].astype(F32)).astype(BF)
+        half = first.shape[0] // 2
+        up, down = lax.optimization_barrier((self.hop(first[:half], 1), self.hop(first[half:], -1)))
+        up = release(up)
         for k in range(far - 1, 0, -1):
-            up, down = low(own[k] + up), low(own[n - k] + down)
-            if k == 1:
-                up = finish(up)
-            up, down = lax.optimization_barrier((up, down))
-            up, down = self.hop(up, 1).astype(F32), self.hop(down, -1).astype(F32)
-        return own[0] + up + down
+            up, down = ring_add(own[k], swapped[k], up, own[n - k], swapped[n - k], down)
+            up, down = lax.optimization_barrier((self.hop(up, 1), self.hop(down, -1)))
+        up = finish(up)
+        return own[0], swapped[0], up, down
+
+
+def ring_add_kernel(own_up, swap_up, up, own_down, swap_down, down, out_up, out_down):
+    length, came = own_up.shape[0], up.shape[0]
+    for own, swap, more, out, start in (
+        (own_up, swap_up, up, out_up, 0),
+        (own_down, swap_down, down, out_down, length - came),
+    ):
+        for at in range(0, length, came):
+            cut = slice(at, at + came)
+            total = own[cut].astype(F32) + swap[cut].astype(F32)
+            if at == start:
+                total = total + more[...].astype(F32)
+            out[cut] = total.astype(BF)
+
+
+def ring_add(*tables):
+    shape = jax.ShapeDtypeStruct(tables[0].shape, BF)
+    return pl.pallas_call(
+        ring_add_kernel, out_shape=[shape, shape], compiler_params=params(), name="ring_add"
+    )(*tables)
 
 
 def project_kernel(count, *refs):
@@ -558,7 +576,7 @@
         grid=(chunks,),
         in_specs=[whole((count, width))] * 4 + [column] * 4,
         out_specs=pl.BlockSpec(memory_space=pl.ANY),
-        out_shape=jax.ShapeDtypeStruct(weights.shape, BF),
+        out_shape=jax.ShapeDtypeStruct((owners, 2 * units, width), BF),
         scratch_shapes=[
             pltpu.VMEM((chunks, owners // chunks, units, width), BF),
             pltpu.VMEM((chunks, owners, own, width), BF),
@@ -570,10 +588,9 @@
 
 
 def out_back_kernel(
-    mid_ref, gn_ref, other_ref, cot_ref, att_ref, w_ref, vec_ref, _, gm_ref, ga_ref, gv_ref, grads_hbm, buf, sem
+    mid_ref, gn_ref, other_ref, cot_ref, att_ref, w_ref, vec_ref, gm_ref, ga_ref, gv_ref, gw_ref
 ):
     width = mid_ref.shape[1]
-    rows = grads_hbm.shape[1]
     normal, scale = normalize(mid_ref[...])
     grad = gn_ref[...] + other_ref[...].astype(F32)
     cot = cot_ref[...].astype(F32)
@@ -581,38 +598,32 @@
     gm_ref[...] = grad_mid
     branch = grad_mid.astype(BF)
     ga_ref[...] = dot_nt(w_ref[...].reshape(width, width), branch).astype(BF).reshape(ga_ref.shape)
-    buf[...] = dot_nn(att_ref[...].reshape(width, -1), branch).astype(BF).reshape(buf.shape)
-    copy = pltpu.make_async_copy(buf, grads_hbm.at[:, pl.ds(rows - buf.shape[1], buf.shape[1])], sem)
-    copy.start()
+    gw_ref[...] = dot_nn(att_ref[...].reshape(width, -1), branch).astype(BF).reshape(gw_ref.shape)
     gv_ref[...] = jnp.zeros_like(gv_ref)
     gv_ref[0:1, :] = jnp.sum(branch.astype(F32), axis=0, keepdims=True)
     gv_ref[1:2, :] = jnp.sum(grad * normal, axis=0, keepdims=True)
     gv_ref[2:3, :] = jnp.sum(grad, axis=0, keepdims=True)
     gv_ref[3:4, :] = jnp.sum(cot, axis=0, keepdims=True)
-    copy.wait()
-
-
-def project_out_back(mid, grad, other, cotangent, attended, weights, vectors, grads):
+
+
+def project_out_back(mid, grad, other, cotangent, attended, weights, vectors):
     owners, own, width, units, chunks = layout_of(weights)
     shape = mid.shape
     packed = attended.shape
-    anywhere = pl.BlockSpec(memory_space=pl.ANY)
     return pl.pallas_call(
         out_back_kernel,
         grid=(1,),
-        in_specs=[whole(shape)] * 4 + [whole(packed), out_rows(weights), whole(vectors.shape), anywhere],
-        out_specs=[whole(shape), whole(packed), whole((8, width)), anywhere],
+        in_specs=[whole(shape)] * 4 + [whole(packed), out_rows(weights), whole(vectors.shape)],
+        out_specs=[whole(shape), whole(packed), whole((8, width)), whole((owners, own, width))],
         out_shape=[
             jax.ShapeDtypeStruct(shape, F32),
             jax.ShapeDtypeStruct(packed, BF),
             jax.ShapeDtypeStruct((8, width), F32),
-            jax.ShapeDtypeStruct(grads.shape, BF),
+            jax.ShapeDtypeStruct((owners, own, width), BF),
         ],
-        scratch_shapes=[pltpu.VMEM((owners, own, width), BF), pltpu.SemaphoreType.DMA],
-        input_output_aliases={7: 3},
         compiler_params=params("arbitrary"),
         name="project_out_back",
-    )(mid, grad, other, cotangent, attended, weights, vectors, grads)
+    )(mid, grad, other, cotangent, attended, weights, vectors)
 
 
 def shares_kernel(starts, d_ref, w_ref, *outs):
@@ -631,19 +642,27 @@
     )(grad_table, weight)
 
 
-def last_kernel(tok_ref, gn_ref, gm_ref, norm_ref, out_ref):
-    normal, scale = normalize(tok_ref[...].astype(F32))
-    grad = norm_backward(gn_ref[...], normal, scale, norm_ref[0:1, :])
-    out_ref[...] = (gm_ref[...] + grad).astype(BF)
-
-
-def last(tokens, grad_normed, grad_middle, norm_rows):
+def last_kernel(tok_ref, one_ref, two_ref, three_ref, four_ref, gm_ref, norm_ref, out_ref):
+    step = 128
+
+    def rows(i, carry):
+        at = pl.ds(pl.multiple_of(i * step, step), step)
+        normal, scale = normalize(tok_ref[at, :].astype(F32))
+        terms = [ref[at, :].astype(F32) for ref in (one_ref, two_ref, three_ref, four_ref)]
+        grad = (terms[0] + terms[1]) + (terms[2] + terms[3])
+        out_ref[at, :] = (gm_ref[at, :] + norm_backward(grad, normal, scale, norm_ref[0:1, :])).astype(BF)
+        return carry
+
+    lax.fori_loop(0, tok_ref.shape[0] // step, rows, 0)
+
+
+def last(tokens, terms, grad_middle, norm_rows):
     return pl.pallas_call(
         last_kernel,
         out_shape=jax.ShapeDtypeStruct(tokens.shape, BF),
         compiler_params=params(),
         name="last",
-    )(tokens, grad_normed, grad_middle, norm_rows)
+    )(tokens, *terms, grad_middle, norm_rows)
 
 
 def exchange(table):
@@ -738,9 +757,15 @@
         segs_here = jnp.pad(segs[first : first + len(pieces)], ((0, 8 - len(pieces)), (0, 0)))
         return project(pieces, segs_here, *ready)
 
-    projected, late = ring.gather(tokens, use, (weight, bias, norm_rows))
-    mine, _ = lax.optimization_barrier((mine, late))
-    weights = lax.all_gather(mine, "shard", axis=0)
+    gathered = []
+
+    def gate(rows):
+        own_weights, rows = lax.optimization_barrier((mine, rows))
+        gathered.append(lax.all_gather(own_weights, "shard", axis=0))
+        return rows
+
+    projected = ring.gather(tokens, use, (weight, bias, norm_rows), gate, min(GATE, ring.far))
+    weights = gathered[0]
     projected, other_cotangent = lax.optimization_barrier((projected, other_cotangent))
     table = lambda *which: [[stage[i] for stage in projected] for i in which]
     attended = exchange(attend(scalars, table(1, 3, 5), owners))
@@ -758,13 +783,15 @@
         (other_normed, other_cotangent, other_hid, other_pre),
         weights,
     )
-    grad_middle, grad_attended, grad_rows, grads = project_out_back(
-        mid, grad_two, other_grad, cotangent, attended, weights, vectors, grads
+    other_grad, grads = lax.optimization_barrier((other_grad, grads))
+    grad_middle, grad_attended, grad_rows, grad_out = project_out_back(
+        mid, grad_two, other_grad, cotangent, attended, weights, vectors
     )
     layer_out = (mid + more + other_more.astype(F32) + fixed[3][None]).astype(BF)
-    shares = lax.psum_scatter(
-        grads.reshape(-1, width), "shard", scatter_dimension=0, tiled=True
-    )
+    summed = lambda t: lax.psum_scatter(t.reshape(-1, width), "shard", scatter_dimension=0, tiled=True)
+    shares = summed(grads)
+    shares, grad_out = lax.optimization_barrier((shares, grad_out))
+    out_share = summed(grad_out)
     grad_table = attend_back(scalars, table(1, 2, 3, 4), exchange(grad_attended))
     at = {piece: i * count for i, piece in enumerate(ring.pieces)}
     order = ring.scatter_order()
@@ -832,7 +859,8 @@
             own, owners, units
         )
         grad_up = in_order(up_of(ours), up_of(theirs), 2).reshape(own, hidden)
-        grad_out = ours[2 * units :] + theirs[2 * units :]
+        out_sum = over_alike(out_share)
+        grad_out = out_sum.astype(F32) + trade(out_sum).astype(F32)
         return (
             piece(4),
             piece(5),
@@ -851,10 +879,10 @@
             piece(3),
         )
 
-    grad_normed = ring.scatter_sum(
+    terms = ring.scatter_sum(
         dict(zip(order, own_shares)), dict(zip(order, other_shares)), release, finish
     )
-    grad_tokens = last(tokens, grad_normed, grad_middle, norm_rows)
+    grad_tokens = last(tokens, terms, grad_middle, norm_rows)
     return (layer_out[None], grad_tokens[None], *results[0])
 
 

time: 517 us -> 511 us (0.988)
  other arithmetic: 43.2 us -> 23.7 us
  Pallas kernels: 157 us -> 167 us
    convert_element_type x7 -> x1, other arithmetic: 15.7 us -> 1.59 us  [scatter_sum(): first = (own[far].astype(F32) + swapped[far].astype(F32)).astype(BF)]
    pallas_call x0 -> x3, Pallas kernels: none -> 11.2 us  [ring_add(): pl.pallas_call(ring_add_kernel, out_shape=[shape, shape], compiler_params...]
    ppermute x7 -> x8, starting transfers between devices: 9.31 us -> 11.4 us  [trade(): return lax.ppermute(table, 'rep', [(r, r ^ 1) for r in range(reps)])]
    ppermute x7 -> x8, waiting for transfers between devices: 13.9 us -> 12.2 us  [trade(): return lax.ppermute(table, 'rep', [(r, r ^ 1) for r in range(reps)])]
    unnamed x94 -> x96, local copies, waits for them, and re-layouts: 12.1 us -> 12.3 us
  transfers between devices with their start and end apart: 44 -> 46, of which waited for: 20 -> 16; matrix products, arithmetic and copies ran while one was open for 16% -> 13% of each run, Pallas kernels for 25% -> 29%
where the time goes in v4:
time: 511 us; the launch traced here: 503 us
  Pallas kernels  167 us (33%)
  waiting for transfers between devices  165 us (32%)
  starting transfers between devices  54.4 us (11%)
  local copies, waits for them, and re-layouts  49.4 us (10%)
  blocking collectives  24.4 us (5%)
  other arithmetic  23.7 us (5%)
  between operations  15.2 us (3%)
    ppermute x16, waiting for transfers between devices, hop(): return lax.ppermute(table, 'shard', pairs)  91.3 us
    all_to_all x3, waiting for transfers between devices, exchange(): lax.all_to_all(table, 'shard', split_axis=0, concat_axis=0, tiled=True)  38.4 us
    pallas_call x1, Pallas kernels, attend_back(): pl.pallas_call(functools.partial(attend_back_kernel, parts), in_specs=[pl...  36.3 us
    pallas_call x5, Pallas kernels, project(): pl.pallas_call(functools.partial(project_kernel, len(pieces)), out_shape=...  30 us
    pallas_call x2, Pallas kernels, feed(): pl.pallas_call(feed_kernel, grid=(chunks,), in_specs=[whole(normed.shape)...  25.4 us
    all_to_all x1, blocking collectives, exchange(): lax.all_to_all(table, 'shard', split_axis=0, concat_axis=0, tiled=True)  24.4 us
    pallas_call x1, Pallas kernels, attend(): pl.pallas_call(functools.partial(attend_kernel, parts), in_specs=[pl.Bloc...  22.9 us
    all_gather x1, waiting for transfers between devices, gate(): gathered.append(lax.all_gather(own_weights, 'shard', axis=0))  22.6 us
  transfers between devices with their start and end apart: 46, of which 16 were waited for; matrix products, arithmetic and copies ran while one was open for 13% of the time, Pallas kernels for 29%

profile of v4, /device:TPU:0, one launch (start us, length us, event | category | flops | bytes accessed | tf_op | source)
XLA Modules:
  0.0 503.1 jit_solution(7150608382829935854)
XLA Ops:
  19.4 6.5 %all-to-all-start = ((bf16[16,64,256]{2,1,0:T(8,128)(2,1)}), bf16[16,64,256]{2,1,0:T(8,128)(2,1)S(1)}, u32[]{:S(2)}, u32[]{:S(2)}) async-start(bf16[16,64,256]{2,1,0:T(8,128)(2,1)} %pad_maximum_fusion.3), calls=%async_computation | async-start | bytes 1048576 | tf_op jit(solution)/shard_map/all_to_all | solution.py:669
  34.6 7.8 %all-to-all-done = bf16[16,64,256]{2,1,0:T(8,128)(2,1)S(1)} async-done(((bf16[16,64,256]{2,1,0:T(8,128)(2,1)}), bf16[16,64,256]{2,1,0:T(8,128)(2,1)S(1)}, u32[]{:S(2)}, u32[]{:S(2)}) %all-to-all-start) | async-done | bytes 524320 | tf_op jit(solution)/shard_map/all_to_all | solution.py:669
  45.2 8.3 %collective-permute-done.2.refs_0_ = bf16[384,1024]{1,0:T(8,128)(2,1)} collective-permute-done((bf16[384,1024]{1,0:T(8,128)(2,1)}, bf16[384,1024]{1,0:T(8,128)(2,1)}, u32[]{:S(2)}, u32[]{:S(2)}) %collective-permute-start.2) | collective-permute-done | bytes 786464 | tf_op jit(solution)/shard_map/ppermute | solution.py:110
  65.6 7.1 %project.6 = (bf16[1536,1024]{1,0:T(8,128)(2,1)}, bf16[1536,128]{1,0:T(8,128)(2,1)}, bf16[1536,128]{1,0:T(8,128)(2,1)}, bf16[12,128,128]{2,1,0:T(8,128)(2,1)}, b...) custom-call(bf16[384,1024]{1,0:T(8,128)(2,1)} %collective-permute-done.refs_0_, ...), custom_call_target="tpu_custom_call" | custom-call | tf_op jit(solution)/shard_map/project/pallas_call | solution.py:232
  72.7 8.7 %collective-permute-done.5.refs_0_ = bf16[384,1024]{1,0:T(8,128)(2,1)S(1)} collective-permute-done((bf16[384,1024]{1,0:T(8,128)(2,1)}, bf16[384,1024]{1,0:T(8,128)(2,1)S(1)}, u32[]{:S(2)}, u32[]{:S(2)}) %collective-permute-start.5) | collective-permute-done | bytes 786464 | tf_op jit(solution)/shard_map/ppermute | solution.py:110
  93.9 7.1 %project.7 = (bf16[1536,1024]{1,0:T(8,128)(2,1)}, bf16[1536,128]{1,0:T(8,128)(2,1)}, bf16[1536,128]{1,0:T(8,128)(2,1)}, bf16[12,128,128]{2,1,0:T(8,128)(2,1)}, b...) custom-call(bf16[384,1024]{1,0:T(8,128)(2,1)} %collective-permute-done.2.refs_0_, ...), custom_call_target="tpu_custom_call" | custom-call | tf_op jit(solution)/shard_map/project/pallas_call | solution.py:232
  109.6 7.3 %project.8 = (bf16[1536,1024]{1,0:T(8,128)(2,1)}, bf16[1536,128]{1,0:T(8,128)(2,1)}, bf16[1536,128]{1,0:T(8,128)(2,1)}, bf16[12,128,128]{2,1,0:T(8,128)(2,1)}, b...) custom-call(bf16[384,1024]{1,0:T(8,128)(2,1)} %copy-done.10, bf16[384,1024]{1,0:T(8,128)(2,1)} %collective-permute-done.6.refs_1_, ...), custom_call_target="tpu_custom_call" | custom-call | tf_op jit(solution)/shard_map/project/pallas_call | solution.py:232
  121.2 22.9 %attend.1 = bf16[16,64,384]{2,1,0:T(8,128)(2,1)} custom-call(s32[768]{0:T(1024)} %and_select_fusion.idx_ref, s32[16]{0:T(128)} %copy-done.31, s32[97]{0:T(128)} %pad_add_fusion.place_ref, bf16[768,128]{1,0:T(8,128)(2,1)} %get-tuple-element.292.refs_0_, bf16[1536,128]{1,0:T(8,128)(2,1)} %get-tuple-element.293.refs_1_, ...), custom_call_target="tpu_custom_call" | custom-call | tf_op jit(solution)/shard_map/attend/pallas_call | solution.py:326
  150.0 30.6 %all-to-all-done.1.att_ref = bf16[16,64,384]{2,1,0:T(8,128)(2,1)S(1)} async-done(((bf16[16,64,384]{2,1,0:T(8,128)(2,1)}), bf16[16,64,384]{2,1,0:T(8,128)(2,1)S(1)}, u32[]{:S(2)}, u32[]{:S(2)}) %all-to-all-start.1) | async-done | bytes 786464 | tf_op jit(solution)/shard_map/all_to_all | solution.py:669
  180.6 22.6 %all-gather.3.cloned.1.call-done = bf16[5120,1024]{1,0:T(8,128)(2,1)} async-done(((bf16[320,1024]{1,0:T(8,128)(2,1)}), bf16[5120,1024]{1,0:T(8,128)(2,1)}) %all-gather.3.cloned.1.call-update) | async-done | bytes 10485776 | tf_op jit(solution)/shard_map/all_gather | solution.py:764
  209.3 13.0 %feed.2 = (f32[384,1024]{1,0:T(8,128)}, f32[384,1024]{1,0:T(8,128)}, bf16[384,2048]{1,0:T(8,128)(2,1)}, bf16[384,2048]{1,0:T(8,128)(2,1)}, f32[8,1024]{1,0:T(8,128)}) custom-call(bf16[384,1024]{1,0:T(8,128)(2,1)} %get-tuple-element.309.n2_ref.na_ref, bf16[384,1024]{1,0:T(8,128)(2,1)} %bitcast.77, bf16[16,320,1024]{2,1,0:T(8,128)(2,1)} %bitcast.63, ...), custom_call_target="tpu_custom_call" | custom-call | tf_op jit(solution)/shard_map/feed/pallas_call | solution.py:517
  222.2 5.4 %collective-permute-done.17.n2_ref.nb_ref = bf16[384,1024]{1,0:T(8,128)(2,1)S(1)} collective-permute-done((bf16[384,1024]{1,0:T(8,128)(2,1)}, bf16[384,1024]{1,0:T(8,128)(2,1)S(1)}, u32[]{:S(2)}, u32[]{:S(2)}) %collective-permute-start.17) | collective-permute-done | bytes 786464 | tf_op jit(solution)/shard_map/ppermute | solution.py:674
  228.5 12.4 %feed.3 = (bf16[384,1024]{1,0:T(8,128)(2,1)}, bf16[384,1024]{1,0:T(8,128)(2,1)}, bf16[384,2048]{1,0:T(8,128)(2,1)}, bf16[384,2048]{1,0:T(8,128)(2,1)}, f32[8,1024]{1,0:T(8,128)}) custom-call(bf16[384,1024]{1,0:T(8,128)(2,1)} %copy-done.8, bf16[384,1024]{1,0:T(8,128)(2,1)} %copy-done.7, bf16[16,320,1024]{2,1,0:T(8,128)(2,1)} %bitcast.65, ...), custom_call_target="tpu_custom_call" | custom-call | tf_op jit(solution)/shard_map/feed/pallas_call | solution.py:517
  242.5 13.7 %feed_grads.1 = bf16[16,256,1024]{2,1,0:T(8,128)(2,1)} custom-call(bf16[384,1024]{1,0:T(8,128)(2,1)} %get-tuple-element.309.n2_ref.na_ref, bf16[384,1024]{1,0:T(8,128)(2,1)} %copy-done.8, bf16[384,1024]{1,0:T(8,128)(2,1)} %bitcast.78, bf16[384,1024]{1,0:T(8,128)(2,1)} %copy-done.7, bf16[384,2048]{1,0:T(8,128)(2,1)} %get-tuple-element.327.ha_ref, ...), custom_call_target="tpu_custom_call" | custom-call | tf_op jit(solution)/shard_map/feed_grads/pallas_call | solution.py:574
  260.9 8.0 %project_out_back.1 = (f32[384,1024]{1,0:T(8,128)}, bf16[16,64,384]{2,1,0:T(8,128)(2,1)}, f32[8,1024]{1,0:T(8,128)}, bf16[16,64,1024]{2,1,0:T(8,128)(2,1)}) custom-call(f32[384,1024]{1,0:T(8,128)} %get-tuple-element.308.mid_ref, f32[384,1024]{1,0:T(8,128)} %get-tuple-element.325.gn_ref, bf16[384,1024]{1,0:T(8,128)(2,1)} %copy-done.11, ...), custom_call_target="tpu_custom_call" | custom-call | tf_op jit(solution)/shard_map/project_out_back/pallas_call | solution.py:613
  268.9 24.4 %all_to_all.20.refs_20_ = bf16[16,64,384]{2,1,0:T(8,128)(2,1)} all-to-all(bf16[16,64,384]{2,1,0:T(8,128)(2,1)} %get-tuple-element.332), channel_id=1, replica_groups=mesh['rep'=2,'shard'=16] {'shard'}, dimensions={0} | all-to-all | bytes 1572864 | tf_op jit(solution)/shard_map/all_to_all | solution.py:669
  293.3 36.3 %attend_back.1.d_ref = bf16[6144,256]{1,0:T(8,128)(2,1)} custom-call(s32[768]{0:T(1024)} %and_select_fusion.idx_ref, s32[16]{0:T(128)} %copy-done.31, s32[97]{0:T(128)} %pad_add_fusion.place_ref, bf16[768,128]{1,0:T(8,128)(2,1)} %get-tuple-element.292.refs_0_, bf16[1536,128]{1,0:T(8,128)(2,1)} %get-tuple-element.293.refs_1_, ...), custom_call_target="tpu_custom_call" | custom-call | tf_op jit(solution)/shard_map/attend_back/pallas_call | solution.py:416
  329.6 5.1 %head_shares.2 = (bf16[384,1024]{1,0:T(8,128)(2,1)}, bf16[384,1024]{1,0:T(8,128)(2,1)}, bf16[384,1024]{1,0:T(8,128)(2,1)}, bf16[384,1024]{1,0:T(8,128)(2,1)}, bf...) custom-call(bf16[6144,256]{1,0:T(8,128)(2,1)} %attend_back.1.d_ref, ...), custom_call_target="tpu_custom_call" | custom-call | tf_op jit(solution)/shard_map/head_shares/pallas_call | solution.py:637
  335.8 5.1 %head_shares.3 = (bf16[384,1024]{1,0:T(8,128)(2,1)}, bf16[384,1024]{1,0:T(8,128)(2,1)}, bf16[384,1024]{1,0:T(8,128)(2,1)}, bf16[384,1024]{1,0:T(8,128)(2,1)}, bf...) custom-call(bf16[6144,256]{1,0:T(8,128)(2,1)} %attend_back.1.d_ref, ...), custom_call_target="tpu_custom_call" | custom-call | tf_op jit(solution)/shard_map/head_shares/pallas_call | solution.py:637
  352.4 9.6 %collective-permute-done.26.down = bf16[192,1024]{1,0:T(8,128)(2,1)} collective-permute-done((bf16[192,1024]{1,0:T(8,128)(2,1)}, bf16[192,1024]{1,0:T(8,128)(2,1)}, u32[]{:S(2)}, u32[]{:S(2)}) %collective-permute-start.26) | collective-permute-done | bytes 393248 | tf_op jit(solution)/shard_map/ppermute | solution.py:110
  362.0 8.5 %collective-permute-done.25.up = bf16[192,1024]{1,0:T(8,128)(2,1)} collective-permute-done((bf16[192,1024]{1,0:T(8,128)(2,1)S(1)}, bf16[192,1024]{1,0:T(8,128)(2,1)}, u32[]{:S(2)}, u32[]{:S(2)}) %collective-permute-start.25) | collective-permute-done | bytes 393248 | tf_op jit(solution)/shard_map/ppermute | solution.py:110
  396.0 20.7 %collective-permute-done.28.up = bf16[384,1024]{1,0:T(8,128)(2,1)S(1)} collective-permute-done((bf16[384,1024]{1,0:T(8,128)(2,1)}, bf16[384,1024]{1,0:T(8,128)(2,1)S(1)}, u32[]{:S(2)}, u32[]{:S(2)}) %collective-permute-start.28) | collective-permute-done | bytes 786464 | tf_op jit(solution)/shard_map/ppermute | solution.py:110
  432.7 18.0 %collective-permute-done.31.up = bf16[384,1024]{1,0:T(8,128)(2,1)} collective-permute-done((bf16[384,1024]{1,0:T(8,128)(2,1)}, bf16[384,1024]{1,0:T(8,128)(2,1)}, u32[]{:S(2)}, u32[]{:S(2)}) %collective-permute-start.31) | collective-permute-done | bytes 786464 | tf_op jit(solution)/shard_map/ppermute | solution.py:110
  465.7 12.4 %collective-permute-done.34.three_ref = bf16[384,1024]{1,0:T(8,128)(2,1)S(1)} collective-permute-done((bf16[384,1024]{1,0:T(8,128)(2,1)}, bf16[384,1024]{1,0:T(8,128)(2,1)S(1)}, u32[]{:S(2)}, u32[]{:S(2)}) %collective-permute-start.34) | collective-permute-done | bytes 786464 | tf_op jit(solution)/shard_map/ppermute | solution.py:110
  (322 shorter events, 166.5 us)
Async XLA Ops:
  7.2 47.7 %collective-permute-start.4 = (bf16[384,1024]{1,0:T(8,128)(2,1)}, bf16[384,1024]{1,0:T(8,128)(2,1)S(1)}, u32[]{:S(2)}, u32[]{:S(2)}) collective-permute-start(bf16[384,1024]{1,0:T(8,128)(2,1)} %bitcast.81), channel_id=1, source_target_pairs={{0,1},{1,0},{2,3},{3,2},{4,5},{5,4},{6,7},{7,6},{8,9},{9,8},{10,11... | collective-permute-start | bytes 2359304 | tf_op jit(solution)/shard_map/ppermute | solution.py:113
  19.4 23.1 %all-to-all-start = ((bf16[16,64,256]{2,1,0:T(8,128)(2,1)}), bf16[16,64,256]{2,1,0:T(8,128)(2,1)S(1)}, u32[]{:S(2)}, u32[]{:S(2)}) async-start(bf16[16,64,256]{2,1,0:T(8,128)(2,1)} %pad_maximum_fusion.3), calls=%async_computation | async-start | bytes 1048576 | tf_op jit(solution)/shard_map/all_to_all | solution.py:669
  25.8 177.3 %all-gather.3.cloned.1.call-start = ((), (), s32[]{:S(2)}) async-start(), calls=%async_computation.8 | async-start | bytes 11141120 | tf_op jit(solution)/shard_map/all_gather | solution.py:764
  34.1 30.4 %collective-permute-start.7 = (bf16[384,1024]{1,0:T(8,128)(2,1)}, bf16[384,1024]{1,0:T(8,128)(2,1)}, u32[]{:S(2)}, u32[]{:S(2)}) collective-permute-start(bf16[384,1024]{1,0:T(8,128)(2,1)} %collective-permute-done.refs_0_), channel_id=1, source_target_pairs={{0,1},{1,0},{2,3},{3,2},{4,5},{5,4},{6,7},{7,6},{8,9},{9,8},{10,11... | collective-permute-start | bytes 2359304 | tf_op jit(solution)/shard_map/ppermute | solution.py:113
  34.1 31.5 %collective-permute-start.8 = (bf16[384,1024]{1,0:T(8,128)(2,1)}, bf16[384,1024]{1,0:T(8,128)(2,1)}, u32[]{:S(2)}, u32[]{:S(2)}) collective-permute-start(bf16[384,1024]{1,0:T(8,128)(2,1)} %collective-permute-done.1.refs_1_), channel_id=1, source_target_pairs={{0,1},{1,0},{2,3},{3,2},{4,5},{5,4},{6,7},{7,6},{8,9},{9,8},{10,11... | collective-permute-start | bytes 2359304 | tf_op jit(solution)/shard_map/ppermute | solution.py:113
  64.5 28.6 %collective-permute-start.11 = (bf16[384,1024]{1,0:T(8,128)(2,1)}, bf16[384,1024]{1,0:T(8,128)(2,1)S(1)}, u32[]{:S(2)}, u32[]{:S(2)}) collective-permute-start(bf16[384,1024]{1,0:T(8,128)(2,1)} %collective-permute-done.2.refs_0_), channel_id=1, source_target_pairs={{0,1},{1,0},{2,3},{3,2},{4,5},{5,4},{6,7},{7,6},{8,9},{9,8},{10,11... | collective-permute-start | bytes 2359304 | tf_op jit(solution)/shard_map/ppermute | solution.py:113
  64.5 28.6 %collective-permute-start.12 = (bf16[384,1024]{1,0:T(8,128)(2,1)}, bf16[384,1024]{1,0:T(8,128)(2,1)}, u32[]{:S(2)}, u32[]{:S(2)}) collective-permute-start(bf16[384,1024]{1,0:T(8,128)(2,1)} %collective-permute-done.3.refs_1_), channel_id=1, source_target_pairs={{0,1},{1,0},{2,3},{3,2},{4,5},{5,4},{6,7},{7,6},{8,9},{9,8},{10,11... | collective-permute-start | bytes 2359304 | tf_op jit(solution)/shard_map/ppermute | solution.py:113
  144.1 36.5 %all-to-all-start.1 = ((bf16[16,64,384]{2,1,0:T(8,128)(2,1)}), bf16[16,64,384]{2,1,0:T(8,128)(2,1)S(1)}, u32[]{:S(2)}, u32[]{:S(2)}) async-start(bf16[16,64,384]{2,1,0:T(8,128)(2,1)} %attend.1), calls=%async_computation.1 | async-start | bytes 1572864 | tf_op jit(solution)/shard_map/all_to_all | solution.py:669
  149.0 245.4 %reduce-scatter.3.cloned.1.call-start = ((), (), s32[]{:S(2)}) async-start(), calls=%async_computation.6 | async-start | bytes 8912896 | tf_op jit(solution)/shard_map/reduce_scatter | solution.py:791
  344.1 26.4 %collective-permute-start.25 = (bf16[192,1024]{1,0:T(8,128)(2,1)S(1)}, bf16[192,1024]{1,0:T(8,128)(2,1)}, u32[]{:S(2)}, u32[]{:S(2)}) collective-permute-start(bf16[192,1024]{1,0:T(8,128)(2,1)S(1)} %get-tuple-element.411), channel_id=1, source_target_pairs={{0,2},{1,3},{2,6},{3,7},{6,10},{7,11},{10,14},{11,15},{14,12},{15,... | collective-permute-start | bytes 1179656 | tf_op jit(solution)/shard_map/ppermute | solution.py:110
  351.9 36.5 %collective-permute-start.23 = (bf16[384,1024]{1,0:T(8,128)(2,1)}, bf16[384,1024]{1,0:T(8,128)(2,1)}, u32[]{:S(2)}, u32[]{:S(2)}) collective-permute-start(bf16[384,1024]{1,0:T(8,128)(2,1)} %get-tuple-element.334), channel_id=1, source_target_pairs={{0,1},{1,0},{2,3},{3,2},{4,5},{5,4},{6,7},{7,6},{8,9},{9,8},{10,11... | collective-permute-start | bytes 2359304 | tf_op jit(solution)/shard_map/ppermute | solution.py:113
  351.9 36.5 %collective-permute-start.27 = (bf16[384,1024]{1,0:T(8,128)(2,1)}, bf16[384,1024]{1,0:T(8,128)(2,1)}, u32[]{:S(2)}, u32[]{:S(2)}) collective-permute-start(bf16[384,1024]{1,0:T(8,128)(2,1)} %get-tuple-element.335), channel_id=1, source_target_pairs={{0,1},{1,0},{2,3},{3,2},{4,5},{5,4},{6,7},{7,6},{8,9},{9,8},{10,11... | collective-permute-start | bytes 2359304 | tf_op jit(solution)/shard_map/ppermute | solution.py:113
  383.6 42.4 %all-to-all-start.3 = ((bf16[16,64,256]{2,1,0:T(8,128)(2,1)}), bf16[16,64,256]{2,1,0:T(8,128)(2,1)S(1)}, u32[]{:S(2)}, u32[]{:S(2)}) async-start(bf16[16,64,256]{2,1,0:T(8,128)(2,1)} %pad_maximum_fusion.4), calls=%async_computation.3 | async-start | bytes 1048576 | tf_op jit(solution)/shard_map/all_to_all | solution.py:669
  388.3 96.7 %reduce-scatter.5.cloned.1.call-start = ((), (), s32[]{:S(2)}) async-start(), calls=%async_computation.7 | async-start | bytes 2228224 | tf_op jit(solution)/shard_map/reduce_scatter | solution.py:791
  391.9 24.8 %collective-permute-start.28 = (bf16[384,1024]{1,0:T(8,128)(2,1)}, bf16[384,1024]{1,0:T(8,128)(2,1)S(1)}, u32[]{:S(2)}, u32[]{:S(2)}) collective-permute-start(bf16[384,1024]{1,0:T(8,128)(2,1)} %get-tuple-element.351), channel_id=1, source_target_pairs={{0,2},{1,3},{2,6},{3,7},{6,10},{7,11},{10,14},{11,15},{14,12},{15,... | collective-permute-start | bytes 2359304 | tf_op jit(solution)/shard_map/ppermute | solution.py:110
  393.9 23.3 %collective-permute-start.22 = (bf16[384,1024]{1,0:T(8,128)(2,1)}, bf16[384,1024]{1,0:T(8,128)(2,1)}, u32[]{:S(2)}, u32[]{:S(2)}) collective-permute-start(bf16[384,1024]{1,0:T(8,128)(2,1)} %get-tuple-element.336), channel_id=1, source_target_pairs={{0,1},{1,0},{2,3},{3,2},{4,5},{5,4},{6,7},{7,6},{8,9},{9,8},{10,11... | collective-permute-start | bytes 2359304 | tf_op jit(solution)/shard_map/ppermute | solution.py:113
  393.9 23.3 %collective-permute-start.30 = (bf16[384,1024]{1,0:T(8,128)(2,1)}, bf16[384,1024]{1,0:T(8,128)(2,1)}, u32[]{:S(2)}, u32[]{:S(2)}) collective-permute-start(bf16[384,1024]{1,0:T(8,128)(2,1)} %get-tuple-element.337), channel_id=1, source_target_pairs={{0,1},{1,0},{2,3},{3,2},{4,5},{5,4},{6,7},{7,6},{8,9},{9,8},{10,11... | collective-permute-start | bytes 2359304 | tf_op jit(solution)/shard_map/ppermute | solution.py:113
  394.4 31.9 %collective-permute-start.18 = (bf16[384,1024]{1,0:T(8,128)(2,1)}, bf16[384,1024]{1,0:T(8,128)(2,1)}, u32[]{:S(2)}, u32[]{:S(2)}) collective-permute-start(bf16[384,1024]{1,0:T(8,128)(2,1)} %get-tuple-element.314), channel_id=1, source_target_pairs={{0,16},{16,0},{1,17},{17,1},{2,18},{18,2},{3,19},{19,3},{4,20},{20... | collective-permute-start | bytes 2359304 | tf_op jit(solution)/shard_map/ppermute | solution.py:674
  416.7 34.0 %collective-permute-start.21 = (bf16[384,1024]{1,0:T(8,128)(2,1)}, bf16[384,1024]{1,0:T(8,128)(2,1)S(1)}, u32[]{:S(2)}, u32[]{:S(2)}) collective-permute-start(bf16[384,1024]{1,0:T(8,128)(2,1)} %get-tuple-element.338), channel_id=1, source_target_pairs={{0,1},{1,0},{2,3},{3,2},{4,5},{5,4},{6,7},{7,6},{8,9},{9,8},{10,11... | collective-permute-start | bytes 2359304 | tf_op jit(solution)/shard_map/ppermute | solution.py:113
  416.7 34.0 %collective-permute-start.33 = (bf16[384,1024]{1,0:T(8,128)(2,1)}, bf16[384,1024]{1,0:T(8,128)(2,1)}, u32[]{:S(2)}, u32[]{:S(2)}) collective-permute-start(bf16[384,1024]{1,0:T(8,128)(2,1)} %get-tuple-element.339), channel_id=1, source_target_pairs={{0,1},{1,0},{2,3},{3,2},{4,5},{5,4},{6,7},{7,6},{8,9},{9,8},{10,11... | collective-permute-start | bytes 2359304 | tf_op jit(solution)/shard_map/ppermute | solution.py:113
  421.7 28.9 %collective-permute-start.31 = (bf16[384,1024]{1,0:T(8,128)(2,1)}, bf16[384,1024]{1,0:T(8,128)(2,1)}, u32[]{:S(2)}, u32[]{:S(2)}) collective-permute-start(bf16[384,1024]{1,0:T(8,128)(2,1)} %get-tuple-element.356), channel_id=1, source_target_pairs={{0,2},{1,3},{2,6},{3,7},{6,10},{7,11},{10,14},{11,15},{14,12},{15,... | collective-permute-start | bytes 2359304 | tf_op jit(solution)/shard_map/ppermute | solution.py:110
  423.0 27.7 %collective-permute-start.32 = (bf16[384,1024]{1,0:T(8,128)(2,1)}, bf16[384,1024]{1,0:T(8,128)(2,1)}, u32[]{:S(2)}, u32[]{:S(2)}) collective-permute-start(bf16[384,1024]{1,0:T(8,128)(2,1)} %get-tuple-element.357), channel_id=1, source_target_pairs={{0,4},{1,5},{2,0},{3,1},{6,2},{7,3},{10,6},{11,7},{14,10},{15,11},... | collective-permute-start | bytes 2359304 | tf_op jit(solution)/shard_map/ppermute | solution.py:110
  431.4 26.9 %collective-permute-start.37 = (bf16[16,64,192]{2,1,0:T(8,128)(2,1)S(1)}, bf16[16,64,192]{2,1,0:T(8,128)(2,1)}, u32[]{:S(2)}, u32[]{:S(2)}) collective-permute-start(bf16[16,64,192]{2,1,0:T(8,128)(2,1)S(1)} %bitcast.89), channel_id=1, source_target_pairs={{0,16},{16,0},{1,17},{17,1},{2,18},{18,2},{3,19},{19,3},{4,20},{20... | collective-permute-start | bytes 1179656 | tf_op jit(solution)/shard_map/ppermute | solution.py:674
  450.7 40.5 %collective-permute-start.20 = (bf16[384,1024]{1,0:T(8,128)(2,1)}, bf16[384,1024]{1,0:T(8,128)(2,1)}, u32[]{:S(2)}, u32[]{:S(2)}) collective-permute-start(bf16[384,1024]{1,0:T(8,128)(2,1)} %get-tuple-element.340), channel_id=1, source_target_pairs={{0,1},{1,0},{2,3},{3,2},{4,5},{5,4},{6,7},{7,6},{8,9},{9,8},{10,11... | collective-permute-start | bytes 2359304 | tf_op jit(solution)/shard_map/ppermute | solution.py:113
  (69 other events, 901.2 us)
Sparse Core Ops, SparseCore 0:
  101.2 101.9 all-gather.2
  260.1 112.3 reduce-scatter.2
  394.5 71.4 reduce-scatter.4
